TPU v7x, 256 devices: a whole 4x4x8 slice. The times are simulated.
256 devices in a mesh: ta: 32 (over x, y, core), ka: 8 (over z).
Axes of the slice: x: 4, y: 4, z: 8, core: 2. Of those that a mesh axis runs over, the one named last changes fastest.
Arguments:
- amplitudes: bfloat16 [512, 163840], P('ka', 'ta'), may hold values from -6 to 6
- integrals: bfloat16 [163840, 5120], P('ta', 'ka'), may hold values from -0.1875 to 0.1875
- other_terms: bfloat16 [512, 163840], P('ka', 'ta'), may hold values from -6 to 6
- tile_block: int32 [1280], replicated, may hold values from 0 to 1279, as said below
- occ_pairs: int32 [512, 2], P('ka'), may hold values from 0 to 149
- occ_energy: float32 [150], replicated, may hold values from -2 to -0.3
- pair_energy: float32 [163840], P('ta'), may hold values from 0.4 to 6
Outputs:
- increment: float32 [512, 163840], P('ka', 'ta')
Inputs may be any that keep to these rules, and one draw needn't show every extreme that they name: `tile_block`: the tiles of one symmetry block share one id, the index of the block's last tile, so ids never fall from tile to tile; a block lies within one region of 40 tiles, spans at most 16 tiles, and every region holds exactly one block of 16 tiles.
All inputs are finite; a program needn't handle non-finite values.
Results may differ from a plain program's by a relative error of at most 0.0075.
Values may be sent and summed in bfloat16 or wider, within the bound.
No kernel may reach another device: no remote copies, remote signals or barrier semaphores. Data moves between devices by JAX's collectives and lax.ppermute only.
A program may use at most 128 MiB of HBM per device.

v0:
```python
import jax
import jax.numpy as jnp
from jax import lax
from jax.sharding import PartitionSpec as P

TILE = 128


def pick_blocks(region_tiles, local_tiles):
    tile_count = region_tiles.shape[1]
    picker = (local_tiles[:, None] == jnp.arange(tile_count, dtype=jnp.int32)[None, :]).astype(
        jnp.float32
    )
    return jnp.dot(region_tiles, picker.T, precision=lax.Precision.HIGHEST)


def shards(amplitudes, integrals, other_terms, tile_block, occ_pairs, occ_energy, pair_energy):
    wide_count = lax.axis_size("ta")
    wide_index = lax.axis_index("ta")
    narrow_index = lax.axis_index("ka")
    region = integrals.shape[0]
    stripe = integrals.shape[1]
    slice_rows = region // wide_count
    region_tiles = tile_block.reshape(wide_count, region // TILE).astype(jnp.float32)
    row_local = (wide_index * slice_rows + jnp.arange(slice_rows, dtype=jnp.int32)) // TILE
    column_local = (narrow_index * stripe + jnp.arange(stripe, dtype=jnp.int32)) // TILE
    row_blocks = pick_blocks(region_tiles, row_local)
    column_blocks = pick_blocks(region_tiles, column_local)
    matches = row_blocks[:, :, None] == column_blocks[:, None, :]
    masked = jnp.where(
        matches, integrals.reshape(wide_count, slice_rows, stripe), jnp.zeros((), integrals.dtype)
    )
    occ_count = occ_energy.shape[0]
    choosers = (
        occ_pairs.reshape(-1)[:, None] == jnp.arange(occ_count, dtype=jnp.int32)[None, :]
    ).astype(jnp.float32)
    energies = jnp.dot(choosers, occ_energy, precision=lax.Precision.HIGHEST).reshape(
        occ_pairs.shape[0], 2
    )
    occupied_sum = energies[:, 0] + energies[:, 1]
    denominator = occupied_sum[:, None] - pair_energy[None, :]
    stripes = lax.all_to_all(amplitudes, "ka", split_axis=1, concat_axis=0, tiled=True)
    partial_value = jnp.einsum(
        "ic,dac->ida",
        stripes,
        lax.all_to_all(masked, "ta", split_axis=0, concat_axis=0, tiled=True),
        preferred_element_type=jnp.float32,
    )
    ladder = lax.psum_scatter(
        partial_value.reshape(partial_value.shape[0], region).astype(jnp.bfloat16),
        "ka",
        scatter_dimension=0,
        tiled=True,
    ).astype(jnp.float32)
    residual = other_terms.astype(jnp.float32) + ladder
    return residual / denominator


def solution(mesh):
    return jax.shard_map(
        shards,
        mesh=mesh,
        in_specs=(P("ka", "ta"), P("ta", "ka"), P("ka", "ta"), P(), P("ka", None), P(), P("ta")),
        out_specs=P("ka", "ta"),
        check_vma=False,
    )
```

profile of v0, /device:TPU:8, one launch (start us, length us, event | category | flops | bytes accessed | tf_op | source)
XLA Modules:
  0.0 202.3 jit_solution(7916339985247155783)
XLA Ops:
  6.5 0.0 copy-start
  6.5 2.0 copy.16
  8.5 8.5 %all-to-all-start.1 = ((bf16[64,8,640]{2,0,1:T(8,128)(2,1)}), bf16[64,8,640]{2,0,1:T(8,128)(2,1)S(1)}, u32[]{:S(2)}, u32[]{:S(2)}) async-start(bf16[64,8,640]{2,0,1:T(8,128)(2,1)} %bitcast.24), calls=%async_computation.1 | async-start | bytes 1310720 | tf_op jit(solution)/shard_map/all_to_all | solution.py:42
  17.0 0.0 reduce-scatter.2.cloned.1.call-start
  17.1 0.7 convert_element_type.25
  17.8 0.1 convert_element_type.26
  17.9 0.4 convolution_bitcast_fusion
  18.3 0.3 convolution_bitcast_fusion.1
  18.6 6.9 %compare_select_fusion = bf16[32,160,640]{2,1,0:T(8,128)(2,1)} fusion(bf16[32,160,640]{2,1,0:T(8,128)(2,1)} %bitcast.26, f32[32,640]{1,0:T(8,128)S(1)} %convolution_bitcast_fusion, f32[32,160]{1,0:T(8,128)S(1)} %convolution_bitcast_fusion.1), kind=kLoop, calls=%fused_computation | loop fusion | flops 6553600 | bytes 13209600 | tf_op jit(solution)/shard_map/jit(_where)/select_n | solution.py:30
  25.5 11.8 %all-to-all-done.1 = bf16[64,8,640]{2,0,1:T(8,128)(2,1)S(1)} async-done(((bf16[64,8,640]{2,0,1:T(8,128)(2,1)}), bf16[64,8,640]{2,0,1:T(8,128)(2,1)S(1)}, u32[]{:S(2)}, u32[]{:S(2)}) %all-to-all-start.1) | async-done | bytes 655392 | tf_op jit(solution)/shard_map/all_to_all | solution.py:42
  37.3 82.3 %all_to_all.24 = bf16[32,160,640]{2,1,0:T(8,128)(2,1)S(1)} all-to-all(bf16[32,160,640]{2,1,0:T(8,128)(2,1)} %compare_select_fusion), channel_id=1, replica_groups=mesh['ta'=32,'ka'=8] {'ta'}, dimensions={0} | all-to-all | bytes 13107200 | tf_op jit(solution)/shard_map/all_to_all | solution.py:46
  119.6 6.0 %convolution_convert_fusion = bf16[32,160,512]{2,1,0:T(8,128)(2,1)} fusion(bf16[32,160,640]{2,1,0:T(8,128)(2,1)S(1)} %all_to_all.24, bf16[512,640,1]{1,0,2:T(8,128)(2,1)S(1)} %bitcast.29), kind=kOutput, calls=%fused_computation.1 | convolution fusion | flops 3358064640 | bytes 12451840 | tf_op jit(solution)/shard_map/ic,dac->ida/dot_general | solution.py:43
  125.7 0.0 copy-start.3
  125.7 0.0 copy-start.1
  125.7 0.0 copy-start.2
  125.7 8.0 %copy.12 = bf16[512,5120]{1,0:T(8,128)(2,1)} copy(bf16[512,5120]{0,1:T(8,128)(2,1)} %bitcast.27) | data formatting | bytes 10485760 | tf_op jit(solution)/shard_map/convert_element_type | solution.py:50
  133.6 0.0 reduce-scatter.2.cloned.1.call-update
  133.6 0.0 copy-done.3
  133.6 0.1 copy.13
  133.7 0.1 eq.63
  133.9 0.0 copy-done
  133.9 0.2 convolution_bitcast_fusion.2
  134.1 0.2 reshape.56
  134.3 0.2 fusion.3
  134.5 58.5 %reduce-scatter.2.cloned.1.call-done = bf16[64,5120]{1,0:T(8,128)(2,1)} async-done(((bf16[512,5120]{1,0:T(8,128)(2,1)}), bf16[64,5120]{1,0:T(8,128)(2,1)}) %reduce-scatter.2.cloned.1.call-update) | async-done | bytes 655376 | tf_op jit(solution)/shard_map/reduce_scatter | solution.py:49
  193.0 0.0 copy-done.1
  193.0 0.0 copy-done.2
  193.0 2.5 %subtract_divide_fusion = f32[64,5120]{1,0:T(8,128)} fusion(bf16[64,5120]{1,0:T(8,128)(2,1)} %reduce-scatter.2.cloned.1.call-done, bf16[64,5120]{1,0:T(8,128)(2,1)S(1)} %copy-done.1, f32[5120]{0:T(1024)S(1)} %copy-done.2, f32[64]{0:T(128)S(1)} %fusion.3), kind=kLoop, calls=%fused_computation.2 | loop fusion | flops 1638400 | bytes 2642176 | tf_op jit(solution)/shard_map/div | solution.py:56
  (2 shorter events, 0.0 us)
Async XLA Ops:
  6.5 127.3 %copy-start = (f32[150]{0:T(256)S(1)}, f32[150]{0:T(256)}, u32[]{:S(2)}) copy-start(f32[150]{0:T(256)} %param.12) | copy-start | bytes 1804
  8.5 28.8 %all-to-all-start.1 = ((bf16[64,8,640]{2,0,1:T(8,128)(2,1)}), bf16[64,8,640]{2,0,1:T(8,128)(2,1)S(1)}, u32[]{:S(2)}, u32[]{:S(2)}) async-start(bf16[64,8,640]{2,0,1:T(8,128)(2,1)} %bitcast.24), calls=%async_computation.1 | async-start | bytes 1310720 | tf_op jit(solution)/shard_map/all_to_all | solution.py:42
  17.0 176.0 %reduce-scatter.2.cloned.1.call-start = ((), (), s32[]{:S(2)}) async-start(), calls=%async_computation.3 | async-start | bytes 5898240 | tf_op jit(solution)/shard_map/reduce_scatter | solution.py:49
  125.7 8.0 %copy-start.3 = (s32[64,2]{0,1:T(2,128)S(1)}, s32[64,2]{0,1:T(2,128)}, u32[]{:S(2)}) copy-start(s32[64,2]{0,1:T(2,128)} %param.11) | copy-start | bytes 1540
  125.7 67.4 %copy-start.1 = (bf16[64,5120]{1,0:T(8,128)(2,1)S(1)}, bf16[64,5120]{1,0:T(8,128)(2,1)}, u32[]{:S(2)}) copy-start(bf16[64,5120]{1,0:T(8,128)(2,1)} %param.9) | copy-start | bytes 1966084
  125.7 67.4 %copy-start.2 = (f32[5120]{0:T(1024)S(1)}, f32[5120]{0:T(1024)}, u32[]{:S(2)}) copy-start(f32[5120]{0:T(1024)} %param.13) | copy-start | bytes 61444
Sparse Core Ops, SparseCore 0:
  133.8 59.2 reduce-scatter.1
where the time goes:
time: 204 us; the launch traced here: 202 us
  blocking collectives  82.3 us (40%)
  waiting for transfers between devices  70.4 us (35%)
  between operations  13.5 us (7%)
  local copies, waits for them, and re-layouts  10.5 us (5%)
  other arithmetic  10.3 us (5%)
  starting transfers between devices  8.5 us (4%)
  matrix products  6.91 us (3%)
    all_to_all x1, blocking collectives, shards(): lax.all_to_all(masked, 'ta', split_axis=0, concat_axis=0, tiled=True)  82.3 us
    reduce_scatter x1, waiting for transfers between devices, shards(): lax.psum_scatter(partial_value.reshape(partial_value.shape[0], region).as...  58.5 us
    all_to_all x1, waiting for transfers between devices, shards(): lax.all_to_all(amplitudes, 'ka', split_axis=1, concat_axis=0, tiled=True)  11.8 us
    all_to_all x1, starting transfers between devices, shards(): lax.all_to_all(amplitudes, 'ka', split_axis=1, concat_axis=0, tiled=True)  8.47 us
    convert_element_type x1, local copies, waits for them, and re-layouts, shards(): partial_value.reshape(partial_value.shape[0], region).astype(jnp.bfloat16)  7.95 us
    select_n x1, other arithmetic, shards(): jnp.where(matches, integrals.reshape(wide_count, slice_rows, stripe), jnp...  6.88 us
    dot_general x1, matrix products, shards(): jnp.einsum('ic,dac->ida', stripes, lax.all_to_all(masked, 'ta', split_axi...  6.03 us
  transfers between devices with their start and end apart: 2, of which 2 were waited for; matrix products, arithmetic and copies ran while one was open for 5% of the time, Pallas kernels for 0%

commit v1 on v0

v1 whole, which is shorter than its diff:
```python
import jax
import jax.numpy as jnp
from jax import lax
from jax.experimental import pallas as pl
from jax.experimental.pallas import tpu as pltpu
from jax.sharding import PartitionSpec as P

TILE = 128
UNIT = 32
STEP = 512


def block_of(tiles, index):
    picker = (index[:, None] == jnp.arange(tiles.shape[0], dtype=jnp.int32)[None, :]).astype(jnp.float32)
    return jnp.dot(picker, tiles, precision=lax.Precision.HIGHEST)


def gather_kernel(index_ref, *refs):
    stripes, window_ref = refs[:-1], refs[-1]
    rows = stripes[0].shape[0]
    for step, stripe in enumerate(stripes):
        slot = lax.rem(index_ref[0] + step, len(stripes))
        window_ref[pl.ds(pl.multiple_of(slot * rows, rows), rows), :] = stripe[...]


def gather(index, stripes):
    rows, width = stripes[0].shape
    return pl.pallas_call(
        gather_kernel,
        in_specs=[pl.BlockSpec(memory_space=pltpu.SMEM)] + [pl.BlockSpec(memory_space=pltpu.VMEM)] * len(stripes),
        out_specs=pl.BlockSpec(memory_space=pltpu.VMEM),
        out_shape=jax.ShapeDtypeStruct((rows * len(stripes), width), stripes[0].dtype),
        name="gather_window",
    )(index, *stripes)


def product_kernel(keep_ref, window_ref, rows_ref, out_ref, masked_ref):
    for unit in range(masked_ref.shape[0] // UNIT):
        rows = pl.ds(unit * UNIT, UNIT)
        keep = keep_ref[unit : unit + 1, :].astype(jnp.bfloat16)
        masked_ref[rows, :] = rows_ref[rows, :] * keep
    out_ref[...] = lax.dot_general(
        window_ref[...], masked_ref[...], (((1,), (1,)), ((), ())), preferred_element_type=jnp.float32
    ).astype(jnp.bfloat16)


def product(window, rows, keep):
    occ, stripe = window.shape
    count = rows.shape[0]
    return pl.pallas_call(
        product_kernel,
        grid=(count // STEP,),
        in_specs=[
            pl.BlockSpec((STEP // UNIT, stripe), lambda t: (t, 0)),
            pl.BlockSpec((occ, stripe), lambda t: (0, 0)),
            pl.BlockSpec((STEP, stripe), lambda t: (t, 0)),
        ],
        out_specs=pl.BlockSpec((occ, STEP), lambda t: (0, t)),
        out_shape=pltpu.HBM((occ, count), jnp.bfloat16),
        scratch_shapes=[pltpu.VMEM((STEP, stripe), jnp.bfloat16)],
        compiler_params=pltpu.CompilerParams(vmem_limit_bytes=16 * 1024 * 1024),
        cost_estimate=pl.CostEstimate(
            flops=2 * occ * stripe * count,
            bytes_accessed=2 * (occ * stripe + count * stripe + occ * count),
            transcendentals=0,
        ),
        name="product",
    )(keep, window, rows)


def shards(amplitudes, integrals, other_terms, tile_block, occ_pairs, occ_energy, pair_energy):
    wide_count = lax.axis_size("ta")
    wide_index = lax.axis_index("ta")
    narrow_count = lax.axis_size("ka")
    narrow_index = lax.axis_index("ka")
    region, stripe = integrals.shape
    slice_rows = region // wide_count
    region_tiles = region // TILE

    stripes = []
    for step in range(narrow_count):
        column = lax.rem(narrow_index + narrow_count - step, narrow_count) * stripe
        part = lax.dynamic_slice(amplitudes, (0, column), (amplitudes.shape[0], stripe))
        pairs = [(i, (i + narrow_count - step) % narrow_count) for i in range(narrow_count)]
        stripes.append(lax.ppermute(part, "ka", pairs) if step else part)
    window = gather(narrow_index.reshape(1), stripes)

    arrived = lax.all_to_all(
        integrals.reshape(wide_count, slice_rows, stripe), "ta", split_axis=0, concat_axis=0, tiled=True
    ).reshape(region, stripe)

    tiles = lax.dynamic_slice(tile_block, (wide_index * region_tiles,), (region_tiles,)).astype(jnp.float32)
    columns = (narrow_index * stripe + jnp.arange(stripe, dtype=jnp.int32)) // TILE
    units = jnp.arange(region // UNIT, dtype=jnp.int32) * UNIT // TILE
    keep = (block_of(tiles, units)[:, None] == block_of(tiles, columns)[None, :]).astype(jnp.float32)

    occ_count = occ_energy.shape[0]
    choosers = (
        occ_pairs.reshape(-1)[:, None] == jnp.arange(occ_count, dtype=jnp.int32)[None, :]
    ).astype(jnp.float32)
    energies = jnp.dot(choosers, occ_energy, precision=lax.Precision.HIGHEST).reshape(occ_pairs.shape[0], 2)
    occupied_sum = energies[:, 0] + energies[:, 1]
    denominator = occupied_sum[:, None] - pair_energy[None, :]

    shares = product(window, arrived, keep)
    ladder = lax.psum_scatter(shares, "ka", scatter_dimension=0, tiled=True).astype(jnp.float32)
    residual = other_terms.astype(jnp.float32) + ladder
    return residual / denominator


def solution(mesh):
    return jax.shard_map(
        shards,
        mesh=mesh,
        in_specs=(P("ka", "ta"), P("ta", "ka"), P("ka", "ta"), P(), P("ka", None), P(), P("ta")),
        out_specs=P("ka", "ta"),
        check_vma=False,
    )
```

time: 204 us -> 201 us (0.985)
  blocking collectives: 82.3 us -> 0 us
  waiting for transfers between devices: 70.4 us -> 139 us
  starting transfers between devices: 8.5 us -> 25 us
  Pallas kernels: 0 us -> 13.3 us
  other arithmetic: 10.3 us -> 2.77 us
  local copies, waits for them, and re-layouts: 10.5 us -> 3.52 us
  matrix products: 6.91 us -> 2.25 us
    all_to_all x1 -> x0, blocking collectives: 82.3 us -> none  [shards(): lax.all_to_all(masked, 'ta', split_axis=0, concat_axis=0, tiled=True)]
    all_to_all x1, waiting for transfers between devices: 11.8 us -> 64.4 us  [shards(): lax.all_to_all(integrals.reshape(wide_count, slice_rows, stripe), 'ta', s...]
    ppermute x0 -> x7, starting transfers between devices: none -> 17.2 us  [shards(): stripes.append(lax.ppermute(part, 'ka', pairs) if step else part)]
    pallas_call x0 -> x2, Pallas kernels: none -> 13.3 us  [the longest x1 11.2 us: product(): pl.pallas_call(product_kernel, grid=(count // STEP,), in_specs=[pl.BlockS...]
    ppermute x0 -> x7, waiting for transfers between devices: none -> 8.23 us  [shards(): stripes.append(lax.ppermute(part, 'ka', pairs) if step else part)]
    convert_element_type x2 -> x0, local copies, waits for them, and re-layouts: 8.03 us -> none  [the longest x1 7.95 us: shards(): partial_value.reshape(partial_value.shape[0], region).astype(jnp.bfloat16)]
    reduce_scatter x1, waiting for transfers between devices: 58.5 us -> 66.1 us  [shards(): lax.psum_scatter(shares, 'ka', scatter_dimension=0, tiled=True)]
    select_n x2 -> x1, other arithmetic: 6.89 us -> 0.01 us  [shards(): units = jnp.arange(region // UNIT, dtype=jnp.int32) * UNIT // TILE]
  transfers between devices with their start and end apart: 2 -> 9, of which waited for: 2 -> 5; matrix products, arithmetic and copies ran while one was open for 5% -> 2% of each run, Pallas kernels for 0% -> 1%
where the time goes in v1:
time: 201 us; the launch traced here: 199 us
  waiting for transfers between devices  139 us (69%)
  starting transfers between devices  25 us (12%)
  between operations  13.6 us (7%)
  Pallas kernels  13.3 us (7%)
  local copies, waits for them, and re-layouts  3.52 us (2%)
  other arithmetic  2.77 us (1%)
  matrix products  2.25 us (1%)
    reduce_scatter x1, waiting for transfers between devices, shards(): lax.psum_scatter(shares, 'ka', scatter_dimension=0, tiled=True)  66.1 us
    all_to_all x1, waiting for transfers between devices, shards(): lax.all_to_all(integrals.reshape(wide_count, slice_rows, stripe), 'ta', s...  64.4 us
    ppermute x7, starting transfers between devices, shards(): stripes.append(lax.ppermute(part, 'ka', pairs) if step else part)  17.2 us
    pallas_call x1, Pallas kernels, product(): pl.pallas_call(product_kernel, grid=(count // STEP,), in_specs=[pl.BlockS...  11.2 us
    ppermute x7, waiting for transfers between devices, shards(): stripes.append(lax.ppermute(part, 'ka', pairs) if step else part)  8.23 us
    all_to_all x1, starting transfers between devices, shards(): lax.all_to_all(integrals.reshape(wide_count, slice_rows, stripe), 'ta', s...  7.72 us
  transfers between devices with their start and end apart: 9, of which 5 were waited for; matrix products, arithmetic and copies ran while one was open for 2% of the time, Pallas kernels for 1%

profile of v1, /device:TPU:8, one launch (start us, length us, event | category | flops | bytes accessed | tf_op | source)
XLA Modules:
  0.0 199.2 jit_solution(12828494759555681640)
XLA Ops:
  6.5 0.0 copy-start
  6.5 7.7 %all-to-all-start = ((bf16[32,160,640]{2,1,0:T(8,128)(2,1)}), bf16[32,160,640]{2,1,0:T(8,128)(2,1)}, u32[]{:S(2)}, u32[]{:S(2)}) async-start(bf16[32,160,640]{2,1,0:T(8,128)(2,1)} %bitcast.14), calls=%async_computation | async-start | bytes 13107200 | tf_op jit(solution)/shard_map/all_to_all | solution.py:88
  14.3 0.0 reduce-scatter.2.cloned.1.call-start
  14.4 0.0 copy-done.2
  14.4 0.7 constant_dynamic-slice_fusion
  15.1 5.9 %collective-permute-start = (bf16[64,640]{1,0:T(8,128)(2,1)S(1)}, bf16[64,640]{1,0:T(8,128)(2,1)S(1)}, u32[]{:S(2)}, u32[]{:S(2)}) collective-permute-start(bf16[64,640]{1,0:T(8,128)(2,1)S(1)} %get-tuple-element.10), channel_id=1, source_target_pairs={{0,7},{1,0},{2,1},{3,2},{4,3},{5,4},{6,5},{7,6},{8,15},{9,8},{10,9... | collective-permute-start | bytes 245768 | tf_op jit(solution)/shard_map/ppermute | solution.py:85
  21.0 1.5 collective-permute-start.1
  22.4 0.4 collective-permute-start.2
  22.9 5.0 %collective-permute-start.3 = (bf16[64,640]{1,0:T(8,128)(2,1)S(1)}, bf16[64,640]{1,0:T(8,128)(2,1)S(1)}, u32[]{:S(2)}, u32[]{:S(2)}) collective-permute-start(bf16[64,640]{1,0:T(8,128)(2,1)S(1)} %get-tuple-element.7), channel_id=1, source_target_pairs={{0,4},{1,5},{2,6},{3,7},{4,0},{5,1},{6,2},{7,3},{8,12},{9,13},{10,... | collective-permute-start | bytes 245768 | tf_op jit(solution)/shard_map/ppermute | solution.py:85
  27.9 0.0 collective-permute-start.4
  27.9 0.9 fusion.1
  28.8 1.2 convolution_reduce_fusion
  30.0 0.0 collective-permute-done.refs_1_
  30.0 0.0 copy-start.4
  30.0 2.5 %collective-permute-start.5 = (bf16[64,640]{1,0:T(8,128)(2,1)S(1)}, bf16[64,640]{1,0:T(8,128)(2,1)S(1)}, u32[]{:S(2)}, u32[]{:S(2)}) collective-permute-start(bf16[64,640]{1,0:T(8,128)(2,1)S(1)} %get-tuple-element.12), channel_id=1, source_target_pairs={{0,2},{1,3},{2,4},{3,5},{4,6},{5,7},{6,0},{7,1},{8,10},{9,11},{10,... | collective-permute-start | bytes 245768 | tf_op jit(solution)/shard_map/ppermute | solution.py:85
  32.6 0.0 collective-permute-done.1.refs_2_
  32.6 1.9 collective-permute-start.6
  34.5 0.1 compare_convert_fusion.keep_ref
  34.6 0.0 collective-permute-done.2.refs_3_
  34.6 0.0 copy-start.6
  34.6 0.0 collective-permute-done.3.refs_4_
  34.6 0.0 copy-start.7
  34.6 4.7 %collective-permute-done.4.refs_5_ = bf16[64,640]{1,0:T(8,128)(2,1)S(1)} collective-permute-done((bf16[64,640]{1,0:T(8,128)(2,1)S(1)}, bf16[64,640]{1,0:T(8,128)(2,1)S(1)}, u32[]{:S(2)}, u32[]{:S(2)}) %collective-permute-start.4) | collective-permute-done | bytes 81952 | tf_op jit(solution)/shard_map/ppermute | solution.py:85
  39.4 2.9 %collective-permute-done.5.refs_6_ = bf16[64,640]{1,0:T(8,128)(2,1)S(1)} collective-permute-done((bf16[64,640]{1,0:T(8,128)(2,1)S(1)}, bf16[64,640]{1,0:T(8,128)(2,1)S(1)}, u32[]{:S(2)}, u32[]{:S(2)}) %collective-permute-start.5) | collective-permute-done | bytes 81952 | tf_op jit(solution)/shard_map/ppermute | solution.py:85
  42.2 0.6 collective-permute-done.6.refs_7_
  42.8 0.0 copy-done.4
  42.8 0.0 copy-done.5
  42.8 0.0 copy-done.6
  42.9 0.0 copy-done.7
  42.9 0.0 copy-done.8
  42.9 0.0 copy-done.9
  42.9 0.6 copy-done.10
  43.5 2.1 %gather_window.1.window_ref = bf16[512,640]{1,0:T(8,128)(2,1)} custom-call(s32[1]{0:T(128)} %bitcast.3.index_ref, bf16[64,640]{1,0:T(8,128)(2,1)} %get-tuple-element.11.refs_0_, bf16[64,640]{1,0:T(8,128)(2,1)} %copy-done.4, bf16[64,640]{1,0:T(8,128)(2,1)} %copy-done.5, bf16[64,640]{1,0:T(8,128)(2,1)} %copy-done.6, bf16[64,640]{1,0:T(8,128)(2,1)} %copy-done.7, ...), custom_call_target="tpu_custom_call" | custom-call | tf_op jit(solution)/shard_map/gather_window/pallas_call | solution.py:28
  45.5 64.4 %all-to-all-done = bf16[32,160,640]{2,1,0:T(8,128)(2,1)} async-done(((bf16[32,160,640]{2,1,0:T(8,128)(2,1)}), bf16[32,160,640]{2,1,0:T(8,128)(2,1)}, u32[]{:S(2)}, u32[]{:S(2)}) %all-to-all-start) | async-done | bytes 6553632 | tf_op jit(solution)/shard_map/all_to_all | solution.py:88
  110.0 1.1 copy-done.1
  111.1 11.2 %product.1 = bf16[512,5120]{1,0:T(8,128)(2,1)} custom-call(f32[160,640]{1,0:T(8,128)S(1)} %compare_convert_fusion.keep_ref, bf16[512,640]{1,0:T(8,128)(2,1)S(1)} %copy-done.1, bf16[5120,640]{1,0:T(8,128)(2,1)} %bitcast.5.rows_ref), custom_call_target="tpu_custom_call" | custom-call | flops 3355443200 | bytes 12451840 | tf_op jit(solution)/shard_map/product/pallas_call | solution.py:50
  122.3 0.0 reduce-scatter.2.cloned.1.call-update
  122.3 0.6 copy-done.12
  123.0 0.1 copy.9
  123.1 0.1 eq.63
  123.2 0.0 copy-done
  123.2 0.2 convolution_bitcast_fusion
  123.4 0.2 reshape.57
  123.6 0.2 fusion.4
  123.8 66.1 %reduce-scatter.2.cloned.1.call-done = bf16[64,5120]{1,0:T(8,128)(2,1)} async-done(((bf16[512,5120]{1,0:T(8,128)(2,1)}), bf16[64,5120]{1,0:T(8,128)(2,1)}) %reduce-scatter.2.cloned.1.call-update) | async-done | bytes 655376 | tf_op jit(solution)/shard_map/reduce_scatter | solution.py:106
  189.9 0.0 copy-done.3
  189.9 0.0 copy-done.11
  189.9 2.5 %subtract_divide_fusion = f32[64,5120]{1,0:T(8,128)} fusion(bf16[64,5120]{1,0:T(8,128)(2,1)} %reduce-scatter.2.cloned.1.call-done, bf16[64,5120]{1,0:T(8,128)(2,1)S(1)} %copy-done.3, f32[5120]{0:T(1024)S(1)} %copy-done.11, f32[64]{0:T(128)S(1)} %fusion.4), kind=kLoop, calls=%fused_computation | loop fusion | flops 1638400 | bytes 2642176 | tf_op jit(solution)/shard_map/div | solution.py:108
  (11 shorter events, 0.0 us)
Async XLA Ops:
  6.5 116.7 %copy-start = (f32[150]{0:T(256)S(1)}, f32[150]{0:T(256)}, u32[]{:S(2)}) copy-start(f32[150]{0:T(256)} %param.12) | copy-start | bytes 1804
  6.5 7.8 %copy-start.2 = (bf16[64,5120]{1,0:T(8,128)(2,1)S(1)}, bf16[64,5120]{1,0:T(8,128)(2,1)}, u32[]{:S(2)}) copy-start(bf16[64,5120]{1,0:T(8,128)(2,1)} %param.7) | copy-start | bytes 1966084
  6.5 103.4 %all-to-all-start = ((bf16[32,160,640]{2,1,0:T(8,128)(2,1)}), bf16[32,160,640]{2,1,0:T(8,128)(2,1)}, u32[]{:S(2)}, u32[]{:S(2)}) async-start(bf16[32,160,640]{2,1,0:T(8,128)(2,1)} %bitcast.14), calls=%async_computation | async-start | bytes 13107200 | tf_op jit(solution)/shard_map/all_to_all | solution.py:88
  14.3 175.6 %reduce-scatter.2.cloned.1.call-start = ((), (), s32[]{:S(2)}) async-start(), calls=%async_computation.2 | async-start | bytes 5898240 | tf_op jit(solution)/shard_map/reduce_scatter | solution.py:106
  15.1 14.9 %collective-permute-start = (bf16[64,640]{1,0:T(8,128)(2,1)S(1)}, bf16[64,640]{1,0:T(8,128)(2,1)S(1)}, u32[]{:S(2)}, u32[]{:S(2)}) collective-permute-start(bf16[64,640]{1,0:T(8,128)(2,1)S(1)} %get-tuple-element.10), channel_id=1, source_target_pairs={{0,7},{1,0},{2,1},{3,2},{4,3},{5,4},{6,5},{7,6},{8,15},{9,8},{10,9... | collective-permute-start | bytes 245768 | tf_op jit(solution)/shard_map/ppermute | solution.py:85
  21.0 11.6 %collective-permute-start.1 = (bf16[64,640]{1,0:T(8,128)(2,1)S(1)}, bf16[64,640]{1,0:T(8,128)(2,1)S(1)}, u32[]{:S(2)}, u32[]{:S(2)}) collective-permute-start(bf16[64,640]{1,0:T(8,128)(2,1)S(1)} %get-tuple-element.9), channel_id=1, source_target_pairs={{0,6},{1,7},{2,0},{3,1},{4,2},{5,3},{6,4},{7,5},{8,14},{9,15},{10,... | collective-permute-start | bytes 245768 | tf_op jit(solution)/shard_map/ppermute | solution.py:85
  22.4 12.2 %collective-permute-start.2 = (bf16[64,640]{1,0:T(8,128)(2,1)S(1)}, bf16[64,640]{1,0:T(8,128)(2,1)S(1)}, u32[]{:S(2)}, u32[]{:S(2)}) collective-permute-start(bf16[64,640]{1,0:T(8,128)(2,1)S(1)} %get-tuple-element.8), channel_id=1, source_target_pairs={{0,5},{1,6},{2,7},{3,0},{4,1},{5,2},{6,3},{7,4},{8,13},{9,14},{10,... | collective-permute-start | bytes 245768 | tf_op jit(solution)/shard_map/ppermute | solution.py:85
  22.9 11.7 %collective-permute-start.3 = (bf16[64,640]{1,0:T(8,128)(2,1)S(1)}, bf16[64,640]{1,0:T(8,128)(2,1)S(1)}, u32[]{:S(2)}, u32[]{:S(2)}) collective-permute-start(bf16[64,640]{1,0:T(8,128)(2,1)S(1)} %get-tuple-element.7), channel_id=1, source_target_pairs={{0,4},{1,5},{2,6},{3,7},{4,0},{5,1},{6,2},{7,3},{8,12},{9,13},{10,... | collective-permute-start | bytes 245768 | tf_op jit(solution)/shard_map/ppermute | solution.py:85
  27.9 11.5 %collective-permute-start.4 = (bf16[64,640]{1,0:T(8,128)(2,1)S(1)}, bf16[64,640]{1,0:T(8,128)(2,1)S(1)}, u32[]{:S(2)}, u32[]{:S(2)}) collective-permute-start(bf16[64,640]{1,0:T(8,128)(2,1)S(1)} %get-tuple-element.6), channel_id=1, source_target_pairs={{0,3},{1,4},{2,5},{3,6},{4,7},{5,0},{6,1},{7,2},{8,11},{9,12},{10,... | collective-permute-start | bytes 245768 | tf_op jit(solution)/shard_map/ppermute | solution.py:85
  30.0 12.8 %copy-start.4 = (bf16[64,640]{1,0:T(8,128)(2,1)}, bf16[64,640]{1,0:T(8,128)(2,1)S(1)}, u32[]{:S(2)}) copy-start(bf16[64,640]{1,0:T(8,128)(2,1)S(1)} %collective-permute-done.refs_1_) | copy-start | bytes 245764
  30.0 12.2 %collective-permute-start.5 = (bf16[64,640]{1,0:T(8,128)(2,1)S(1)}, bf16[64,640]{1,0:T(8,128)(2,1)S(1)}, u32[]{:S(2)}, u32[]{:S(2)}) collective-permute-start(bf16[64,640]{1,0:T(8,128)(2,1)S(1)} %get-tuple-element.12), channel_id=1, source_target_pairs={{0,2},{1,3},{2,4},{3,5},{4,6},{5,7},{6,0},{7,1},{8,10},{9,11},{10,... | collective-permute-start | bytes 245768 | tf_op jit(solution)/shard_map/ppermute | solution.py:85
  32.6 10.3 %copy-start.5 = (bf16[64,640]{1,0:T(8,128)(2,1)}, bf16[64,640]{1,0:T(8,128)(2,1)S(1)}, u32[]{:S(2)}) copy-start(bf16[64,640]{1,0:T(8,128)(2,1)S(1)} %collective-permute-done.1.refs_2_) | copy-start | bytes 245764
  32.6 10.3 %collective-permute-start.6 = (bf16[64,640]{1,0:T(8,128)(2,1)S(1)}, bf16[64,640]{1,0:T(8,128)(2,1)S(1)}, u32[]{:S(2)}, u32[]{:S(2)}) collective-permute-start(bf16[64,640]{1,0:T(8,128)(2,1)S(1)} %get-tuple-element.5), channel_id=1, source_target_pairs={{0,1},{1,2},{2,3},{3,4},{4,5},{5,6},{6,7},{7,0},{8,9},{9,10},{10,1... | collective-permute-start | bytes 245768 | tf_op jit(solution)/shard_map/ppermute | solution.py:85
  34.6 8.3 %copy-start.6 = (bf16[64,640]{1,0:T(8,128)(2,1)}, bf16[64,640]{1,0:T(8,128)(2,1)S(1)}, u32[]{:S(2)}) copy-start(bf16[64,640]{1,0:T(8,128)(2,1)S(1)} %collective-permute-done.2.refs_3_) | copy-start | bytes 245764
  34.6 8.2 %copy-start.7 = (bf16[64,640]{1,0:T(8,128)(2,1)}, bf16[64,640]{1,0:T(8,128)(2,1)S(1)}, u32[]{:S(2)}) copy-start(bf16[64,640]{1,0:T(8,128)(2,1)S(1)} %collective-permute-done.3.refs_4_) | copy-start | bytes 245764
  39.4 3.5 %copy-start.8 = (bf16[64,640]{1,0:T(8,128)(2,1)}, bf16[64,640]{1,0:T(8,128)(2,1)S(1)}, u32[]{:S(2)}) copy-start(bf16[64,640]{1,0:T(8,128)(2,1)S(1)} %collective-permute-done.4.refs_5_) | copy-start | bytes 245764
  42.2 0.6 copy-start.9
  42.8 0.6 copy-start.10
  110.0 1.1 copy-start.1
  122.3 0.7 copy-start.12
  122.3 67.6 %copy-start.3 = (bf16[64,5120]{1,0:T(8,128)(2,1)S(1)}, bf16[64,5120]{1,0:T(8,128)(2,1)}, u32[]{:S(2)}) copy-start(bf16[64,5120]{1,0:T(8,128)(2,1)} %param.9) | copy-start | bytes 1966084
  122.3 67.6 %copy-start.11 = (f32[5120]{0:T(1024)S(1)}, f32[5120]{0:T(1024)}, u32[]{:S(2)}) copy-start(f32[5120]{0:T(1024)} %param.13) | copy-start | bytes 61444
Sparse Core Ops, SparseCore 0:
  122.4 67.3 reduce-scatter.1

commit v2 on v1

v2 whole, which is shorter than its diff:
```python
import jax
import jax.numpy as jnp
from jax import lax
from jax.experimental import pallas as pl
from jax.experimental.pallas import tpu as pltpu
from jax.sharding import PartitionSpec as P

TILE = 128
UNIT = 16
COST = pl.CostEstimate(flops=1000, bytes_accessed=1000, transcendentals=0)
CHUNKS = (112, 48)
STEPS = (896, 768)
SPAN = 1280


def block_of(tiles, index):
    picker = (index[:, None] == jnp.arange(tiles.shape[0], dtype=jnp.int32)[None, :]).astype(jnp.float32)
    return jnp.dot(picker, tiles, precision=lax.Precision.HIGHEST)


def gather(stripes, held):
    count = len(stripes)
    rows, width = stripes[0].shape

    def kernel(*refs):
        window_ref = refs[count + len(held)]
        for slot, stripe in enumerate(refs[:count]):
            window_ref[slot * rows : (slot + 1) * rows, :] = stripe[...]

    vmem, anywhere = pl.BlockSpec(memory_space=pltpu.VMEM), pl.BlockSpec(memory_space=pl.ANY)
    window, *held = pl.pallas_call(
        kernel,
        in_specs=[vmem] * count + [anywhere] * len(held),
        out_specs=[vmem] + [anywhere] * len(held),
        out_shape=[jax.ShapeDtypeStruct((rows * count, width), stripes[0].dtype)]
        + [pltpu.HBM(h.shape, h.dtype) for h in held],
        input_output_aliases={count + n: 1 + n for n in range(len(held))},
        name="gather_window",
    )(*stripes, *held)
    return window, held


def product_kernel(keep_ref, window_ref, rows_ref, *refs):
    outs, masked_ref = refs[:-1], refs[-1]
    window = outs[0].shape[0]
    for unit in range(masked_ref.shape[0] // UNIT):
        rows = pl.ds(unit * UNIT, UNIT)
        keep = keep_ref[unit : unit + 1, :].astype(jnp.bfloat16)
        masked_ref[rows, :] = rows_ref[rows, :] * keep
    shares = lax.dot_general(
        window_ref[...], masked_ref[...], (((1,), (1,)), ((), ())), preferred_element_type=jnp.float32
    ).astype(jnp.bfloat16)
    for slot, out in enumerate(outs):
        out[...] = shares[slot * window : (slot + 1) * window]


def product(window, rows, keep, slots, step):
    occ, stripe = window.shape
    count = rows.shape[0]
    return pl.pallas_call(
        product_kernel,
        grid=(count // step,),
        in_specs=[
            pl.BlockSpec((step // UNIT, stripe), lambda t: (t, 0)),
            pl.BlockSpec((occ, stripe), lambda t: (0, 0)),
            pl.BlockSpec((step, stripe), lambda t: (t, 0)),
        ],
        out_specs=[pl.BlockSpec((occ // slots, step), lambda t: (0, t))] * slots,
        out_shape=[pltpu.HBM((occ // slots, count), jnp.bfloat16)] * slots,
        scratch_shapes=[pltpu.VMEM((step, stripe), jnp.bfloat16)],
        compiler_params=pltpu.CompilerParams(vmem_limit_bytes=24 * 1024 * 1024),
        cost_estimate=COST,
        name="product",
    )(keep, window, rows)


def finish_kernel(*refs):
    count = len(CHUNKS)
    pieces, places = refs[: 3 * count], refs[3 * count : 4 * count]
    other_ref, occ_ref, pair_ref, out_ref = refs[4 * count :]
    residual = other_ref[...].astype(jnp.float32)
    for chunk, place in enumerate(places):
        own, up, down = (piece[...].astype(jnp.float32) for piece in pieces[3 * chunk : 3 * chunk + 3])
        share = own + up + down
        high = share.astype(jnp.bfloat16)
        low = (share - high.astype(jnp.float32)).astype(jnp.bfloat16)
        residual = residual + jnp.dot(high, place[...], preferred_element_type=jnp.float32)
        residual = residual + jnp.dot(low, place[...], preferred_element_type=jnp.float32)
    out_ref[...] = residual / (occ_ref[...] - pair_ref[...])


def finish(pieces, places, other_terms, occupied_sum, pair_energy):
    window, region = other_terms.shape
    spans = region // SPAN
    return pl.pallas_call(
        finish_kernel,
        grid=(spans,),
        in_specs=[pl.BlockSpec((window, p.shape[1] // spans), lambda t: (0, t)) for p in pieces]
        + [pl.BlockSpec(p.shape, lambda t: (0, 0)) for p in places]
        + [
            pl.BlockSpec((window, SPAN), lambda t: (0, t)),
            pl.BlockSpec((window, 1), lambda t: (0, 0)),
            pl.BlockSpec((1, SPAN), lambda t: (0, t)),
        ],
        out_specs=pl.BlockSpec((window, SPAN), lambda t: (0, t)),
        out_shape=jax.ShapeDtypeStruct((window, region), jnp.float32),
        compiler_params=pltpu.CompilerParams(vmem_limit_bytes=24 * 1024 * 1024),
        cost_estimate=COST,
        name="finish",
    )(*pieces, *places, other_terms, occupied_sum, pair_energy)


def shift(values, count, step):
    return lax.ppermute(values, "ka", [(i, (i + step) % count) for i in range(count)])


def shards(amplitudes, integrals, other_terms, tile_block, occ_pairs, occ_energy, pair_energy):
    wide_count = lax.axis_size("ta")
    wide_index = lax.axis_index("ta")
    narrow_count = lax.axis_size("ka")
    narrow_index = lax.axis_index("ka")
    region, stripe = integrals.shape
    slice_rows = region // wide_count
    region_tiles = region // TILE
    dealt = integrals.reshape(wide_count, slice_rows, stripe)

    stripes = []
    for step in range(narrow_count):
        column = lax.rem(narrow_index + narrow_count - step, narrow_count) * stripe
        part = lax.dynamic_slice(amplitudes, (0, column), (amplitudes.shape[0], stripe))
        stripes.append(shift(part, narrow_count, -step) if step else part)

    tiles = lax.dynamic_slice(tile_block, (wide_index * region_tiles,), (region_tiles,)).astype(jnp.float32)
    columns = (narrow_index * stripe + jnp.arange(stripe, dtype=jnp.int32)) // TILE
    column_blocks = block_of(tiles, columns)

    occ_count = occ_energy.shape[0]
    choosers = (
        occ_pairs.reshape(-1)[:, None] == jnp.arange(occ_count, dtype=jnp.int32)[None, :]
    ).astype(jnp.float32)
    energies = jnp.dot(choosers, occ_energy, precision=lax.Precision.HIGHEST).reshape(occ_pairs.shape[0], 2)
    occupied_sum = (energies[:, 0] + energies[:, 1])[:, None]

    starts = [sum(CHUNKS[:i]) for i in range(len(CHUNKS))]
    sends = [dealt[:, first : first + size] for first, size in zip(starts, CHUNKS)]
    later, _ = lax.optimization_barrier((sends[1:], stripes[1]))
    window, later = gather(stripes, later)
    sends = sends[:1] + later

    def exchange(index, size, after):
        sent = sends[index]
        if after:
            sent, *_ = lax.optimization_barrier((sent, *after))
        arrived = lax.all_to_all(sent, "ta", split_axis=0, concat_axis=0, tiled=True)
        return arrived.reshape(wide_count * size, stripe)

    def shared(arrived, first, size, step):
        per_slice = size // UNIT
        unit = jnp.arange(wide_count * per_slice, dtype=jnp.int32)
        row_tile = ((unit // per_slice) * slice_rows + first + (unit % per_slice) * UNIT) // TILE
        keep = (block_of(tiles, row_tile)[:, None] == column_blocks[None, :]).astype(jnp.float32)
        return product(window, arrived, keep, narrow_count, step)

    def reduced(shares):
        up, down = shares[far], shares[far + 1]
        for hop in range(1, far + 1):
            up = shift(up, narrow_count, 1)
            if hop < far:
                up = (up.astype(jnp.float32) + shares[far - hop].astype(jnp.float32)).astype(jnp.bfloat16)
        for hop in range(1, far):
            down = shift(down, narrow_count, -1)
            if hop < far - 1:
                down = (down.astype(jnp.float32) + shares[far + 1 + hop].astype(jnp.float32)).astype(jnp.bfloat16)
        return [shares[0], up, down]

    group = SPAN
    per_group = group // slice_rows
    far = narrow_count // 2
    places = []
    for first, size in zip(starts, CHUNKS):
        source = jnp.arange(per_group * size, dtype=jnp.int32)
        target = (source // size) * slice_rows + first + source % size
        places.append((target[:, None] == jnp.arange(group, dtype=jnp.int32)[None, :]).astype(jnp.bfloat16))

    arrived = []
    for index, size in enumerate(CHUNKS):
        arrived.append(exchange(index, size, arrived[-1:]))
    pieces = []
    for index, size in enumerate(CHUNKS):
        pieces += reduced(shared(arrived[index], starts[index], size, STEPS[index]))
    return finish(pieces, places, other_terms, occupied_sum, pair_energy[None, :])


def solution(mesh):
    return jax.shard_map(
        shards,
        mesh=mesh,
        in_specs=(P("ka", "ta"), P("ta", "ka"), P("ka", "ta"), P(), P("ka", None), P(), P("ta")),
        out_specs=P("ka", "ta"),
        check_vma=False,
    )
```

time: 201 us -> 167 us (0.83)
  waiting for transfers between devices: 139 us -> 68.8 us
  starting transfers between devices: 25 us -> 53.2 us
  between operations: 13.6 us -> 0.42 us
  local copies, waits for them, and re-layouts: 3.52 us -> 12.8 us
  other arithmetic: 2.77 us -> 8.69 us
  Pallas kernels: 13.3 us -> 19.2 us
    reduce_scatter x1 -> x0, waiting for transfers between devices: 66.1 us -> none  [shards(): lax.psum_scatter(shares, 'ka', scatter_dimension=0, tiled=True)]
    all_to_all x1 -> x2, waiting for transfers between devices: 64.4 us -> 27.2 us  [exchange(): lax.all_to_all(sent, 'ta', split_axis=0, concat_axis=0, tiled=True)]
    ppermute x7 -> x21, waiting for transfers between devices: 8.23 us -> 41.6 us  [shift(): lax.ppermute(values, 'ka', [(i, (i + step) % count) for i in range(count)])]
    ppermute x7 -> x21, starting transfers between devices: 17.2 us -> 41 us  [shift(): lax.ppermute(values, 'ka', [(i, (i + step) % count) for i in range(count)])]
    convert_element_type x1 -> x14, other arithmetic: 0.09 us -> 8.53 us  [the longest x6 4.56 us: reduced(): (up.astype(jnp.float32) + shares[far - hop].astype(jnp.float32)).astype(j...]
    slice x0 -> x2, local copies, waits for them, and re-layouts: none -> 7.82 us  [shards(): dealt[:, first:first + size]]
    pallas_call x2 -> x4, Pallas kernels: 13.3 us -> 19.2 us  [the longest x2 10.7 us: product(): pl.pallas_call(product_kernel, grid=(count // step,), in_specs=[pl.BlockS...]
    all_to_all x1 -> x2, starting transfers between devices: 7.72 us -> 12.2 us  [exchange(): lax.all_to_all(sent, 'ta', split_axis=0, concat_axis=0, tiled=True)]
  transfers between devices with their start and end apart: 9 -> 23, of which waited for: 5 -> 11; matrix products, arithmetic and copies ran while one was open for 2% -> 10% of each run, Pallas kernels for 1% -> 4%
where the time goes in v2:
time: 167 us; the launch traced here: 166 us
  waiting for transfers between devices  68.8 us (41%)
  starting transfers between devices  53.2 us (32%)
  Pallas kernels  19.2 us (11%)
  local copies, waits for them, and re-layouts  12.8 us (8%)
  other arithmetic  8.69 us (5%)
  matrix products  3.14 us (2%)
    ppermute x21, waiting for transfers between devices, shift(): lax.ppermute(values, 'ka', [(i, (i + step) % count) for i in range(count)])  41.6 us
    ppermute x21, starting transfers between devices, shift(): lax.ppermute(values, 'ka', [(i, (i + step) % count) for i in range(count)])  41 us
    all_to_all x2, waiting for transfers between devices, exchange(): lax.all_to_all(sent, 'ta', split_axis=0, concat_axis=0, tiled=True)  27.2 us
    all_to_all x2, starting transfers between devices, exchange(): lax.all_to_all(sent, 'ta', split_axis=0, concat_axis=0, tiled=True)  12.2 us
    pallas_call x2, Pallas kernels, product(): pl.pallas_call(product_kernel, grid=(count // step,), in_specs=[pl.BlockS...  10.7 us
    slice x2, local copies, waits for them, and re-layouts, shards(): dealt[:, first:first + size]  7.82 us
    pallas_call x1, Pallas kernels, finish(): pl.pallas_call(finish_kernel, grid=(spans,), in_specs=[pl.BlockSpec((wind...  6.5 us
    convert_element_type x6, other arithmetic, reduced(): (up.astype(jnp.float32) + shares[far - hop].astype(jnp.float32)).astype(j...  4.56 us
  transfers between devices with their start and end apart: 23, of which 11 were waited for; matrix products, arithmetic and copies ran while one was open for 10% of the time, Pallas kernels for 4%

profile of v2, /device:TPU:8, one launch (start us, length us, event | category | flops | bytes accessed | tf_op | source)
XLA Modules:
  0.0 166.3 jit_solution(16605371448240381804)
XLA Ops:
  0.0 4.9 %slice.17 = bf16[32,112,640]{2,1,0:T(8,128)(2,1)} slice(bf16[32,160,640]{2,1,0:T(8,128)(2,1)} %bitcast.20), slice={[0:32], [0:112], [0:640]} | slice | bytes 9175040 | tf_op jit(solution)/shard_map/slice | solution.py:145
  4.9 7.7 %all-to-all-start = ((bf16[32,112,640]{2,1,0:T(8,128)(2,1)}), bf16[32,112,640]{2,1,0:T(8,128)(2,1)}, u32[]{:S(2)}, u32[]{:S(2)}) async-start(bf16[32,112,640]{2,1,0:T(8,128)(2,1)} %slice.17), calls=%async_computation | async-start | bytes 9175040 | tf_op jit(solution)/shard_map/all_to_all | solution.py:154
  12.6 0.8 constant_dynamic-slice_fusion
  13.4 5.9 %collective-permute-start = (bf16[64,640]{1,0:T(8,128)(2,1)}, bf16[64,640]{1,0:T(8,128)(2,1)S(1)}, u32[]{:S(2)}, u32[]{:S(2)}) collective-permute-start(bf16[64,640]{1,0:T(8,128)(2,1)} %get-tuple-element.50), channel_id=1, source_target_pairs={{0,7},{1,0},{2,1},{3,2},{4,3},{5,4},{6,5},{7,6},{8,15},{9,8},{10,9... | collective-permute-start | bytes 245768 | tf_op jit(solution)/shard_map/ppermute | solution.py:114
  19.3 1.5 collective-permute-start.1
  20.8 0.4 collective-permute-start.2
  21.2 5.0 %collective-permute-start.3 = (bf16[64,640]{1,0:T(8,128)(2,1)}, bf16[64,640]{1,0:T(8,128)(2,1)}, u32[]{:S(2)}, u32[]{:S(2)}) collective-permute-start(bf16[64,640]{1,0:T(8,128)(2,1)} %get-tuple-element.47), channel_id=1, source_target_pairs={{0,4},{1,5},{2,6},{3,7},{4,0},{5,1},{6,2},{7,3},{8,12},{9,13},{10,... | collective-permute-start | bytes 245768 | tf_op jit(solution)/shard_map/ppermute | solution.py:114
  26.2 3.0 %slice.16.refs_8_ = bf16[32,48,640]{2,1,0:T(8,128)(2,1)} slice(bf16[32,160,640]{2,1,0:T(8,128)(2,1)} %bitcast.21), slice={[0:32], [112:160], [0:640]} | slice | bytes 3932160 | tf_op jit(solution)/shard_map/slice | solution.py:145
  29.5 0.9 convolution_bitcast_fusion.1
  30.4 1.1 convolution_reduce_fusion
  31.6 0.9 fusion.3
  32.8 0.4 fusion.refs_6_
  33.4 0.8 reshape.148
  34.3 2.5 %collective-permute-start.5 = (bf16[64,640]{1,0:T(8,128)(2,1)S(1)}, bf16[64,640]{1,0:T(8,128)(2,1)S(1)}, u32[]{:S(2)}, u32[]{:S(2)}) collective-permute-start(bf16[64,640]{1,0:T(8,128)(2,1)S(1)} %get-tuple-element.52), channel_id=1, source_target_pairs={{0,2},{1,3},{2,4},{3,5},{4,6},{5,7},{6,0},{7,1},{8,10},{9,11},{10,... | collective-permute-start | bytes 245768 | tf_op jit(solution)/shard_map/ppermute | solution.py:114
  36.7 1.9 %collective-permute-start.6 = (bf16[64,640]{1,0:T(8,128)(2,1)S(1)}, bf16[64,640]{1,0:T(8,128)(2,1)S(1)}, u32[]{:S(2)}, u32[]{:S(2)}) collective-permute-start(bf16[64,640]{1,0:T(8,128)(2,1)S(1)} %get-tuple-element.45), channel_id=1, source_target_pairs={{0,1},{1,2},{2,3},{3,4},{4,5},{5,6},{6,7},{7,0},{8,9},{9,10},{10,1... | collective-permute-start | bytes 245768 | tf_op jit(solution)/shard_map/ppermute | solution.py:114
  38.7 4.2 %collective-permute-done.5.refs_6_ = bf16[64,640]{1,0:T(8,128)(2,1)S(1)} collective-permute-done((bf16[64,640]{1,0:T(8,128)(2,1)S(1)}, bf16[64,640]{1,0:T(8,128)(2,1)S(1)}, u32[]{:S(2)}, u32[]{:S(2)}) %collective-permute-start.5) | collective-permute-done | bytes 81952 | tf_op jit(solution)/shard_map/ppermute | solution.py:114
  42.9 0.4 collective-permute-done.6.refs_7_
  43.5 0.7 copy-done.18
  44.1 2.1 %gather_window.1 = (bf16[512,640]{1,0:T(8,128)(2,1)}, bf16[32,48,640]{2,1,0:T(8,128)(2,1)}) custom-call(bf16[64,640]{1,0:T(8,128)(2,1)} %get-tuple-element.51.refs_0_, bf16[64,640]{1,0:T(8,128)(2,1)} %copy-done.15, bf16[64,640]{1,0:T(8,128)(2,1)} %copy-done.16, bf16[64,640]{1,0:T(8,128)(2,1)} %collective-permute-done.2.refs_3_, ...), custom_call_target="tpu_custom_call", output_to_operand_aliasing={{1}: (8, {})} | custom-call | tf_op jit(solution)/shard_map/gather_window/pallas_call | solution.py:31
  46.2 27.2 %all-to-all-done = bf16[32,112,640]{2,1,0:T(8,128)(2,1)} async-done(((bf16[32,112,640]{2,1,0:T(8,128)(2,1)}), bf16[32,112,640]{2,1,0:T(8,128)(2,1)}, u32[]{:S(2)}, u32[]{:S(2)}) %all-to-all-start) | async-done | bytes 4587552 | tf_op jit(solution)/shard_map/all_to_all | solution.py:154
  73.4 1.1 copy-done.1
  74.5 6.9 %product.2 = (bf16[64,3584]{1,0:T(8,128)(2,1)}, bf16[64,3584]{1,0:T(8,128)(2,1)}, bf16[64,3584]{1,0:T(8,128)(2,1)}, bf16[64,3584]{1,0:T(8,128)(2,1)}, bf16[64,35...) custom-call(f32[224,640]{1,0:T(8,128)S(1)} %compare_convert_fusion.keep_ref, ...), custom_call_target="tpu_custom_call" | custom-call | flops 1000 | bytes 1000 | tf_op jit(solution)/shard_map/product/pallas_call | solution.py:60
  81.4 2.0 %collective-permute-start.7 = (bf16[64,3584]{1,0:T(8,128)(2,1)}, bf16[64,3584]{1,0:T(8,128)(2,1)}, u32[]{:S(2)}, u32[]{:S(2)}) collective-permute-start(bf16[64,3584]{1,0:T(8,128)(2,1)} %get-tuple-element.28), channel_id=1, source_target_pairs={{0,1},{1,2},{2,3},{3,4},{4,5},{5,6},{6,7},{7,0},{8,9},{9,10},{10,1... | collective-permute-start | bytes 1376264 | tf_op jit(solution)/shard_map/ppermute | solution.py:114
  83.5 4.5 %all-to-all-start.1 = ((bf16[32,48,640]{2,1,0:T(8,128)(2,1)}), bf16[32,48,640]{2,1,0:T(8,128)(2,1)}, u32[]{:S(2)}, u32[]{:S(2)}) async-start(bf16[32,48,640]{2,1,0:T(8,128)(2,1)} %get-tuple-element.36), calls=%async_computation.1 | async-start | bytes 3932160 | tf_op jit(solution)/shard_map/all_to_all | solution.py:154
  88.1 4.0 %collective-permute-start.11 = (bf16[64,3584]{1,0:T(8,128)(2,1)}, bf16[64,3584]{1,0:T(8,128)(2,1)S(1)}, u32[]{:S(2)}, u32[]{:S(2)}) collective-permute-start(bf16[64,3584]{1,0:T(8,128)(2,1)} %get-tuple-element.32), channel_id=1, source_target_pairs={{0,7},{1,0},{2,1},{3,2},{4,3},{5,4},{6,5},{7,6},{8,15},{9,8},{10,9... | collective-permute-start | bytes 1376264 | tf_op jit(solution)/shard_map/ppermute | solution.py:114
  92.1 5.7 %collective-permute-done.7 = bf16[64,3584]{1,0:T(8,128)(2,1)} collective-permute-done((bf16[64,3584]{1,0:T(8,128)(2,1)}, bf16[64,3584]{1,0:T(8,128)(2,1)}, u32[]{:S(2)}, u32[]{:S(2)}) %collective-permute-start.7) | collective-permute-done | bytes 458784 | tf_op jit(solution)/shard_map/ppermute | solution.py:114
  97.9 1.3 add_convert_fusion.4
  99.2 2.8 %collective-permute-done.11 = bf16[64,3584]{1,0:T(8,128)(2,1)S(1)} collective-permute-done((bf16[64,3584]{1,0:T(8,128)(2,1)}, bf16[64,3584]{1,0:T(8,128)(2,1)S(1)}, u32[]{:S(2)}, u32[]{:S(2)}) %collective-permute-start.11) | collective-permute-done | bytes 458784 | tf_op jit(solution)/shard_map/ppermute | solution.py:114
  102.0 1.1 add_convert_fusion.1
  103.2 3.8 %collective-permute-start.12 = (bf16[64,3584]{1,0:T(8,128)(2,1)S(1)}, bf16[64,3584]{1,0:T(8,128)(2,1)S(1)}, u32[]{:S(2)}, u32[]{:S(2)}) collective-permute-start(bf16[64,3584]{1,0:T(8,128)(2,1)S(1)} %add_convert_fusion.1), channel_id=1, source_target_pairs={{0,7},{1,0},{2,1},{3,2},{4,3},{5,4},{6,5},{7,6},{8,15},{9,8},{10,9... | collective-permute-start | bytes 1376264 | tf_op jit(solution)/shard_map/ppermute | solution.py:114
  107.0 4.9 %collective-permute-done.8 = bf16[64,3584]{1,0:T(8,128)(2,1)S(1)} collective-permute-done((bf16[64,3584]{1,0:T(8,128)(2,1)S(1)}, bf16[64,3584]{1,0:T(8,128)(2,1)S(1)}, u32[]{:S(2)}, u32[]{:S(2)}) %collective-permute-start.8) | collective-permute-done | bytes 458784 | tf_op jit(solution)/shard_map/ppermute | solution.py:114
  111.9 0.9 add_convert_fusion.3
  112.8 3.0 %collective-permute-done.12 = bf16[64,3584]{1,0:T(8,128)(2,1)S(1)} collective-permute-done((bf16[64,3584]{1,0:T(8,128)(2,1)S(1)}, bf16[64,3584]{1,0:T(8,128)(2,1)S(1)}, u32[]{:S(2)}, u32[]{:S(2)}) %collective-permute-start.12) | collective-permute-done | bytes 458784 | tf_op jit(solution)/shard_map/ppermute | solution.py:114
  115.8 0.9 add_convert_fusion
  116.7 3.7 %collective-permute-start.13 = (bf16[64,3584]{1,0:T(8,128)(2,1)}, bf16[64,3584]{1,0:T(8,128)(2,1)}, u32[]{:S(2)}, u32[]{:S(2)}) collective-permute-start(bf16[64,3584]{1,0:T(8,128)(2,1)} %add_convert_fusion), channel_id=1, source_target_pairs={{0,7},{1,0},{2,1},{3,2},{4,3},{5,4},{6,5},{7,6},{8,15},{9,8},{10,9... | collective-permute-start | bytes 1376264 | tf_op jit(solution)/shard_map/ppermute | solution.py:114
  120.4 1.1 copy-done.2
  121.5 3.8 %product.3 = (bf16[64,1536]{1,0:T(8,128)(2,1)}, bf16[64,1536]{1,0:T(8,128)(2,1)}, bf16[64,1536]{1,0:T(8,128)(2,1)}, bf16[64,1536]{1,0:T(8,128)(2,1)}, bf16[64,15...) custom-call(f32[96,640]{1,0:T(8,128)S(1)} %compare_convert_fusion.1.keep_ref, ...), custom_call_target="tpu_custom_call" | custom-call | flops 1000 | bytes 1000 | tf_op jit(solution)/shard_map/product/pallas_call | solution.py:60
  125.5 1.3 add_convert_fusion.2
  126.9 3.2 %collective-permute-start.18 = (bf16[64,1536]{1,0:T(8,128)(2,1)}, bf16[64,1536]{1,0:T(8,128)(2,1)S(1)}, u32[]{:S(2)}, u32[]{:S(2)}) collective-permute-start(bf16[64,1536]{1,0:T(8,128)(2,1)} %get-tuple-element.42), channel_id=1, source_target_pairs={{0,7},{1,0},{2,1},{3,2},{4,3},{5,4},{6,5},{7,6},{8,15},{9,8},{10,9... | collective-permute-start | bytes 589832 | tf_op jit(solution)/shard_map/ppermute | solution.py:114
  130.1 4.6 %collective-permute-done.14 = bf16[64,1536]{1,0:T(8,128)(2,1)S(1)} collective-permute-done((bf16[64,1536]{1,0:T(8,128)(2,1)}, bf16[64,1536]{1,0:T(8,128)(2,1)S(1)}, u32[]{:S(2)}, u32[]{:S(2)}) %collective-permute-start.14) | collective-permute-done | bytes 196640 | tf_op jit(solution)/shard_map/ppermute | solution.py:114
  134.7 1.0 add_convert_fusion.9
  135.8 1.0 add_convert_fusion.6
  136.8 3.3 %collective-permute-start.19 = (bf16[64,1536]{1,0:T(8,128)(2,1)S(1)}, bf16[64,1536]{1,0:T(8,128)(2,1)S(1)}, u32[]{:S(2)}, u32[]{:S(2)}) collective-permute-start(bf16[64,1536]{1,0:T(8,128)(2,1)S(1)} %add_convert_fusion.6), channel_id=1, source_target_pairs={{0,7},{1,0},{2,1},{3,2},{4,3},{5,4},{6,5},{7,6},{8,15},{9,8},{10,9... | collective-permute-start | bytes 589832 | tf_op jit(solution)/shard_map/ppermute | solution.py:114
  140.1 5.3 %collective-permute-done.15 = bf16[64,1536]{1,0:T(8,128)(2,1)S(1)} collective-permute-done((bf16[64,1536]{1,0:T(8,128)(2,1)S(1)}, bf16[64,1536]{1,0:T(8,128)(2,1)S(1)}, u32[]{:S(2)}, u32[]{:S(2)}) %collective-permute-start.15) | collective-permute-done | bytes 196640 | tf_op jit(solution)/shard_map/ppermute | solution.py:114
  145.6 3.3 %collective-permute-start.20 = (bf16[64,1536]{1,0:T(8,128)(2,1)S(1)}, bf16[64,1536]{1,0:T(8,128)(2,1)S(1)}, u32[]{:S(2)}, u32[]{:S(2)}) collective-permute-start(bf16[64,1536]{1,0:T(8,128)(2,1)S(1)} %add_convert_fusion.5), channel_id=1, source_target_pairs={{0,7},{1,0},{2,1},{3,2},{4,3},{5,4},{6,5},{7,6},{8,15},{9,8},{10,9... | collective-permute-start | bytes 589832 | tf_op jit(solution)/shard_map/ppermute | solution.py:114
  148.9 3.9 %collective-permute-done.16 = bf16[64,1536]{1,0:T(8,128)(2,1)S(1)} collective-permute-done((bf16[64,1536]{1,0:T(8,128)(2,1)S(1)}, bf16[64,1536]{1,0:T(8,128)(2,1)S(1)}, u32[]{:S(2)}, u32[]{:S(2)}) %collective-permute-start.16) | collective-permute-done | bytes 196640 | tf_op jit(solution)/shard_map/ppermute | solution.py:114
  153.0 6.8 %collective-permute-done.17.refs_4_ = bf16[64,1536]{1,0:T(8,128)(2,1)S(1)} collective-permute-done((bf16[64,1536]{1,0:T(8,128)(2,1)S(1)}, bf16[64,1536]{1,0:T(8,128)(2,1)S(1)}, u32[]{:S(2)}, u32[]{:S(2)}) %collective-permute-start.17) | collective-permute-done | bytes 196640 | tf_op jit(solution)/shard_map/ppermute | solution.py:114
  159.8 6.5 %finish.1 = f32[64,5120]{1,0:T(8,128)} custom-call(bf16[64,3584]{1,0:T(8,128)(2,1)S(1)} %copy-done.4, bf16[64,3584]{1,0:T(8,128)(2,1)S(1)} %collective-permute-done.10.refs_1_, bf16[64,3584]{1,0:T(8,128)(2,1)} %collective-permute-done.13.refs_2_, bf16[64,1536]{1,0:T(8,128)(2,1)S(1)} %copy-done.5, bf16[64,1536]{1,0:T(8,128)(2,1)S(1)} %collective-permute-done.17.refs_4_, ...), custom_call_target="tpu_custom_call" | custom-call | flops 1000 | bytes 1000 | tf_op jit(solution)/shard_map/finish/pallas_call | solution.py:95
  (72 shorter events, 2.1 us)
Async XLA Ops:
  0.0 33.2 %copy-start = (f32[150]{0:T(256)S(1)}, f32[150]{0:T(256)}, u32[]{:S(2)}) copy-start(f32[150]{0:T(256)} %param.12) | copy-start | bytes 1804
  4.9 7.8 %copy-start.7 = (bf16[64,5120]{1,0:T(8,128)(2,1)S(1)}, bf16[64,5120]{1,0:T(8,128)(2,1)}, u32[]{:S(2)}) copy-start(bf16[64,5120]{1,0:T(8,128)(2,1)} %param.7) | copy-start | bytes 1966084
  4.9 68.5 %all-to-all-start = ((bf16[32,112,640]{2,1,0:T(8,128)(2,1)}), bf16[32,112,640]{2,1,0:T(8,128)(2,1)}, u32[]{:S(2)}, u32[]{:S(2)}) async-start(bf16[32,112,640]{2,1,0:T(8,128)(2,1)} %slice.17), calls=%async_computation | async-start | bytes 9175040 | tf_op jit(solution)/shard_map/all_to_all | solution.py:154
  13.4 15.8 %copy-start.19 = (s32[64,2]{0,1:T(2,128)S(1)}, s32[64,2]{0,1:T(2,128)}, u32[]{:S(2)}) copy-start(s32[64,2]{0,1:T(2,128)} %param.11) | copy-start | bytes 1540
  13.4 20.8 %collective-permute-start = (bf16[64,640]{1,0:T(8,128)(2,1)}, bf16[64,640]{1,0:T(8,128)(2,1)S(1)}, u32[]{:S(2)}, u32[]{:S(2)}) collective-permute-start(bf16[64,640]{1,0:T(8,128)(2,1)} %get-tuple-element.50), channel_id=1, source_target_pairs={{0,7},{1,0},{2,1},{3,2},{4,3},{5,4},{6,5},{7,6},{8,15},{9,8},{10,9... | collective-permute-start | bytes 245768 | tf_op jit(solution)/shard_map/ppermute | solution.py:114
  19.3 17.4 %collective-permute-start.1 = (bf16[64,640]{1,0:T(8,128)(2,1)}, bf16[64,640]{1,0:T(8,128)(2,1)S(1)}, u32[]{:S(2)}, u32[]{:S(2)}) collective-permute-start(bf16[64,640]{1,0:T(8,128)(2,1)} %get-tuple-element.49), channel_id=1, source_target_pairs={{0,6},{1,7},{2,0},{3,1},{4,2},{5,3},{6,4},{7,5},{8,14},{9,15},{10,... | collective-permute-start | bytes 245768 | tf_op jit(solution)/shard_map/ppermute | solution.py:114
  20.8 17.9 %collective-permute-start.2 = (bf16[64,640]{1,0:T(8,128)(2,1)}, bf16[64,640]{1,0:T(8,128)(2,1)}, u32[]{:S(2)}, u32[]{:S(2)}) collective-permute-start(bf16[64,640]{1,0:T(8,128)(2,1)} %get-tuple-element.48), channel_id=1, source_target_pairs={{0,5},{1,6},{2,7},{3,0},{4,1},{5,2},{6,3},{7,4},{8,13},{9,14},{10,... | collective-permute-start | bytes 245768 | tf_op jit(solution)/shard_map/ppermute | solution.py:114
  21.2 17.5 %collective-permute-start.3 = (bf16[64,640]{1,0:T(8,128)(2,1)}, bf16[64,640]{1,0:T(8,128)(2,1)}, u32[]{:S(2)}, u32[]{:S(2)}) collective-permute-start(bf16[64,640]{1,0:T(8,128)(2,1)} %get-tuple-element.47), channel_id=1, source_target_pairs={{0,4},{1,5},{2,6},{3,7},{4,0},{5,1},{6,2},{7,3},{8,12},{9,13},{10,... | collective-permute-start | bytes 245768 | tf_op jit(solution)/shard_map/ppermute | solution.py:114
  26.2 12.4 %collective-permute-start.4 = (bf16[64,640]{1,0:T(8,128)(2,1)S(1)}, bf16[64,640]{1,0:T(8,128)(2,1)}, u32[]{:S(2)}, u32[]{:S(2)}) collective-permute-start(bf16[64,640]{1,0:T(8,128)(2,1)S(1)} %get-tuple-element.46), channel_id=1, source_target_pairs={{0,3},{1,4},{2,5},{3,6},{4,7},{5,0},{6,1},{7,2},{8,11},{9,12},{10,... | collective-permute-start | bytes 245768 | tf_op jit(solution)/shard_map/ppermute | solution.py:114
  34.3 9.9 %copy-start.15 = (bf16[64,640]{1,0:T(8,128)(2,1)}, bf16[64,640]{1,0:T(8,128)(2,1)S(1)}, u32[]{:S(2)}) copy-start(bf16[64,640]{1,0:T(8,128)(2,1)S(1)} %collective-permute-done.refs_1_) | copy-start | bytes 245764
  34.3 8.6 %collective-permute-start.5 = (bf16[64,640]{1,0:T(8,128)(2,1)S(1)}, bf16[64,640]{1,0:T(8,128)(2,1)S(1)}, u32[]{:S(2)}, u32[]{:S(2)}) collective-permute-start(bf16[64,640]{1,0:T(8,128)(2,1)S(1)} %get-tuple-element.52), channel_id=1, source_target_pairs={{0,2},{1,3},{2,4},{3,5},{4,6},{5,7},{6,0},{7,1},{8,10},{9,11},{10,... | collective-permute-start | bytes 245768 | tf_op jit(solution)/shard_map/ppermute | solution.py:114
  36.7 7.4 %copy-start.16 = (bf16[64,640]{1,0:T(8,128)(2,1)}, bf16[64,640]{1,0:T(8,128)(2,1)S(1)}, u32[]{:S(2)}) copy-start(bf16[64,640]{1,0:T(8,128)(2,1)S(1)} %collective-permute-done.1.refs_2_) | copy-start | bytes 245764
  36.7 6.5 %collective-permute-start.6 = (bf16[64,640]{1,0:T(8,128)(2,1)S(1)}, bf16[64,640]{1,0:T(8,128)(2,1)S(1)}, u32[]{:S(2)}, u32[]{:S(2)}) collective-permute-start(bf16[64,640]{1,0:T(8,128)(2,1)S(1)} %get-tuple-element.45), channel_id=1, source_target_pairs={{0,1},{1,2},{2,3},{3,4},{4,5},{5,6},{6,7},{7,0},{8,9},{9,10},{10,1... | collective-permute-start | bytes 245768 | tf_op jit(solution)/shard_map/ppermute | solution.py:114
  42.9 0.6 copy-start.17
  43.5 0.7 copy-start.18
  73.4 1.1 copy-start.1
  81.4 16.5 %collective-permute-start.7 = (bf16[64,3584]{1,0:T(8,128)(2,1)}, bf16[64,3584]{1,0:T(8,128)(2,1)}, u32[]{:S(2)}, u32[]{:S(2)}) collective-permute-start(bf16[64,3584]{1,0:T(8,128)(2,1)} %get-tuple-element.28), channel_id=1, source_target_pairs={{0,1},{1,2},{2,3},{3,4},{4,5},{5,6},{6,7},{7,0},{8,9},{9,10},{10,1... | collective-permute-start | bytes 1376264 | tf_op jit(solution)/shard_map/ppermute | solution.py:114
  83.5 36.9 %all-to-all-start.1 = ((bf16[32,48,640]{2,1,0:T(8,128)(2,1)}), bf16[32,48,640]{2,1,0:T(8,128)(2,1)}, u32[]{:S(2)}, u32[]{:S(2)}) async-start(bf16[32,48,640]{2,1,0:T(8,128)(2,1)} %get-tuple-element.36), calls=%async_computation.1 | async-start | bytes 3932160 | tf_op jit(solution)/shard_map/all_to_all | solution.py:154
  88.1 23.8 %copy-start.10 = (bf16[64,3584]{1,0:T(8,128)(2,1)S(1)}, bf16[64,3584]{1,0:T(8,128)(2,1)}, u32[]{:S(2)}) copy-start(bf16[64,3584]{1,0:T(8,128)(2,1)} %get-tuple-element.30) | copy-start | bytes 1376260
  88.1 27.7 %copy-start.9 = (bf16[64,3584]{1,0:T(8,128)(2,1)S(1)}, bf16[64,3584]{1,0:T(8,128)(2,1)}, u32[]{:S(2)}) copy-start(bf16[64,3584]{1,0:T(8,128)(2,1)} %get-tuple-element.34) | copy-start | bytes 1376260
  88.1 13.9 %collective-permute-start.11 = (bf16[64,3584]{1,0:T(8,128)(2,1)}, bf16[64,3584]{1,0:T(8,128)(2,1)S(1)}, u32[]{:S(2)}, u32[]{:S(2)}) collective-permute-start(bf16[64,3584]{1,0:T(8,128)(2,1)} %get-tuple-element.32), channel_id=1, source_target_pairs={{0,7},{1,0},{2,1},{3,2},{4,3},{5,4},{6,5},{7,6},{8,15},{9,8},{10,9... | collective-permute-start | bytes 1376264 | tf_op jit(solution)/shard_map/ppermute | solution.py:114
  99.2 12.8 %collective-permute-start.8 = (bf16[64,3584]{1,0:T(8,128)(2,1)S(1)}, bf16[64,3584]{1,0:T(8,128)(2,1)S(1)}, u32[]{:S(2)}, u32[]{:S(2)}) collective-permute-start(bf16[64,3584]{1,0:T(8,128)(2,1)S(1)} %add_convert_fusion.4), channel_id=1, source_target_pairs={{0,1},{1,2},{2,3},{3,4},{4,5},{5,6},{6,7},{7,0},{8,9},{9,10},{10,1... | collective-permute-start | bytes 1376264 | tf_op jit(solution)/shard_map/ppermute | solution.py:114
  103.2 12.6 %collective-permute-start.12 = (bf16[64,3584]{1,0:T(8,128)(2,1)S(1)}, bf16[64,3584]{1,0:T(8,128)(2,1)S(1)}, u32[]{:S(2)}, u32[]{:S(2)}) collective-permute-start(bf16[64,3584]{1,0:T(8,128)(2,1)S(1)} %add_convert_fusion.1), channel_id=1, source_target_pairs={{0,7},{1,0},{2,1},{3,2},{4,3},{5,4},{6,5},{7,6},{8,15},{9,8},{10,9... | collective-permute-start | bytes 1376264 | tf_op jit(solution)/shard_map/ppermute | solution.py:114
  112.8 12.6 %collective-permute-start.9 = (bf16[64,3584]{1,0:T(8,128)(2,1)}, bf16[64,3584]{1,0:T(8,128)(2,1)}, u32[]{:S(2)}, u32[]{:S(2)}) collective-permute-start(bf16[64,3584]{1,0:T(8,128)(2,1)} %add_convert_fusion.3), channel_id=1, source_target_pairs={{0,1},{1,2},{2,3},{3,4},{4,5},{5,6},{6,7},{7,0},{8,9},{9,10},{10,1... | collective-permute-start | bytes 1376264 | tf_op jit(solution)/shard_map/ppermute | solution.py:114
  116.7 36.3 %collective-permute-start.13 = (bf16[64,3584]{1,0:T(8,128)(2,1)}, bf16[64,3584]{1,0:T(8,128)(2,1)}, u32[]{:S(2)}, u32[]{:S(2)}) collective-permute-start(bf16[64,3584]{1,0:T(8,128)(2,1)} %add_convert_fusion), channel_id=1, source_target_pairs={{0,7},{1,0},{2,1},{3,2},{4,3},{5,4},{6,5},{7,6},{8,15},{9,8},{10,9... | collective-permute-start | bytes 1376264 | tf_op jit(solution)/shard_map/ppermute | solution.py:114
  120.4 1.1 copy-start.2
  121.5 4.0 %copy-start.8 = (bf16[64,3584]{1,0:T(8,128)(2,1)S(1)}, bf16[64,3584]{1,0:T(8,128)(2,1)}, u32[]{:S(2)}) copy-start(bf16[64,3584]{1,0:T(8,128)(2,1)} %get-tuple-element.31) | copy-start | bytes 1376260
  125.3 20.1 %copy-start.14 = (bf16[64,1536]{1,0:T(8,128)(2,1)S(1)}, bf16[64,1536]{1,0:T(8,128)(2,1)}, u32[]{:S(2)}) copy-start(bf16[64,1536]{1,0:T(8,128)(2,1)} %get-tuple-element.40) | copy-start | bytes 589828
  125.3 20.2 %copy-start.13 = (bf16[64,1536]{1,0:T(8,128)(2,1)S(1)}, bf16[64,1536]{1,0:T(8,128)(2,1)}, u32[]{:S(2)}) copy-start(bf16[64,1536]{1,0:T(8,128)(2,1)} %get-tuple-element.44) | copy-start | bytes 589828
  125.3 27.5 %copy-start.12 = (bf16[64,1536]{1,0:T(8,128)(2,1)S(1)}, bf16[64,1536]{1,0:T(8,128)(2,1)}, u32[]{:S(2)}) copy-start(bf16[64,1536]{1,0:T(8,128)(2,1)} %get-tuple-element.41) | copy-start | bytes 589828
  125.3 27.6 %copy-start.11 = (f32[64,2]{1,0:T(8,128)S(1)}, f32[64,2]{1,0:T(8,128)}, u32[]{:S(2)}) copy-start(f32[64,2]{1,0:T(8,128)} %reshape.148) | copy-start | bytes 1540
  125.3 34.5 %copy-start.3 = (bf16[64,5120]{1,0:T(8,128)(2,1)S(1)}, bf16[64,5120]{1,0:T(8,128)(2,1)}, u32[]{:S(2)}) copy-start(bf16[64,5120]{1,0:T(8,128)(2,1)} %refs_8_.1) | copy-start | bytes 1966084
  125.3 34.5 %copy-start.4 = (bf16[64,3584]{1,0:T(8,128)(2,1)S(1)}, bf16[64,3584]{1,0:T(8,128)(2,1)}, u32[]{:S(2)}) copy-start(bf16[64,3584]{1,0:T(8,128)(2,1)} %get-tuple-element.27.refs_0_) | copy-start | bytes 1376260
  125.3 34.5 %copy-start.5 = (bf16[64,1536]{1,0:T(8,128)(2,1)S(1)}, bf16[64,1536]{1,0:T(8,128)(2,1)}, u32[]{:S(2)}) copy-start(bf16[64,1536]{1,0:T(8,128)(2,1)} %get-tuple-element.37.refs_3_) | copy-start | bytes 589828
  125.3 34.5 %copy-start.6 = (f32[5120]{0:T(1024)S(1)}, f32[5120]{0:T(1024)}, u32[]{:S(2)}) copy-start(f32[5120]{0:T(1024)} %param.13) | copy-start | bytes 61444
  125.4 9.3 %collective-permute-start.14 = (bf16[64,1536]{1,0:T(8,128)(2,1)}, bf16[64,1536]{1,0:T(8,128)(2,1)S(1)}, u32[]{:S(2)}, u32[]{:S(2)}) collective-permute-start(bf16[64,1536]{1,0:T(8,128)(2,1)} %get-tuple-element.38), channel_id=1, source_target_pairs={{0,1},{1,2},{2,3},{3,4},{4,5},{5,6},{6,7},{7,0},{8,9},{9,10},{10,1... | collective-permute-start | bytes 589832 | tf_op jit(solution)/shard_map/ppermute | solution.py:114
  126.8 26.2 %collective-permute-start.10 = (bf16[64,3584]{1,0:T(8,128)(2,1)S(1)}, bf16[64,3584]{1,0:T(8,128)(2,1)S(1)}, u32[]{:S(2)}, u32[]{:S(2)}) collective-permute-start(bf16[64,3584]{1,0:T(8,128)(2,1)S(1)} %add_convert_fusion.2), channel_id=1, source_target_pairs={{0,1},{1,2},{2,3},{3,4},{4,5},{5,6},{6,7},{7,0},{8,9},{9,10},{10,1... | collective-permute-start | bytes 1376264 | tf_op jit(solution)/shard_map/ppermute | solution.py:114
  126.9 8.9 %collective-permute-start.18 = (bf16[64,1536]{1,0:T(8,128)(2,1)}, bf16[64,1536]{1,0:T(8,128)(2,1)S(1)}, u32[]{:S(2)}, u32[]{:S(2)}) collective-permute-start(bf16[64,1536]{1,0:T(8,128)(2,1)} %get-tuple-element.42), channel_id=1, source_target_pairs={{0,7},{1,0},{2,1},{3,2},{4,3},{5,4},{6,5},{7,6},{8,15},{9,8},{10,9... | collective-permute-start | bytes 589832 | tf_op jit(solution)/shard_map/ppermute | solution.py:114
  135.7 9.7 %collective-permute-start.15 = (bf16[64,1536]{1,0:T(8,128)(2,1)S(1)}, bf16[64,1536]{1,0:T(8,128)(2,1)S(1)}, u32[]{:S(2)}, u32[]{:S(2)}) collective-permute-start(bf16[64,1536]{1,0:T(8,128)(2,1)S(1)} %add_convert_fusion.9), channel_id=1, source_target_pairs={{0,1},{1,2},{2,3},{3,4},{4,5},{5,6},{6,7},{7,0},{8,9},{9,10},{10,1... | collective-permute-start | bytes 589832 | tf_op jit(solution)/shard_map/ppermute | solution.py:114
  136.8 8.7 %collective-permute-start.19 = (bf16[64,1536]{1,0:T(8,128)(2,1)S(1)}, bf16[64,1536]{1,0:T(8,128)(2,1)S(1)}, u32[]{:S(2)}, u32[]{:S(2)}) collective-permute-start(bf16[64,1536]{1,0:T(8,128)(2,1)S(1)} %add_convert_fusion.6), channel_id=1, source_target_pairs={{0,7},{1,0},{2,1},{3,2},{4,3},{5,4},{6,5},{7,6},{8,15},{9,8},{10,9... | collective-permute-start | bytes 589832 | tf_op jit(solution)/shard_map/ppermute | solution.py:114
  145.4 7.4 %collective-permute-start.16 = (bf16[64,1536]{1,0:T(8,128)(2,1)S(1)}, bf16[64,1536]{1,0:T(8,128)(2,1)S(1)}, u32[]{:S(2)}, u32[]{:S(2)}) collective-permute-start(bf16[64,1536]{1,0:T(8,128)(2,1)S(1)} %add_convert_fusion.8), channel_id=1, source_target_pairs={{0,1},{1,2},{2,3},{3,4},{4,5},{5,6},{6,7},{7,0},{8,9},{9,10},{10,1... | collective-permute-start | bytes 589832 | tf_op jit(solution)/shard_map/ppermute | solution.py:114
  145.6 7.5 %collective-permute-start.20 = (bf16[64,1536]{1,0:T(8,128)(2,1)S(1)}, bf16[64,1536]{1,0:T(8,128)(2,1)S(1)}, u32[]{:S(2)}, u32[]{:S(2)}) collective-permute-start(bf16[64,1536]{1,0:T(8,128)(2,1)S(1)} %add_convert_fusion.5), channel_id=1, source_target_pairs={{0,7},{1,0},{2,1},{3,2},{4,3},{5,4},{6,5},{7,6},{8,15},{9,8},{10,9... | collective-permute-start | bytes 589832 | tf_op jit(solution)/shard_map/ppermute | solution.py:114
  152.8 7.0 %collective-permute-start.17 = (bf16[64,1536]{1,0:T(8,128)(2,1)S(1)}, bf16[64,1536]{1,0:T(8,128)(2,1)S(1)}, u32[]{:S(2)}, u32[]{:S(2)}) collective-permute-start(bf16[64,1536]{1,0:T(8,128)(2,1)S(1)} %add_convert_fusion.7), channel_id=1, source_target_pairs={{0,1},{1,2},{2,3},{3,4},{4,5},{5,6},{6,7},{7,0},{8,9},{9,10},{10,1... | collective-permute-start | bytes 589832 | tf_op jit(solution)/shard_map/ppermute | solution.py:114

commit v3 on v2

v3 whole, which is shorter than its diff:
```python
import functools

import jax
import jax.numpy as jnp
from jax import lax
from jax.experimental import pallas as pl
from jax.experimental.pallas import tpu as pltpu
from jax.sharding import PartitionSpec as P

TILE = 128
UNIT = 16
COST = pl.CostEstimate(flops=1000, bytes_accessed=1000, transcendentals=0)
CHUNKS = (112, 48)
STEPS = (1792, 768)
SPAN = 1280


def block_of(tiles, index):
    picker = (index[:, None] == jnp.arange(tiles.shape[0], dtype=jnp.int32)[None, :]).astype(jnp.float32)
    return jnp.dot(picker, tiles, precision=lax.Precision.HIGHEST)


def gather(stripes, held):
    count = len(stripes)
    rows, width = stripes[0].shape

    def kernel(*refs):
        window_ref = refs[count + len(held)]
        for slot, stripe in enumerate(refs[:count]):
            window_ref[slot * rows : (slot + 1) * rows, :] = stripe[...]

    vmem, anywhere = pl.BlockSpec(memory_space=pltpu.VMEM), pl.BlockSpec(memory_space=pl.ANY)
    window, *held = pl.pallas_call(
        kernel,
        in_specs=[vmem] * count + [anywhere] * len(held),
        out_specs=[vmem] + [anywhere] * len(held),
        out_shape=[pltpu.VMEM((rows * count, width), stripes[0].dtype)]
        + [pltpu.HBM(h.shape, h.dtype) for h in held],
        input_output_aliases={count + n: 1 + n for n in range(len(held))},
        name="gather_window",
    )(*stripes, *held)
    return window, held


def product_kernel(rings, keep_ref, window_ref, rows_ref, *refs):
    outs, masked_ref = refs[:-1], refs[-1]
    slots = len(outs) // rings
    window = outs[0].shape[0]
    for unit in range(masked_ref.shape[0] // UNIT):
        rows = pl.ds(unit * UNIT, UNIT)
        keep = keep_ref[unit : unit + 1, :].astype(jnp.bfloat16)
        masked_ref[rows, :] = rows_ref[rows, :] * keep
    shares = lax.dot_general(
        window_ref[...], masked_ref[...], (((1,), (1,)), ((), ())), preferred_element_type=jnp.float32
    ).astype(jnp.bfloat16)
    for ring in range(rings):

        @pl.when(pl.program_id(0) // (pl.num_programs(0) // rings) == ring)
        def _():
            for slot in range(slots):
                outs[ring * slots + slot][...] = shares[slot * window : (slot + 1) * window]


def ring_block(rows, width, ring, share):
    return pl.BlockSpec((rows, width), lambda t: (0, jnp.clip(t - ring * share, 0, share - 1)))


def product(window, rows, keep, slots, step, rings, space):
    occ, stripe = window.shape
    count = rows.shape[0]
    return pl.pallas_call(
        functools.partial(product_kernel, rings),
        grid=(count // step,),
        in_specs=[
            pl.BlockSpec((step // UNIT, stripe), lambda t: (t, 0)),
            pl.BlockSpec((occ, stripe), lambda t: (0, 0)),
            pl.BlockSpec((step, stripe), lambda t: (t, 0)),
        ],
        out_specs=[ring_block(occ // slots, step, n // slots, count // step // rings) for n in range(slots * rings)],
        out_shape=[space((occ // slots, count // rings), jnp.bfloat16)] * (slots * rings),
        scratch_shapes=[pltpu.VMEM((step, stripe), jnp.bfloat16)],
        compiler_params=pltpu.CompilerParams(vmem_limit_bytes=24 * 1024 * 1024),
        cost_estimate=COST,
        name="product",
    )(keep, window, rows)


def placed(pieces, place):
    own, up, down = (piece[...].astype(jnp.float32) for piece in pieces)
    share = own + up + down
    high = share.astype(jnp.bfloat16)
    low = (share - high.astype(jnp.float32)).astype(jnp.bfloat16)
    moved = jnp.dot(high, place[...], preferred_element_type=jnp.float32)
    return moved + jnp.dot(low, place[...], preferred_element_type=jnp.float32)


def begin_kernel(own, up, down, place, other_ref, out_ref):
    out_ref[...] = other_ref[...].astype(jnp.float32) + placed((own, up, down), place)


def begin(pieces, place, other_terms, ring, rings):
    window, region = other_terms.shape
    share = region // SPAN // rings
    return pl.pallas_call(
        begin_kernel,
        grid=(share,),
        in_specs=[pl.BlockSpec((window, place.shape[0]), lambda t: (0, t))] * 3
        + [pl.BlockSpec(place.shape, lambda t: (0, 0)), pl.BlockSpec((window, SPAN), lambda t: (0, t + ring * share))],
        out_specs=pl.BlockSpec((window, SPAN), lambda t: (0, t)),
        out_shape=pltpu.VMEM((window, region // rings), jnp.float32),
        compiler_params=pltpu.CompilerParams(vmem_limit_bytes=24 * 1024 * 1024),
        cost_estimate=COST,
        name="begin",
    )(*pieces, place, other_terms)


def finish_kernel(own, up, down, place, *refs):
    residuals, (occ_ref, pair_ref, out_ref) = refs[:-3], refs[-3:]
    last = placed((own, up, down), place)
    for ring, residual in enumerate(residuals):

        @pl.when(pl.program_id(0) // (pl.num_programs(0) // len(residuals)) == ring)
        def _():
            out_ref[...] = (residual[...] + last) / (occ_ref[...] - pair_ref[...])


def finish(pieces, place, residuals, occupied_sum, pair_energy):
    window, region = pieces[0].shape[0], pair_energy.shape[1]
    spans = region // SPAN
    return pl.pallas_call(
        finish_kernel,
        grid=(spans,),
        in_specs=[pl.BlockSpec((window, place.shape[0]), lambda t: (0, t))] * 3
        + [pl.BlockSpec(place.shape, lambda t: (0, 0))]
        + [ring_block(window, SPAN, ring, spans // len(residuals)) for ring in range(len(residuals))]
        + [pl.BlockSpec((window, 1), lambda t: (0, 0)), pl.BlockSpec((1, SPAN), lambda t: (0, t))],
        out_specs=pl.BlockSpec((window, SPAN), lambda t: (0, t)),
        out_shape=jax.ShapeDtypeStruct((window, region), jnp.float32),
        compiler_params=pltpu.CompilerParams(vmem_limit_bytes=24 * 1024 * 1024),
        cost_estimate=COST,
        name="finish",
    )(*pieces, place, *residuals, occupied_sum, pair_energy)


def shift(values, count, step):
    return lax.ppermute(values, "ka", [(i, (i + step) % count) for i in range(count)])


def shards(amplitudes, integrals, other_terms, tile_block, occ_pairs, occ_energy, pair_energy):
    wide_count = lax.axis_size("ta")
    wide_index = lax.axis_index("ta")
    narrow_count = lax.axis_size("ka")
    narrow_index = lax.axis_index("ka")
    region, stripe = integrals.shape
    slice_rows = region // wide_count
    region_tiles = region // TILE
    dealt = integrals.reshape(wide_count, slice_rows, stripe)

    def parts(steps):
        return jnp.stack(
            [
                lax.dynamic_slice(
                    amplitudes,
                    (0, lax.rem(narrow_index + narrow_count + step, narrow_count) * stripe),
                    (amplitudes.shape[0], stripe),
                )
                for step in steps
            ]
        )

    far = narrow_count // 2
    stripes = [None] * narrow_count
    stripes[0] = parts([0])[0]
    rising, falling = parts(range(1, far + 1)), parts(range(-1, -far, -1))
    for hop in range(1, far + 1):
        rising = shift(rising, narrow_count, 1)
        stripes[narrow_count - hop] = rising[0]
        rising = rising[1:]
        if hop < far:
            falling = shift(falling, narrow_count, -1)
            stripes[hop] = falling[0]
            falling = falling[1:]

    tiles = lax.dynamic_slice(tile_block, (wide_index * region_tiles,), (region_tiles,)).astype(jnp.float32)
    columns = (narrow_index * stripe + jnp.arange(stripe, dtype=jnp.int32)) // TILE
    column_blocks = block_of(tiles, columns)

    occ_count = occ_energy.shape[0]
    choosers = (
        occ_pairs.reshape(-1)[:, None] == jnp.arange(occ_count, dtype=jnp.int32)[None, :]
    ).astype(jnp.float32)
    energies = jnp.dot(choosers, occ_energy, precision=lax.Precision.HIGHEST).reshape(occ_pairs.shape[0], 2)
    occupied_sum = (energies[:, 0] + energies[:, 1])[:, None]

    starts = [sum(CHUNKS[:i]) for i in range(len(CHUNKS))]
    sends = [dealt[:, first : first + size] for first, size in zip(starts, CHUNKS)]
    later, _ = lax.optimization_barrier((sends[1:], stripes[1]))
    group = SPAN
    per_group = group // slice_rows
    places = []
    for first, size in zip(starts, CHUNKS):
        source = jnp.arange(per_group * size, dtype=jnp.int32)
        target = (source // size) * slice_rows + first + source % size
        places.append((target[:, None] == jnp.arange(group, dtype=jnp.int32)[None, :]).astype(jnp.bfloat16))
    window, held = gather(stripes, list(later) + places)
    sends, places = sends[:1] + held[: len(later)], held[len(later) :]

    def exchange(index, size, after):
        sent = sends[index]
        if after:
            sent, *_ = lax.optimization_barrier((sent, *after))
        arrived = lax.all_to_all(sent, "ta", split_axis=0, concat_axis=0, tiled=True)
        return arrived.reshape(wide_count * size, stripe)

    def shared(arrived, first, size, step, rings):
        per_slice = size // UNIT
        unit = jnp.arange(wide_count * per_slice, dtype=jnp.int32)
        row_tile = ((unit // per_slice) * slice_rows + first + (unit % per_slice) * UNIT) // TILE
        keep = (block_of(tiles, row_tile)[:, None] == column_blocks[None, :]).astype(jnp.float32)
        space = pltpu.VMEM if first else pltpu.HBM
        return product(window, arrived, keep, narrow_count, step, rings, space)

    def reduced(shares, turn, after):
        long, short = shares[far], shares[(far + turn) % narrow_count]
        for hop in range(1, far + 1):
            if hop == far - 1 and after:
                short, *_ = lax.optimization_barrier((short, *after))
            long = shift(long, narrow_count, turn)
            if hop < far:
                mine = shares[(turn * (far - hop)) % narrow_count]
                long = (long.astype(jnp.float32) + mine.astype(jnp.float32)).astype(jnp.bfloat16)
                short = shift(short, narrow_count, -turn)
            if hop < far - 1:
                mine = shares[(far + turn * (hop + 1)) % narrow_count]
                short = (short.astype(jnp.float32) + mine.astype(jnp.float32)).astype(jnp.bfloat16)
        return [shares[0], long, short]

    arrived = []
    for index, size in enumerate(CHUNKS):
        arrived.append(exchange(index, size, arrived[-1:]))
    shares = [shared(arrived[n], starts[n], CHUNKS[n], STEPS[n], 1) for n in range(len(CHUNKS))]
    pieces = [reduced(shares[0], 1, shares[1][:1]), reduced(shares[1], -1, [])]
    residual = begin(pieces[0], places[0], other_terms, 0, 1)
    return finish(pieces[1], places[1], [residual], occupied_sum, pair_energy[None, :])


def solution(mesh):
    return jax.shard_map(
        shards,
        mesh=mesh,
        in_specs=(P("ka", "ta"), P("ta", "ka"), P("ka", "ta"), P(), P("ka", None), P(), P("ta")),
        out_specs=P("ka", "ta"),
        check_vma=False,
    )
```

time: 167 us -> 160 us (0.958)
  starting transfers between devices: 53.2 us -> 49.9 us
  Pallas kernels: 19.2 us -> 17.5 us
    all_to_all x2, waiting for transfers between devices: 27.2 us -> 18.7 us  [exchange(): lax.all_to_all(sent, 'ta', split_axis=0, concat_axis=0, tiled=True)]
    ppermute x21, waiting for transfers between devices: 41.6 us -> 49.3 us  [shift(): lax.ppermute(values, 'ka', [(i, (i + step) % count) for i in range(count)])]
    convert_element_type x10, other arithmetic: 7.6 us -> 3.76 us  [the longest x6 3.44 us: reduced(): (long.astype(jnp.float32) + mine.astype(jnp.float32)).astype(jnp.bfloat16)]
    pallas_call x1, Pallas kernels: 6.5 us -> 3.42 us  [finish(): pl.pallas_call(finish_kernel, grid=(spans,), in_specs=[pl.BlockSpec((wind...]
    ppermute x21, starting transfers between devices: 41 us -> 38.2 us  [shift(): lax.ppermute(values, 'ka', [(i, (i + step) % count) for i in range(count)])]
    squeeze x0 -> x4, local copies, waits for them, and re-layouts: none -> 2.54 us  [the longest x3 1.9 us: shards(): stripes[narrow_count - hop] = rising[0]]
    unnamed x41 -> x29, local copies, waits for them, and re-layouts: 3.24 us -> 0.79 us
    convert_element_type x2, other arithmetic: 0.66 us -> 3.06 us  [shards(): (target[:, None] == jnp.arange(group, dtype=jnp.int32)[None, :]).astype(j...]
  transfers between devices with their start and end apart: 23 -> 23, of which waited for: 11 -> 12; matrix products, arithmetic and copies ran while one was open for 10% -> 11% of each run, Pallas kernels for 4% -> 5%
where the time goes in v3:
time: 160 us; the launch traced here: 159 us
  waiting for transfers between devices  68 us (42%)
  starting transfers between devices  49.9 us (31%)
  Pallas kernels  17.5 us (11%)
  local copies, waits for them, and re-layouts  13.1 us (8%)
  other arithmetic  7.31 us (5%)
  matrix products  3.09 us (2%)
    ppermute x21, waiting for transfers between devices, shift(): lax.ppermute(values, 'ka', [(i, (i + step) % count) for i in range(count)])  49.3 us
    ppermute x21, starting transfers between devices, shift(): lax.ppermute(values, 'ka', [(i, (i + step) % count) for i in range(count)])  38.2 us
    all_to_all x2, waiting for transfers between devices, exchange(): lax.all_to_all(sent, 'ta', split_axis=0, concat_axis=0, tiled=True)  18.7 us
    all_to_all x2, starting transfers between devices, exchange(): lax.all_to_all(sent, 'ta', split_axis=0, concat_axis=0, tiled=True)  11.6 us
    pallas_call x2, Pallas kernels, product(): pl.pallas_call(functools.partial(product_kernel, rings), grid=(count // s...  8.84 us
    slice x2, local copies, waits for them, and re-layouts, shards(): dealt[:, first:first + size]  7.95 us
    pallas_call x1, Pallas kernels, begin(): pl.pallas_call(begin_kernel, grid=(share,), in_specs=[pl.BlockSpec((windo...  4.03 us
    convert_element_type x6, other arithmetic, reduced(): (long.astype(jnp.float32) + mine.astype(jnp.float32)).astype(jnp.bfloat16)  3.44 us
  transfers between devices with their start and end apart: 23, of which 12 were waited for; matrix products, arithmetic and copies ran while one was open for 11% of the time, Pallas kernels for 5%

profile of v3, /device:TPU:8, one launch (start us, length us, event | category | flops | bytes accessed | tf_op | source)
XLA Modules:
  0.0 159.3 jit_solution(7260550201772908951)
XLA Ops:
  0.0 4.9 %slice.67 = bf16[32,112,640]{2,1,0:T(8,128)(2,1)} slice(bf16[32,160,640]{2,1,0:T(8,128)(2,1)} %bitcast.47), slice={[0:32], [0:112], [0:640]} | slice | bytes 9175040 | tf_op jit(solution)/shard_map/slice | solution.py:196
  4.9 7.7 %all-to-all-start = ((bf16[32,112,640]{2,1,0:T(8,128)(2,1)}), bf16[32,112,640]{2,1,0:T(8,128)(2,1)}, u32[]{:S(2)}, u32[]{:S(2)}) async-start(bf16[32,112,640]{2,1,0:T(8,128)(2,1)} %slice.67), calls=%async_computation | async-start | bytes 9175040 | tf_op jit(solution)/shard_map/all_to_all | solution.py:212
  12.7 0.7 dynamic-slice_bitcast_fusion.3
  13.4 5.9 %collective-permute-start = (bf16[3,64,640]{2,1,0:T(8,128)(2,1)S(1)}, bf16[3,64,640]{2,1,0:T(8,128)(2,1)S(1)}, u32[]{:S(2)}, u32[]{:S(2)}) collective-permute-start(bf16[3,64,640]{2,1,0:T(8,128)(2,1)S(1)} %pad_maximum_fusion.1), channel_id=1, source_target_pairs={{0,7},{1,0},{2,1},{3,2},{4,3},{5,4},{6,5},{7,6},{8,15},{9,8},{10,9... | collective-permute-start | bytes 737288 | tf_op jit(solution)/shard_map/ppermute | solution.py:146
  19.6 0.9 fusion.3
  20.5 1.3 fusion.1.refs_10_
  21.8 1.8 %fusion.refs_9_ = bf16[896,1280]{1,0:T(8,128)(2,1)} fusion(s32[896]{0:T(1024)S(1)} %fusion.14), kind=kLoop, calls=%fused_computation.1 | loop fusion | flops 2293760 | bytes 2297344 | tf_op jit(solution)/shard_map/convert_element_type | solution.py:204
  23.6 1.1 convolution_reduce_fusion
  24.7 3.1 %slice.66.refs_8_ = bf16[32,48,640]{2,1,0:T(8,128)(2,1)} slice(bf16[32,160,640]{2,1,0:T(8,128)(2,1)} %bitcast.48), slice={[0:32], [112:160], [0:640]} | slice | bytes 3932160 | tf_op jit(solution)/shard_map/slice | solution.py:196
  28.2 3.3 %collective-permute-start.1 = (bf16[2,64,640]{2,1,0:T(8,128)(2,1)S(1)}, bf16[2,64,640]{2,1,0:T(8,128)(2,1)S(1)}, u32[]{:S(2)}, u32[]{:S(2)}) collective-permute-start(bf16[2,64,640]{2,1,0:T(8,128)(2,1)S(1)} %slice.57), channel_id=1, source_target_pairs={{0,7},{1,0},{2,1},{3,2},{4,3},{5,4},{6,5},{7,6},{8,15},{9,8},{10,9... | collective-permute-start | bytes 491528 | tf_op jit(solution)/shard_map/ppermute | solution.py:146
  31.6 0.6 slice_bitcast_fusion.4.refs_1_
  32.2 0.6 slice_bitcast_fusion.refs_7_
  32.9 7.1 %collective-permute-done.4 = bf16[3,64,640]{2,1,0:T(8,128)(2,1)S(1)} collective-permute-done((bf16[3,64,640]{2,1,0:T(8,128)(2,1)S(1)}, bf16[3,64,640]{2,1,0:T(8,128)(2,1)S(1)}, u32[]{:S(2)}, u32[]{:S(2)}) %collective-permute-start.4) | collective-permute-done | bytes 245792 | tf_op jit(solution)/shard_map/ppermute | solution.py:146
  40.1 0.6 fusion.38
  40.7 3.2 %collective-permute-start.2 = (bf16[1,64,640]{2,1,0:T(8,128)(2,1)S(1)}, bf16[1,64,640]{2,1,0:T(8,128)(2,1)S(1)}, u32[]{:S(2)}, u32[]{:S(2)}) collective-permute-start(bf16[1,64,640]{2,1,0:T(8,128)(2,1)S(1)} %get-tuple-element.61), channel_id=1, source_target_pairs={{0,7},{1,0},{2,1},{3,2},{4,3},{5,4},{6,5},{7,6},{8,15},{9,8},{10,9... | collective-permute-start | bytes 245768 | tf_op jit(solution)/shard_map/ppermute | solution.py:146
  43.9 2.6 %collective-permute-done.5 = bf16[2,64,640]{2,1,0:T(8,128)(2,1)S(1)} collective-permute-done((bf16[2,64,640]{2,1,0:T(8,128)(2,1)S(1)}, bf16[2,64,640]{2,1,0:T(8,128)(2,1)S(1)}, u32[]{:S(2)}, u32[]{:S(2)}) %collective-permute-start.5) | collective-permute-done | bytes 163872 | tf_op jit(solution)/shard_map/ppermute | solution.py:146
  46.6 0.6 slice_bitcast_fusion.2
  47.2 0.6 slice_bitcast_fusion.1.refs_6_
  47.8 5.0 %collective-permute-done.6 = bf16[1,64,640]{2,1,0:T(8,128)(2,1)S(1)} collective-permute-done((bf16[1,64,640]{2,1,0:T(8,128)(2,1)S(1)}, bf16[1,64,640]{2,1,0:T(8,128)(2,1)S(1)}, u32[]{:S(2)}, u32[]{:S(2)}) %collective-permute-start.6) | collective-permute-done | bytes 81952 | tf_op jit(solution)/shard_map/ppermute | solution.py:146
  52.9 0.6 copy-done.12
  53.5 1.2 gather_window.1
  54.7 18.7 %all-to-all-done = bf16[32,112,640]{2,1,0:T(8,128)(2,1)} async-done(((bf16[32,112,640]{2,1,0:T(8,128)(2,1)}), bf16[32,112,640]{2,1,0:T(8,128)(2,1)}, u32[]{:S(2)}, u32[]{:S(2)}) %all-to-all-start) | async-done | bytes 4587552 | tf_op jit(solution)/shard_map/all_to_all | solution.py:212
  73.4 6.7 %product.3 = (bf16[64,3584]{1,0:T(8,128)(2,1)}, bf16[64,3584]{1,0:T(8,128)(2,1)}, bf16[64,3584]{1,0:T(8,128)(2,1)}, bf16[64,3584]{1,0:T(8,128)(2,1)}, bf16[64,35...) custom-call(f32[224,640]{1,0:T(8,128)S(1)} %compare_convert_fusion.keep_ref, ...), custom_call_target="tpu_custom_call" | custom-call | flops 1000 | bytes 1000 | tf_op jit(solution)/shard_map/product/pallas_call | solution.py:71
  80.1 1.9 %collective-permute-start.14 = (bf16[64,3584]{1,0:T(8,128)(2,1)}, bf16[64,3584]{1,0:T(8,128)(2,1)}, u32[]{:S(2)}, u32[]{:S(2)}) collective-permute-start(bf16[64,3584]{1,0:T(8,128)(2,1)} %get-tuple-element.42), channel_id=1, source_target_pairs={{0,1},{1,2},{2,3},{3,4},{4,5},{5,6},{6,7},{7,0},{8,9},{9,10},{10,1... | collective-permute-start | bytes 1376264 | tf_op jit(solution)/shard_map/ppermute | solution.py:146
  82.2 0.2 reshape.148
  82.5 0.9 convolution_bitcast_fusion.1
  83.5 3.9 %all-to-all-start.1 = ((bf16[32,48,640]{2,1,0:T(8,128)(2,1)}), bf16[32,48,640]{2,1,0:T(8,128)(2,1)S(1)}, u32[]{:S(2)}, u32[]{:S(2)}) async-start(bf16[32,48,640]{2,1,0:T(8,128)(2,1)} %get-tuple-element.31), calls=%async_computation.1 | async-start | bytes 3932160 | tf_op jit(solution)/shard_map/all_to_all | solution.py:212
  87.5 4.2 %collective-permute-start.18 = (bf16[64,3584]{1,0:T(8,128)(2,1)}, bf16[64,3584]{1,0:T(8,128)(2,1)S(1)}, u32[]{:S(2)}, u32[]{:S(2)}) collective-permute-start(bf16[64,3584]{1,0:T(8,128)(2,1)} %get-tuple-element.46), channel_id=1, source_target_pairs={{0,7},{1,0},{2,1},{3,2},{4,3},{5,4},{6,5},{7,6},{8,15},{9,8},{10,9... | collective-permute-start | bytes 1376264 | tf_op jit(solution)/shard_map/ppermute | solution.py:146
  91.7 4.9 %collective-permute-done.14 = bf16[64,3584]{1,0:T(8,128)(2,1)} collective-permute-done((bf16[64,3584]{1,0:T(8,128)(2,1)}, bf16[64,3584]{1,0:T(8,128)(2,1)}, u32[]{:S(2)}, u32[]{:S(2)}) %collective-permute-start.14) | collective-permute-done | bytes 458784 | tf_op jit(solution)/shard_map/ppermute | solution.py:146
  96.6 1.3 add_convert_fusion.4
  98.0 3.8 %collective-permute-done.18 = bf16[64,3584]{1,0:T(8,128)(2,1)S(1)} collective-permute-done((bf16[64,3584]{1,0:T(8,128)(2,1)}, bf16[64,3584]{1,0:T(8,128)(2,1)S(1)}, u32[]{:S(2)}, u32[]{:S(2)}) %collective-permute-start.18) | collective-permute-done | bytes 458784 | tf_op jit(solution)/shard_map/ppermute | solution.py:146
  101.9 3.7 %collective-permute-start.19 = (bf16[64,3584]{1,0:T(8,128)(2,1)S(1)}, bf16[64,3584]{1,0:T(8,128)(2,1)S(1)}, u32[]{:S(2)}, u32[]{:S(2)}) collective-permute-start(bf16[64,3584]{1,0:T(8,128)(2,1)S(1)} %add_convert_fusion.1), channel_id=1, source_target_pairs={{0,7},{1,0},{2,1},{3,2},{4,3},{5,4},{6,5},{7,6},{8,15},{9,8},{10,9... | collective-permute-start | bytes 1376264 | tf_op jit(solution)/shard_map/ppermute | solution.py:146
  105.6 5.1 %collective-permute-done.15 = bf16[64,3584]{1,0:T(8,128)(2,1)S(1)} collective-permute-done((bf16[64,3584]{1,0:T(8,128)(2,1)S(1)}, bf16[64,3584]{1,0:T(8,128)(2,1)S(1)}, u32[]{:S(2)}, u32[]{:S(2)}) %collective-permute-start.15) | collective-permute-done | bytes 458784 | tf_op jit(solution)/shard_map/ppermute | solution.py:146
  110.7 0.9 add_convert_fusion.3
  111.5 2.9 %collective-permute-done.19 = bf16[64,3584]{1,0:T(8,128)(2,1)S(1)} collective-permute-done((bf16[64,3584]{1,0:T(8,128)(2,1)S(1)}, bf16[64,3584]{1,0:T(8,128)(2,1)S(1)}, u32[]{:S(2)}, u32[]{:S(2)}) %collective-permute-start.19) | collective-permute-done | bytes 458784 | tf_op jit(solution)/shard_map/ppermute | solution.py:146
  114.6 2.1 %product.2 = (bf16[64,1536]{1,0:T(8,128)(2,1)S(1)}, bf16[64,1536]{1,0:T(8,128)(2,1)S(1)}, bf16[64,1536]{1,0:T(8,128)(2,1)S(1)}, bf16[64,1536]{1,0:T(8,128)(2,1)S...) custom-call(f32[96,640]{1,0:T(8,128)S(1)} %compare_convert_fusion.1., ...), custom_call_target="tpu_custom_call" | custom-call | flops 1000 | bytes 1000 | tf_op jit(solution)/shard_map/product/pallas_call | solution.py:71
  116.7 3.8 %collective-permute-start.7 = (bf16[64,1536]{1,0:T(8,128)(2,1)S(1)}, bf16[64,1536]{1,0:T(8,128)(2,1)S(1)}, u32[]{:S(2)}, u32[]{:S(2)}) collective-permute-start(bf16[64,1536]{1,0:T(8,128)(2,1)S(1)} %get-tuple-element.33), channel_id=1, source_target_pairs={{0,7},{1,0},{2,1},{3,2},{4,3},{5,4},{6,5},{7,6},{8,15},{9,8},{10,9... | collective-permute-start | bytes 589832 | tf_op jit(solution)/shard_map/ppermute | solution.py:146
  120.5 3.1 %collective-permute-done.16 = bf16[64,3584]{1,0:T(8,128)(2,1)} collective-permute-done((bf16[64,3584]{1,0:T(8,128)(2,1)}, bf16[64,3584]{1,0:T(8,128)(2,1)}, u32[]{:S(2)}, u32[]{:S(2)}) %collective-permute-start.16) | collective-permute-done | bytes 458784 | tf_op jit(solution)/shard_map/ppermute | solution.py:146
  123.6 1.1 add_convert_fusion.2
  125.0 3.2 %collective-permute-start.20 = (bf16[64,3584]{1,0:T(8,128)(2,1)S(1)}, bf16[64,3584]{1,0:T(8,128)(2,1)S(1)}, u32[]{:S(2)}, u32[]{:S(2)}) collective-permute-start(bf16[64,3584]{1,0:T(8,128)(2,1)S(1)} %add_convert_fusion), channel_id=1, source_target_pairs={{0,7},{1,0},{2,1},{3,2},{4,3},{5,4},{6,5},{7,6},{8,15},{9,8},{10,9... | collective-permute-start | bytes 1376264 | tf_op jit(solution)/shard_map/ppermute | solution.py:146
  128.2 2.0 %collective-permute-start.8 = (bf16[64,1536]{1,0:T(8,128)(2,1)S(1)}, bf16[64,1536]{1,0:T(8,128)(2,1)S(1)}, u32[]{:S(2)}, u32[]{:S(2)}) collective-permute-start(bf16[64,1536]{1,0:T(8,128)(2,1)S(1)} %add_convert_fusion.9), channel_id=1, source_target_pairs={{0,7},{1,0},{2,1},{3,2},{4,3},{5,4},{6,5},{7,6},{8,15},{9,8},{10,9... | collective-permute-start | bytes 589832 | tf_op jit(solution)/shard_map/ppermute | solution.py:146
  130.3 9.7 %collective-permute-done.11 = bf16[64,1536]{1,0:T(8,128)(2,1)S(1)} collective-permute-done((bf16[64,1536]{1,0:T(8,128)(2,1)S(1)}, bf16[64,1536]{1,0:T(8,128)(2,1)S(1)}, u32[]{:S(2)}, u32[]{:S(2)}) %collective-permute-start.11) | collective-permute-done | bytes 196640 | tf_op jit(solution)/shard_map/ppermute | solution.py:146
  140.1 3.3 %collective-permute-start.9 = (bf16[64,1536]{1,0:T(8,128)(2,1)S(1)}, bf16[64,1536]{1,0:T(8,128)(2,1)S(1)}, u32[]{:S(2)}, u32[]{:S(2)}) collective-permute-start(bf16[64,1536]{1,0:T(8,128)(2,1)S(1)} %add_convert_fusion.8), channel_id=1, source_target_pairs={{0,7},{1,0},{2,1},{3,2},{4,3},{5,4},{6,5},{7,6},{8,15},{9,8},{10,9... | collective-permute-start | bytes 589832 | tf_op jit(solution)/shard_map/ppermute | solution.py:146
  143.4 4.4 %collective-permute-done.12 = bf16[64,1536]{1,0:T(8,128)(2,1)S(1)} collective-permute-done((bf16[64,1536]{1,0:T(8,128)(2,1)S(1)}, bf16[64,1536]{1,0:T(8,128)(2,1)S(1)}, u32[]{:S(2)}, u32[]{:S(2)}) %collective-permute-start.12) | collective-permute-done | bytes 196640 | tf_op jit(solution)/shard_map/ppermute | solution.py:146
  148.0 0.6 collective-permute-done.9
  148.6 3.0 %collective-permute-start.10 = (bf16[64,1536]{1,0:T(8,128)(2,1)S(1)}, bf16[64,1536]{1,0:T(8,128)(2,1)S(1)}, u32[]{:S(2)}, u32[]{:S(2)}) collective-permute-start(bf16[64,1536]{1,0:T(8,128)(2,1)S(1)} %add_convert_fusion.7), channel_id=1, source_target_pairs={{0,7},{1,0},{2,1},{3,2},{4,3},{5,4},{6,5},{7,6},{8,15},{9,8},{10,9... | collective-permute-start | bytes 589832 | tf_op jit(solution)/shard_map/ppermute | solution.py:146
  151.8 4.0 %begin.1.refs_0_ = f32[64,5120]{1,0:T(8,128)S(1)} custom-call(bf16[64,3584]{1,0:T(8,128)(2,1)S(1)} %copy-done.4, bf16[64,3584]{1,0:T(8,128)(2,1)S(1)} %collective-permute-done.17.up, bf16[64,3584]{1,0:T(8,128)(2,1)S(1)} %collective-permute-done.20.down, bf16[896,1280]{1,0:T(8,128)(2,1)S(1)} %copy-done.1, bf16[64,5120]{1,0:T(8,128)(2,1)S(1)} %copy-done.3), custom_call_target="tpu_custom_call" | custom-call | flops 1000 | bytes 1000 | tf_op jit(solution)/shard_map/begin/pallas_call | solution.py:104
  155.9 3.4 %finish.1 = f32[64,5120]{1,0:T(8,128)} custom-call(bf16[64,1536]{1,0:T(8,128)(2,1)S(1)} %get-tuple-element.32.own, bf16[64,1536]{1,0:T(8,128)(2,1)S(1)} %collective-permute-done.10.up, bf16[64,1536]{1,0:T(8,128)(2,1)S(1)} %collective-permute-done.13.down, bf16[384,1280]{1,0:T(8,128)(2,1)S(1)} %copy-done.2, f32[64,5120]{1,0:T(8,128)S(1)} %begin.1.refs_0_, ...), custom_call_target="tpu_custom_call" | custom-call | flops 1000 | bytes 1000 | tf_op jit(solution)/shard_map/finish/pallas_call | solution.py:130
  (71 shorter events, 2.2 us)
Async XLA Ops:
  0.0 82.0 %copy-start = (f32[150]{0:T(256)S(1)}, f32[150]{0:T(256)}, u32[]{:S(2)}) copy-start(f32[150]{0:T(256)} %param.12) | copy-start | bytes 1804
  4.9 7.8 %copy-start.6 = (bf16[64,5120]{1,0:T(8,128)(2,1)S(1)}, bf16[64,5120]{1,0:T(8,128)(2,1)}, u32[]{:S(2)}) copy-start(bf16[64,5120]{1,0:T(8,128)(2,1)} %param.7) | copy-start | bytes 1966084
  4.9 68.5 %all-to-all-start = ((bf16[32,112,640]{2,1,0:T(8,128)(2,1)}), bf16[32,112,640]{2,1,0:T(8,128)(2,1)}, u32[]{:S(2)}, u32[]{:S(2)}) async-start(bf16[32,112,640]{2,1,0:T(8,128)(2,1)} %slice.67), calls=%async_computation | async-start | bytes 9175040 | tf_op jit(solution)/shard_map/all_to_all | solution.py:212
  13.4 14.7 %collective-permute-start = (bf16[3,64,640]{2,1,0:T(8,128)(2,1)S(1)}, bf16[3,64,640]{2,1,0:T(8,128)(2,1)S(1)}, u32[]{:S(2)}, u32[]{:S(2)}) collective-permute-start(bf16[3,64,640]{2,1,0:T(8,128)(2,1)S(1)} %pad_maximum_fusion.1), channel_id=1, source_target_pairs={{0,7},{1,0},{2,1},{3,2},{4,3},{5,4},{6,5},{7,6},{8,15},{9,8},{10,9... | collective-permute-start | bytes 737288 | tf_op jit(solution)/shard_map/ppermute | solution.py:146
  19.4 12.0 %collective-permute-start.3 = (bf16[4,64,640]{2,1,0:T(8,128)(2,1)S(1)}, bf16[4,64,640]{2,1,0:T(8,128)(2,1)S(1)}, u32[]{:S(2)}, u32[]{:S(2)}) collective-permute-start(bf16[4,64,640]{2,1,0:T(8,128)(2,1)S(1)} %pad_maximum_fusion), channel_id=1, source_target_pairs={{0,1},{1,2},{2,3},{3,4},{4,5},{5,6},{6,7},{7,0},{8,9},{9,10},{10,1... | collective-permute-start | bytes 983048 | tf_op jit(solution)/shard_map/ppermute | solution.py:146
  23.6 4.2 %copy-start.13 = (s32[64,2]{0,1:T(2,128)S(1)}, s32[64,2]{0,1:T(2,128)}, u32[]{:S(2)}) copy-start(s32[64,2]{0,1:T(2,128)} %param.11) | copy-start | bytes 1540
  28.2 11.9 %collective-permute-start.1 = (bf16[2,64,640]{2,1,0:T(8,128)(2,1)S(1)}, bf16[2,64,640]{2,1,0:T(8,128)(2,1)S(1)}, u32[]{:S(2)}, u32[]{:S(2)}) collective-permute-start(bf16[2,64,640]{2,1,0:T(8,128)(2,1)S(1)} %slice.57), channel_id=1, source_target_pairs={{0,7},{1,0},{2,1},{3,2},{4,3},{5,4},{6,5},{7,6},{8,15},{9,8},{10,9... | collective-permute-start | bytes 491528 | tf_op jit(solution)/shard_map/ppermute | solution.py:146
  31.5 8.5 %collective-permute-start.4 = (bf16[3,64,640]{2,1,0:T(8,128)(2,1)S(1)}, bf16[3,64,640]{2,1,0:T(8,128)(2,1)S(1)}, u32[]{:S(2)}, u32[]{:S(2)}) collective-permute-start(bf16[3,64,640]{2,1,0:T(8,128)(2,1)S(1)} %slice.60), channel_id=1, source_target_pairs={{0,1},{1,2},{2,3},{3,4},{4,5},{5,6},{6,7},{7,0},{8,9},{9,10},{10,1... | collective-permute-start | bytes 737288 | tf_op jit(solution)/shard_map/ppermute | solution.py:146
  40.0 6.6 %collective-permute-start.5 = (bf16[2,64,640]{2,1,0:T(8,128)(2,1)S(1)}, bf16[2,64,640]{2,1,0:T(8,128)(2,1)S(1)}, u32[]{:S(2)}, u32[]{:S(2)}) collective-permute-start(bf16[2,64,640]{2,1,0:T(8,128)(2,1)S(1)} %slice.61), channel_id=1, source_target_pairs={{0,1},{1,2},{2,3},{3,4},{4,5},{5,6},{6,7},{7,0},{8,9},{9,10},{10,1... | collective-permute-start | bytes 491528 | tf_op jit(solution)/shard_map/ppermute | solution.py:146
  40.7 7.1 %collective-permute-start.2 = (bf16[1,64,640]{2,1,0:T(8,128)(2,1)S(1)}, bf16[1,64,640]{2,1,0:T(8,128)(2,1)S(1)}, u32[]{:S(2)}, u32[]{:S(2)}) collective-permute-start(bf16[1,64,640]{2,1,0:T(8,128)(2,1)S(1)} %get-tuple-element.61), channel_id=1, source_target_pairs={{0,7},{1,0},{2,1},{3,2},{4,3},{5,4},{6,5},{7,6},{8,15},{9,8},{10,9... | collective-permute-start | bytes 245768 | tf_op jit(solution)/shard_map/ppermute | solution.py:146
  47.2 5.7 %collective-permute-start.6 = (bf16[1,64,640]{2,1,0:T(8,128)(2,1)S(1)}, bf16[1,64,640]{2,1,0:T(8,128)(2,1)S(1)}, u32[]{:S(2)}, u32[]{:S(2)}) collective-permute-start(bf16[1,64,640]{2,1,0:T(8,128)(2,1)S(1)} %get-tuple-element.60), channel_id=1, source_target_pairs={{0,1},{1,2},{2,3},{3,4},{4,5},{5,6},{6,7},{7,0},{8,9},{9,10},{10,1... | collective-permute-start | bytes 245768 | tf_op jit(solution)/shard_map/ppermute | solution.py:146
  47.8 5.0 %copy-start.11 = (bf16[1,64,640]{2,1,0:T(8,128)(2,1)}, bf16[1,64,640]{2,1,0:T(8,128)(2,1)S(1)}, u32[]{:S(2)}) copy-start(bf16[1,64,640]{2,1,0:T(8,128)(2,1)S(1)} %collective-permute-done.2) | copy-start | bytes 245764
  52.9 0.6 copy-start.12
  80.1 16.5 %collective-permute-start.14 = (bf16[64,3584]{1,0:T(8,128)(2,1)}, bf16[64,3584]{1,0:T(8,128)(2,1)}, u32[]{:S(2)}, u32[]{:S(2)}) collective-permute-start(bf16[64,3584]{1,0:T(8,128)(2,1)} %get-tuple-element.42), channel_id=1, source_target_pairs={{0,1},{1,2},{2,3},{3,4},{4,5},{5,6},{6,7},{7,0},{8,9},{9,10},{10,1... | collective-permute-start | bytes 1376264 | tf_op jit(solution)/shard_map/ppermute | solution.py:146
  83.5 18.3 %copy-start.10 = (bf16[64,3584]{1,0:T(8,128)(2,1)S(1)}, bf16[64,3584]{1,0:T(8,128)(2,1)}, u32[]{:S(2)}) copy-start(bf16[64,3584]{1,0:T(8,128)(2,1)} %get-tuple-element.47) | copy-start | bytes 1376260
  83.5 31.1 %all-to-all-start.1 = ((bf16[32,48,640]{2,1,0:T(8,128)(2,1)}), bf16[32,48,640]{2,1,0:T(8,128)(2,1)S(1)}, u32[]{:S(2)}, u32[]{:S(2)}) async-start(bf16[32,48,640]{2,1,0:T(8,128)(2,1)} %get-tuple-element.31), calls=%async_computation.1 | async-start | bytes 3932160 | tf_op jit(solution)/shard_map/all_to_all | solution.py:212
  87.5 23.2 %copy-start.9 = (bf16[64,3584]{1,0:T(8,128)(2,1)S(1)}, bf16[64,3584]{1,0:T(8,128)(2,1)}, u32[]{:S(2)}) copy-start(bf16[64,3584]{1,0:T(8,128)(2,1)} %get-tuple-element.44) | copy-start | bytes 1376260
  87.5 27.0 %copy-start.8 = (bf16[64,3584]{1,0:T(8,128)(2,1)S(1)}, bf16[64,3584]{1,0:T(8,128)(2,1)}, u32[]{:S(2)}) copy-start(bf16[64,3584]{1,0:T(8,128)(2,1)} %get-tuple-element.48) | copy-start | bytes 1376260
  87.5 14.3 %collective-permute-start.18 = (bf16[64,3584]{1,0:T(8,128)(2,1)}, bf16[64,3584]{1,0:T(8,128)(2,1)S(1)}, u32[]{:S(2)}, u32[]{:S(2)}) collective-permute-start(bf16[64,3584]{1,0:T(8,128)(2,1)} %get-tuple-element.46), channel_id=1, source_target_pairs={{0,7},{1,0},{2,1},{3,2},{4,3},{5,4},{6,5},{7,6},{8,15},{9,8},{10,9... | collective-permute-start | bytes 1376264 | tf_op jit(solution)/shard_map/ppermute | solution.py:146
  97.9 12.8 %collective-permute-start.15 = (bf16[64,3584]{1,0:T(8,128)(2,1)S(1)}, bf16[64,3584]{1,0:T(8,128)(2,1)S(1)}, u32[]{:S(2)}, u32[]{:S(2)}) collective-permute-start(bf16[64,3584]{1,0:T(8,128)(2,1)S(1)} %add_convert_fusion.4), channel_id=1, source_target_pairs={{0,1},{1,2},{2,3},{3,4},{4,5},{5,6},{6,7},{7,0},{8,9},{9,10},{10,1... | collective-permute-start | bytes 1376264 | tf_op jit(solution)/shard_map/ppermute | solution.py:146
  101.9 12.6 %collective-permute-start.19 = (bf16[64,3584]{1,0:T(8,128)(2,1)S(1)}, bf16[64,3584]{1,0:T(8,128)(2,1)S(1)}, u32[]{:S(2)}, u32[]{:S(2)}) collective-permute-start(bf16[64,3584]{1,0:T(8,128)(2,1)S(1)} %add_convert_fusion.1), channel_id=1, source_target_pairs={{0,7},{1,0},{2,1},{3,2},{4,3},{5,4},{6,5},{7,6},{8,15},{9,8},{10,9... | collective-permute-start | bytes 1376264 | tf_op jit(solution)/shard_map/ppermute | solution.py:146
  111.5 12.1 %collective-permute-start.16 = (bf16[64,3584]{1,0:T(8,128)(2,1)}, bf16[64,3584]{1,0:T(8,128)(2,1)}, u32[]{:S(2)}, u32[]{:S(2)}) collective-permute-start(bf16[64,3584]{1,0:T(8,128)(2,1)} %add_convert_fusion.3), channel_id=1, source_target_pairs={{0,1},{1,2},{2,3},{3,4},{4,5},{5,6},{6,7},{7,0},{8,9},{9,10},{10,1... | collective-permute-start | bytes 1376264 | tf_op jit(solution)/shard_map/ppermute | solution.py:146
  114.6 9.0 %copy-start.7 = (bf16[64,3584]{1,0:T(8,128)(2,1)S(1)}, bf16[64,3584]{1,0:T(8,128)(2,1)}, u32[]{:S(2)}) copy-start(bf16[64,3584]{1,0:T(8,128)(2,1)} %get-tuple-element.45) | copy-start | bytes 1376260
  116.7 35.0 %copy-start.1 = (bf16[896,1280]{1,0:T(8,128)(2,1)S(1)}, bf16[896,1280]{1,0:T(8,128)(2,1)}, u32[]{:S(2)}) copy-start(bf16[896,1280]{1,0:T(8,128)(2,1)} %get-tuple-element.50.place) | copy-start | bytes 6881284
  116.7 35.0 %copy-start.3 = (bf16[64,5120]{1,0:T(8,128)(2,1)S(1)}, bf16[64,5120]{1,0:T(8,128)(2,1)}, u32[]{:S(2)}) copy-start(bf16[64,5120]{1,0:T(8,128)(2,1)} %other_ref.1) | copy-start | bytes 1966084
  116.7 35.0 %copy-start.4 = (bf16[64,3584]{1,0:T(8,128)(2,1)S(1)}, bf16[64,3584]{1,0:T(8,128)(2,1)}, u32[]{:S(2)}) copy-start(bf16[64,3584]{1,0:T(8,128)(2,1)} %get-tuple-element.41.own) | copy-start | bytes 1376260
  116.7 11.5 %collective-permute-start.7 = (bf16[64,1536]{1,0:T(8,128)(2,1)S(1)}, bf16[64,1536]{1,0:T(8,128)(2,1)S(1)}, u32[]{:S(2)}, u32[]{:S(2)}) collective-permute-start(bf16[64,1536]{1,0:T(8,128)(2,1)S(1)} %get-tuple-element.33), channel_id=1, source_target_pairs={{0,7},{1,0},{2,1},{3,2},{4,3},{5,4},{6,5},{7,6},{8,15},{9,8},{10,9... | collective-permute-start | bytes 589832 | tf_op jit(solution)/shard_map/ppermute | solution.py:146
  124.8 26.9 %collective-permute-start.17 = (bf16[64,3584]{1,0:T(8,128)(2,1)S(1)}, bf16[64,3584]{1,0:T(8,128)(2,1)S(1)}, u32[]{:S(2)}, u32[]{:S(2)}) collective-permute-start(bf16[64,3584]{1,0:T(8,128)(2,1)S(1)} %add_convert_fusion.2), channel_id=1, source_target_pairs={{0,1},{1,2},{2,3},{3,4},{4,5},{5,6},{6,7},{7,0},{8,9},{9,10},{10,1... | collective-permute-start | bytes 1376264 | tf_op jit(solution)/shard_map/ppermute | solution.py:146
  124.9 15.0 %collective-permute-start.11 = (bf16[64,1536]{1,0:T(8,128)(2,1)S(1)}, bf16[64,1536]{1,0:T(8,128)(2,1)S(1)}, u32[]{:S(2)}, u32[]{:S(2)}) collective-permute-start(bf16[64,1536]{1,0:T(8,128)(2,1)S(1)} %get-tuple-element.37), channel_id=1, source_target_pairs={{0,1},{1,2},{2,3},{3,4},{4,5},{5,6},{6,7},{7,0},{8,9},{9,10},{10,1... | collective-permute-start | bytes 589832 | tf_op jit(solution)/shard_map/ppermute | solution.py:146
  125.0 26.8 %collective-permute-start.20 = (bf16[64,3584]{1,0:T(8,128)(2,1)S(1)}, bf16[64,3584]{1,0:T(8,128)(2,1)S(1)}, u32[]{:S(2)}, u32[]{:S(2)}) collective-permute-start(bf16[64,3584]{1,0:T(8,128)(2,1)S(1)} %add_convert_fusion), channel_id=1, source_target_pairs={{0,7},{1,0},{2,1},{3,2},{4,3},{5,4},{6,5},{7,6},{8,15},{9,8},{10,9... | collective-permute-start | bytes 1376264 | tf_op jit(solution)/shard_map/ppermute | solution.py:146
  128.2 11.8 %collective-permute-start.8 = (bf16[64,1536]{1,0:T(8,128)(2,1)S(1)}, bf16[64,1536]{1,0:T(8,128)(2,1)S(1)}, u32[]{:S(2)}, u32[]{:S(2)}) collective-permute-start(bf16[64,1536]{1,0:T(8,128)(2,1)S(1)} %add_convert_fusion.9), channel_id=1, source_target_pairs={{0,7},{1,0},{2,1},{3,2},{4,3},{5,4},{6,5},{7,6},{8,15},{9,8},{10,9... | collective-permute-start | bytes 589832 | tf_op jit(solution)/shard_map/ppermute | solution.py:146
  140.0 7.9 %collective-permute-start.12 = (bf16[64,1536]{1,0:T(8,128)(2,1)S(1)}, bf16[64,1536]{1,0:T(8,128)(2,1)S(1)}, u32[]{:S(2)}, u32[]{:S(2)}) collective-permute-start(bf16[64,1536]{1,0:T(8,128)(2,1)S(1)} %add_convert_fusion.6), channel_id=1, source_target_pairs={{0,1},{1,2},{2,3},{3,4},{4,5},{5,6},{6,7},{7,0},{8,9},{9,10},{10,1... | collective-permute-start | bytes 589832 | tf_op jit(solution)/shard_map/ppermute | solution.py:146
  140.1 8.4 %collective-permute-start.9 = (bf16[64,1536]{1,0:T(8,128)(2,1)S(1)}, bf16[64,1536]{1,0:T(8,128)(2,1)S(1)}, u32[]{:S(2)}, u32[]{:S(2)}) collective-permute-start(bf16[64,1536]{1,0:T(8,128)(2,1)S(1)} %add_convert_fusion.8), channel_id=1, source_target_pairs={{0,7},{1,0},{2,1},{3,2},{4,3},{5,4},{6,5},{7,6},{8,15},{9,8},{10,9... | collective-permute-start | bytes 589832 | tf_op jit(solution)/shard_map/ppermute | solution.py:146
  147.9 7.9 %collective-permute-start.13 = (bf16[64,1536]{1,0:T(8,128)(2,1)S(1)}, bf16[64,1536]{1,0:T(8,128)(2,1)S(1)}, u32[]{:S(2)}, u32[]{:S(2)}) collective-permute-start(bf16[64,1536]{1,0:T(8,128)(2,1)S(1)} %add_convert_fusion.5), channel_id=1, source_target_pairs={{0,1},{1,2},{2,3},{3,4},{4,5},{5,6},{6,7},{7,0},{8,9},{9,10},{10,1... | collective-permute-start | bytes 589832 | tf_op jit(solution)/shard_map/ppermute | solution.py:146
  148.6 7.2 %collective-permute-start.10 = (bf16[64,1536]{1,0:T(8,128)(2,1)S(1)}, bf16[64,1536]{1,0:T(8,128)(2,1)S(1)}, u32[]{:S(2)}, u32[]{:S(2)}) collective-permute-start(bf16[64,1536]{1,0:T(8,128)(2,1)S(1)} %add_convert_fusion.7), channel_id=1, source_target_pairs={{0,7},{1,0},{2,1},{3,2},{4,3},{5,4},{6,5},{7,6},{8,15},{9,8},{10,9... | collective-permute-start | bytes 589832 | tf_op jit(solution)/shard_map/ppermute | solution.py:146
  151.8 4.1 %copy-start.2 = (bf16[384,1280]{1,0:T(8,128)(2,1)S(1)}, bf16[384,1280]{1,0:T(8,128)(2,1)}, u32[]{:S(2)}) copy-start(bf16[384,1280]{1,0:T(8,128)(2,1)} %get-tuple-element.40.place) | copy-start | bytes 2949124
  151.8 4.1 %copy-start.5 = (f32[5120]{0:T(1024)S(1)}, f32[5120]{0:T(1024)}, u32[]{:S(2)}) copy-start(f32[5120]{0:T(1024)} %param.13) | copy-start | bytes 61444

commit v4 on v3

--- a/solution.py
+++ b/solution.py
@@ -90,8 +90,8 @@
     share = own + up + down
     high = share.astype(jnp.bfloat16)
     low = (share - high.astype(jnp.float32)).astype(jnp.bfloat16)
-    moved = jnp.dot(high, place[...], preferred_element_type=jnp.float32)
-    return moved + jnp.dot(low, place[...], preferred_element_type=jnp.float32)
+    moved = jnp.dot(jnp.concatenate([high, low], axis=0), place[...], preferred_element_type=jnp.float32)
+    return moved[: share.shape[0]] + moved[share.shape[0] :]
 
 
 def begin_kernel(own, up, down, place, other_ref, out_ref):

time: 160 us -> 159 us (level)
  Pallas kernels: 17.5 us -> 15.4 us
    pallas_call x1, Pallas kernels: 4.03 us -> 2.38 us  [begin(): pl.pallas_call(begin_kernel, grid=(share,), in_specs=[pl.BlockSpec((windo...]
  transfers between devices with their start and end apart: 23 -> 23, of which waited for: 12 -> 13; matrix products, arithmetic and copies ran while one was open for 11% -> 11% of each run, Pallas kernels for 5% -> 4%
where the time goes in v4:
time: 159 us; the launch traced here: 158 us
  waiting for transfers between devices  68.6 us (43%)
  starting transfers between devices  49.9 us (31%)
  Pallas kernels  15.4 us (10%)
  local copies, waits for them, and re-layouts  13.1 us (8%)
  other arithmetic  7.31 us (5%)
  matrix products  3.09 us (2%)
    ppermute x21, waiting for transfers between devices, shift(): lax.ppermute(values, 'ka', [(i, (i + step) % count) for i in range(count)])  50 us
    ppermute x21, starting transfers between devices, shift(): lax.ppermute(values, 'ka', [(i, (i + step) % count) for i in range(count)])  38.2 us
    all_to_all x2, waiting for transfers between devices, exchange(): lax.all_to_all(sent, 'ta', split_axis=0, concat_axis=0, tiled=True)  18.7 us
    all_to_all x2, starting transfers between devices, exchange(): lax.all_to_all(sent, 'ta', split_axis=0, concat_axis=0, tiled=True)  11.6 us
    pallas_call x2, Pallas kernels, product(): pl.pallas_call(functools.partial(product_kernel, rings), grid=(count // s...  8.84 us
    slice x2, local copies, waits for them, and re-layouts, shards(): dealt[:, first:first + size]  7.95 us
    convert_element_type x6, other arithmetic, reduced(): (long.astype(jnp.float32) + mine.astype(jnp.float32)).astype(jnp.bfloat16)  3.44 us
  transfers between devices with their start and end apart: 23, of which 13 were waited for; matrix products, arithmetic and copies ran while one was open for 11% of the time, Pallas kernels for 4%

profile of v4, /device:TPU:8, one launch (start us, length us, event | category | flops | bytes accessed | tf_op | source)
XLA Modules:
  0.0 157.9 jit_solution(5462010730281161577)
XLA Ops:
  0.0 4.9 %slice.67 = bf16[32,112,640]{2,1,0:T(8,128)(2,1)} slice(bf16[32,160,640]{2,1,0:T(8,128)(2,1)} %bitcast.47), slice={[0:32], [0:112], [0:640]} | slice | bytes 9175040 | tf_op jit(solution)/shard_map/slice | solution.py:196
  4.9 7.7 %all-to-all-start = ((bf16[32,112,640]{2,1,0:T(8,128)(2,1)}), bf16[32,112,640]{2,1,0:T(8,128)(2,1)}, u32[]{:S(2)}, u32[]{:S(2)}) async-start(bf16[32,112,640]{2,1,0:T(8,128)(2,1)} %slice.67), calls=%async_computation | async-start | bytes 9175040 | tf_op jit(solution)/shard_map/all_to_all | solution.py:212
  12.7 0.7 dynamic-slice_bitcast_fusion.3
  13.4 5.9 %collective-permute-start = (bf16[3,64,640]{2,1,0:T(8,128)(2,1)S(1)}, bf16[3,64,640]{2,1,0:T(8,128)(2,1)S(1)}, u32[]{:S(2)}, u32[]{:S(2)}) collective-permute-start(bf16[3,64,640]{2,1,0:T(8,128)(2,1)S(1)} %pad_maximum_fusion.1), channel_id=1, source_target_pairs={{0,7},{1,0},{2,1},{3,2},{4,3},{5,4},{6,5},{7,6},{8,15},{9,8},{10,9... | collective-permute-start | bytes 737288 | tf_op jit(solution)/shard_map/ppermute | solution.py:146
  19.6 0.9 fusion.3
  20.5 1.3 fusion.1.refs_10_
  21.8 1.8 %fusion.refs_9_ = bf16[896,1280]{1,0:T(8,128)(2,1)} fusion(s32[896]{0:T(1024)S(1)} %fusion.14), kind=kLoop, calls=%fused_computation.1 | loop fusion | flops 2293760 | bytes 2297344 | tf_op jit(solution)/shard_map/convert_element_type | solution.py:204
  23.6 1.1 convolution_reduce_fusion
  24.7 3.1 %slice.66.refs_8_ = bf16[32,48,640]{2,1,0:T(8,128)(2,1)} slice(bf16[32,160,640]{2,1,0:T(8,128)(2,1)} %bitcast.48), slice={[0:32], [112:160], [0:640]} | slice | bytes 3932160 | tf_op jit(solution)/shard_map/slice | solution.py:196
  28.2 3.3 %collective-permute-start.1 = (bf16[2,64,640]{2,1,0:T(8,128)(2,1)S(1)}, bf16[2,64,640]{2,1,0:T(8,128)(2,1)S(1)}, u32[]{:S(2)}, u32[]{:S(2)}) collective-permute-start(bf16[2,64,640]{2,1,0:T(8,128)(2,1)S(1)} %slice.57), channel_id=1, source_target_pairs={{0,7},{1,0},{2,1},{3,2},{4,3},{5,4},{6,5},{7,6},{8,15},{9,8},{10,9... | collective-permute-start | bytes 491528 | tf_op jit(solution)/shard_map/ppermute | solution.py:146
  31.6 0.6 slice_bitcast_fusion.4.refs_1_
  32.2 0.6 slice_bitcast_fusion.refs_7_
  32.9 7.1 %collective-permute-done.4 = bf16[3,64,640]{2,1,0:T(8,128)(2,1)S(1)} collective-permute-done((bf16[3,64,640]{2,1,0:T(8,128)(2,1)S(1)}, bf16[3,64,640]{2,1,0:T(8,128)(2,1)S(1)}, u32[]{:S(2)}, u32[]{:S(2)}) %collective-permute-start.4) | collective-permute-done | bytes 245792 | tf_op jit(solution)/shard_map/ppermute | solution.py:146
  40.1 0.6 fusion.38
  40.7 3.2 %collective-permute-start.2 = (bf16[1,64,640]{2,1,0:T(8,128)(2,1)S(1)}, bf16[1,64,640]{2,1,0:T(8,128)(2,1)S(1)}, u32[]{:S(2)}, u32[]{:S(2)}) collective-permute-start(bf16[1,64,640]{2,1,0:T(8,128)(2,1)S(1)} %get-tuple-element.61), channel_id=1, source_target_pairs={{0,7},{1,0},{2,1},{3,2},{4,3},{5,4},{6,5},{7,6},{8,15},{9,8},{10,9... | collective-permute-start | bytes 245768 | tf_op jit(solution)/shard_map/ppermute | solution.py:146
  43.9 2.6 %collective-permute-done.5 = bf16[2,64,640]{2,1,0:T(8,128)(2,1)S(1)} collective-permute-done((bf16[2,64,640]{2,1,0:T(8,128)(2,1)S(1)}, bf16[2,64,640]{2,1,0:T(8,128)(2,1)S(1)}, u32[]{:S(2)}, u32[]{:S(2)}) %collective-permute-start.5) | collective-permute-done | bytes 163872 | tf_op jit(solution)/shard_map/ppermute | solution.py:146
  46.6 0.6 slice_bitcast_fusion.2
  47.2 0.6 slice_bitcast_fusion.1.refs_6_
  47.8 5.0 %collective-permute-done.6 = bf16[1,64,640]{2,1,0:T(8,128)(2,1)S(1)} collective-permute-done((bf16[1,64,640]{2,1,0:T(8,128)(2,1)S(1)}, bf16[1,64,640]{2,1,0:T(8,128)(2,1)S(1)}, u32[]{:S(2)}, u32[]{:S(2)}) %collective-permute-start.6) | collective-permute-done | bytes 81952 | tf_op jit(solution)/shard_map/ppermute | solution.py:146
  52.9 0.6 copy-done.12
  53.5 1.2 gather_window.1
  54.7 18.7 %all-to-all-done = bf16[32,112,640]{2,1,0:T(8,128)(2,1)} async-done(((bf16[32,112,640]{2,1,0:T(8,128)(2,1)}), bf16[32,112,640]{2,1,0:T(8,128)(2,1)}, u32[]{:S(2)}, u32[]{:S(2)}) %all-to-all-start) | async-done | bytes 4587552 | tf_op jit(solution)/shard_map/all_to_all | solution.py:212
  73.4 6.7 %product.3 = (bf16[64,3584]{1,0:T(8,128)(2,1)}, bf16[64,3584]{1,0:T(8,128)(2,1)}, bf16[64,3584]{1,0:T(8,128)(2,1)}, bf16[64,3584]{1,0:T(8,128)(2,1)}, bf16[64,35...) custom-call(f32[224,640]{1,0:T(8,128)S(1)} %compare_convert_fusion.keep_ref, ...), custom_call_target="tpu_custom_call" | custom-call | flops 1000 | bytes 1000 | tf_op jit(solution)/shard_map/product/pallas_call | solution.py:71
  80.1 1.9 %collective-permute-start.14 = (bf16[64,3584]{1,0:T(8,128)(2,1)}, bf16[64,3584]{1,0:T(8,128)(2,1)}, u32[]{:S(2)}, u32[]{:S(2)}) collective-permute-start(bf16[64,3584]{1,0:T(8,128)(2,1)} %get-tuple-element.42), channel_id=1, source_target_pairs={{0,1},{1,2},{2,3},{3,4},{4,5},{5,6},{6,7},{7,0},{8,9},{9,10},{10,1... | collective-permute-start | bytes 1376264 | tf_op jit(solution)/shard_map/ppermute | solution.py:146
  82.5 0.9 convolution_bitcast_fusion.1
  83.5 3.9 %all-to-all-start.1 = ((bf16[32,48,640]{2,1,0:T(8,128)(2,1)}), bf16[32,48,640]{2,1,0:T(8,128)(2,1)S(1)}, u32[]{:S(2)}, u32[]{:S(2)}) async-start(bf16[32,48,640]{2,1,0:T(8,128)(2,1)} %get-tuple-element.31), calls=%async_computation.1 | async-start | bytes 3932160 | tf_op jit(solution)/shard_map/all_to_all | solution.py:212
  87.5 4.2 %collective-permute-start.18 = (bf16[64,3584]{1,0:T(8,128)(2,1)}, bf16[64,3584]{1,0:T(8,128)(2,1)S(1)}, u32[]{:S(2)}, u32[]{:S(2)}) collective-permute-start(bf16[64,3584]{1,0:T(8,128)(2,1)} %get-tuple-element.46), channel_id=1, source_target_pairs={{0,7},{1,0},{2,1},{3,2},{4,3},{5,4},{6,5},{7,6},{8,15},{9,8},{10,9... | collective-permute-start | bytes 1376264 | tf_op jit(solution)/shard_map/ppermute | solution.py:146
  91.7 4.9 %collective-permute-done.14 = bf16[64,3584]{1,0:T(8,128)(2,1)} collective-permute-done((bf16[64,3584]{1,0:T(8,128)(2,1)}, bf16[64,3584]{1,0:T(8,128)(2,1)}, u32[]{:S(2)}, u32[]{:S(2)}) %collective-permute-start.14) | collective-permute-done | bytes 458784 | tf_op jit(solution)/shard_map/ppermute | solution.py:146
  96.6 1.3 add_convert_fusion.4
  98.0 3.8 %collective-permute-done.18 = bf16[64,3584]{1,0:T(8,128)(2,1)S(1)} collective-permute-done((bf16[64,3584]{1,0:T(8,128)(2,1)}, bf16[64,3584]{1,0:T(8,128)(2,1)S(1)}, u32[]{:S(2)}, u32[]{:S(2)}) %collective-permute-start.18) | collective-permute-done | bytes 458784 | tf_op jit(solution)/shard_map/ppermute | solution.py:146
  101.9 3.7 %collective-permute-start.19 = (bf16[64,3584]{1,0:T(8,128)(2,1)S(1)}, bf16[64,3584]{1,0:T(8,128)(2,1)S(1)}, u32[]{:S(2)}, u32[]{:S(2)}) collective-permute-start(bf16[64,3584]{1,0:T(8,128)(2,1)S(1)} %add_convert_fusion.1), channel_id=1, source_target_pairs={{0,7},{1,0},{2,1},{3,2},{4,3},{5,4},{6,5},{7,6},{8,15},{9,8},{10,9... | collective-permute-start | bytes 1376264 | tf_op jit(solution)/shard_map/ppermute | solution.py:146
  105.6 5.1 %collective-permute-done.15 = bf16[64,3584]{1,0:T(8,128)(2,1)S(1)} collective-permute-done((bf16[64,3584]{1,0:T(8,128)(2,1)S(1)}, bf16[64,3584]{1,0:T(8,128)(2,1)S(1)}, u32[]{:S(2)}, u32[]{:S(2)}) %collective-permute-start.15) | collective-permute-done | bytes 458784 | tf_op jit(solution)/shard_map/ppermute | solution.py:146
  110.7 0.9 add_convert_fusion.3
  111.5 2.9 %collective-permute-done.19 = bf16[64,3584]{1,0:T(8,128)(2,1)S(1)} collective-permute-done((bf16[64,3584]{1,0:T(8,128)(2,1)S(1)}, bf16[64,3584]{1,0:T(8,128)(2,1)S(1)}, u32[]{:S(2)}, u32[]{:S(2)}) %collective-permute-start.19) | collective-permute-done | bytes 458784 | tf_op jit(solution)/shard_map/ppermute | solution.py:146
  114.6 2.1 %product.2 = (bf16[64,1536]{1,0:T(8,128)(2,1)S(1)}, bf16[64,1536]{1,0:T(8,128)(2,1)S(1)}, bf16[64,1536]{1,0:T(8,128)(2,1)S(1)}, bf16[64,1536]{1,0:T(8,128)(2,1)S...) custom-call(f32[96,640]{1,0:T(8,128)S(1)} %compare_convert_fusion.1., ...), custom_call_target="tpu_custom_call" | custom-call | flops 1000 | bytes 1000 | tf_op jit(solution)/shard_map/product/pallas_call | solution.py:71
  116.7 3.8 %collective-permute-start.7 = (bf16[64,1536]{1,0:T(8,128)(2,1)S(1)}, bf16[64,1536]{1,0:T(8,128)(2,1)S(1)}, u32[]{:S(2)}, u32[]{:S(2)}) collective-permute-start(bf16[64,1536]{1,0:T(8,128)(2,1)S(1)} %get-tuple-element.33), channel_id=1, source_target_pairs={{0,7},{1,0},{2,1},{3,2},{4,3},{5,4},{6,5},{7,6},{8,15},{9,8},{10,9... | collective-permute-start | bytes 589832 | tf_op jit(solution)/shard_map/ppermute | solution.py:146
  120.5 3.1 %collective-permute-done.16 = bf16[64,3584]{1,0:T(8,128)(2,1)} collective-permute-done((bf16[64,3584]{1,0:T(8,128)(2,1)}, bf16[64,3584]{1,0:T(8,128)(2,1)}, u32[]{:S(2)}, u32[]{:S(2)}) %collective-permute-start.16) | collective-permute-done | bytes 458784 | tf_op jit(solution)/shard_map/ppermute | solution.py:146
  123.6 1.1 add_convert_fusion.2
  125.0 3.2 %collective-permute-start.20 = (bf16[64,3584]{1,0:T(8,128)(2,1)S(1)}, bf16[64,3584]{1,0:T(8,128)(2,1)S(1)}, u32[]{:S(2)}, u32[]{:S(2)}) collective-permute-start(bf16[64,3584]{1,0:T(8,128)(2,1)S(1)} %add_convert_fusion), channel_id=1, source_target_pairs={{0,7},{1,0},{2,1},{3,2},{4,3},{5,4},{6,5},{7,6},{8,15},{9,8},{10,9... | collective-permute-start | bytes 1376264 | tf_op jit(solution)/shard_map/ppermute | solution.py:146
  128.2 2.0 %collective-permute-start.8 = (bf16[64,1536]{1,0:T(8,128)(2,1)S(1)}, bf16[64,1536]{1,0:T(8,128)(2,1)S(1)}, u32[]{:S(2)}, u32[]{:S(2)}) collective-permute-start(bf16[64,1536]{1,0:T(8,128)(2,1)S(1)} %add_convert_fusion.9), channel_id=1, source_target_pairs={{0,7},{1,0},{2,1},{3,2},{4,3},{5,4},{6,5},{7,6},{8,15},{9,8},{10,9... | collective-permute-start | bytes 589832 | tf_op jit(solution)/shard_map/ppermute | solution.py:146
  130.3 9.7 %collective-permute-done.11 = bf16[64,1536]{1,0:T(8,128)(2,1)S(1)} collective-permute-done((bf16[64,1536]{1,0:T(8,128)(2,1)S(1)}, bf16[64,1536]{1,0:T(8,128)(2,1)S(1)}, u32[]{:S(2)}, u32[]{:S(2)}) %collective-permute-start.11) | collective-permute-done | bytes 196640 | tf_op jit(solution)/shard_map/ppermute | solution.py:146
  140.1 3.3 %collective-permute-start.9 = (bf16[64,1536]{1,0:T(8,128)(2,1)S(1)}, bf16[64,1536]{1,0:T(8,128)(2,1)S(1)}, u32[]{:S(2)}, u32[]{:S(2)}) collective-permute-start(bf16[64,1536]{1,0:T(8,128)(2,1)S(1)} %add_convert_fusion.8), channel_id=1, source_target_pairs={{0,7},{1,0},{2,1},{3,2},{4,3},{5,4},{6,5},{7,6},{8,15},{9,8},{10,9... | collective-permute-start | bytes 589832 | tf_op jit(solution)/shard_map/ppermute | solution.py:146
  143.4 4.4 %collective-permute-done.12 = bf16[64,1536]{1,0:T(8,128)(2,1)S(1)} collective-permute-done((bf16[64,1536]{1,0:T(8,128)(2,1)S(1)}, bf16[64,1536]{1,0:T(8,128)(2,1)S(1)}, u32[]{:S(2)}, u32[]{:S(2)}) %collective-permute-start.12) | collective-permute-done | bytes 196640 | tf_op jit(solution)/shard_map/ppermute | solution.py:146
  148.0 0.6 collective-permute-done.9
  148.6 3.0 %collective-permute-start.10 = (bf16[64,1536]{1,0:T(8,128)(2,1)S(1)}, bf16[64,1536]{1,0:T(8,128)(2,1)S(1)}, u32[]{:S(2)}, u32[]{:S(2)}) collective-permute-start(bf16[64,1536]{1,0:T(8,128)(2,1)S(1)} %add_convert_fusion.7), channel_id=1, source_target_pairs={{0,7},{1,0},{2,1},{3,2},{4,3},{5,4},{6,5},{7,6},{8,15},{9,8},{10,9... | collective-permute-start | bytes 589832 | tf_op jit(solution)/shard_map/ppermute | solution.py:146
  151.8 2.4 %begin.1.refs_0_ = f32[64,5120]{1,0:T(8,128)S(1)} custom-call(bf16[64,3584]{1,0:T(8,128)(2,1)S(1)} %copy-done.4, bf16[64,3584]{1,0:T(8,128)(2,1)S(1)} %collective-permute-done.17.up, bf16[64,3584]{1,0:T(8,128)(2,1)S(1)} %collective-permute-done.20.down, bf16[896,1280]{1,0:T(8,128)(2,1)S(1)} %copy-done.1, bf16[64,5120]{1,0:T(8,128)(2,1)S(1)} %copy-done.3), custom_call_target="tpu_custom_call" | custom-call | flops 1000 | bytes 1000 | tf_op jit(solution)/shard_map/begin/pallas_call | solution.py:104
  154.2 0.7 collective-permute-done.13.down
  154.9 3.0 %finish.1 = f32[64,5120]{1,0:T(8,128)} custom-call(bf16[64,1536]{1,0:T(8,128)(2,1)S(1)} %get-tuple-element.32.own, bf16[64,1536]{1,0:T(8,128)(2,1)S(1)} %collective-permute-done.10.up, bf16[64,1536]{1,0:T(8,128)(2,1)S(1)} %collective-permute-done.13.down, bf16[384,1280]{1,0:T(8,128)(2,1)S(1)} %copy-done.2, f32[64,5120]{1,0:T(8,128)S(1)} %begin.1.refs_0_, ...), custom_call_target="tpu_custom_call" | custom-call | flops 1000 | bytes 1000 | tf_op jit(solution)/shard_map/finish/pallas_call | solution.py:130
  (71 shorter events, 2.4 us)
Async XLA Ops:
  0.0 82.0 %copy-start = (f32[150]{0:T(256)S(1)}, f32[150]{0:T(256)}, u32[]{:S(2)}) copy-start(f32[150]{0:T(256)} %param.12) | copy-start | bytes 1804
  4.9 7.8 %copy-start.6 = (bf16[64,5120]{1,0:T(8,128)(2,1)S(1)}, bf16[64,5120]{1,0:T(8,128)(2,1)}, u32[]{:S(2)}) copy-start(bf16[64,5120]{1,0:T(8,128)(2,1)} %param.7) | copy-start | bytes 1966084
  4.9 68.5 %all-to-all-start = ((bf16[32,112,640]{2,1,0:T(8,128)(2,1)}), bf16[32,112,640]{2,1,0:T(8,128)(2,1)}, u32[]{:S(2)}, u32[]{:S(2)}) async-start(bf16[32,112,640]{2,1,0:T(8,128)(2,1)} %slice.67), calls=%async_computation | async-start | bytes 9175040 | tf_op jit(solution)/shard_map/all_to_all | solution.py:212
  13.4 14.7 %collective-permute-start = (bf16[3,64,640]{2,1,0:T(8,128)(2,1)S(1)}, bf16[3,64,640]{2,1,0:T(8,128)(2,1)S(1)}, u32[]{:S(2)}, u32[]{:S(2)}) collective-permute-start(bf16[3,64,640]{2,1,0:T(8,128)(2,1)S(1)} %pad_maximum_fusion.1), channel_id=1, source_target_pairs={{0,7},{1,0},{2,1},{3,2},{4,3},{5,4},{6,5},{7,6},{8,15},{9,8},{10,9... | collective-permute-start | bytes 737288 | tf_op jit(solution)/shard_map/ppermute | solution.py:146
  19.4 12.0 %collective-permute-start.3 = (bf16[4,64,640]{2,1,0:T(8,128)(2,1)S(1)}, bf16[4,64,640]{2,1,0:T(8,128)(2,1)S(1)}, u32[]{:S(2)}, u32[]{:S(2)}) collective-permute-start(bf16[4,64,640]{2,1,0:T(8,128)(2,1)S(1)} %pad_maximum_fusion), channel_id=1, source_target_pairs={{0,1},{1,2},{2,3},{3,4},{4,5},{5,6},{6,7},{7,0},{8,9},{9,10},{10,1... | collective-permute-start | bytes 983048 | tf_op jit(solution)/shard_map/ppermute | solution.py:146
  23.6 4.2 %copy-start.13 = (s32[64,2]{0,1:T(2,128)S(1)}, s32[64,2]{0,1:T(2,128)}, u32[]{:S(2)}) copy-start(s32[64,2]{0,1:T(2,128)} %param.11) | copy-start | bytes 1540
  28.2 11.9 %collective-permute-start.1 = (bf16[2,64,640]{2,1,0:T(8,128)(2,1)S(1)}, bf16[2,64,640]{2,1,0:T(8,128)(2,1)S(1)}, u32[]{:S(2)}, u32[]{:S(2)}) collective-permute-start(bf16[2,64,640]{2,1,0:T(8,128)(2,1)S(1)} %slice.57), channel_id=1, source_target_pairs={{0,7},{1,0},{2,1},{3,2},{4,3},{5,4},{6,5},{7,6},{8,15},{9,8},{10,9... | collective-permute-start | bytes 491528 | tf_op jit(solution)/shard_map/ppermute | solution.py:146
  31.5 8.5 %collective-permute-start.4 = (bf16[3,64,640]{2,1,0:T(8,128)(2,1)S(1)}, bf16[3,64,640]{2,1,0:T(8,128)(2,1)S(1)}, u32[]{:S(2)}, u32[]{:S(2)}) collective-permute-start(bf16[3,64,640]{2,1,0:T(8,128)(2,1)S(1)} %slice.60), channel_id=1, source_target_pairs={{0,1},{1,2},{2,3},{3,4},{4,5},{5,6},{6,7},{7,0},{8,9},{9,10},{10,1... | collective-permute-start | bytes 737288 | tf_op jit(solution)/shard_map/ppermute | solution.py:146
  40.0 6.6 %collective-permute-start.5 = (bf16[2,64,640]{2,1,0:T(8,128)(2,1)S(1)}, bf16[2,64,640]{2,1,0:T(8,128)(2,1)S(1)}, u32[]{:S(2)}, u32[]{:S(2)}) collective-permute-start(bf16[2,64,640]{2,1,0:T(8,128)(2,1)S(1)} %slice.61), channel_id=1, source_target_pairs={{0,1},{1,2},{2,3},{3,4},{4,5},{5,6},{6,7},{7,0},{8,9},{9,10},{10,1... | collective-permute-start | bytes 491528 | tf_op jit(solution)/shard_map/ppermute | solution.py:146
  40.7 7.1 %collective-permute-start.2 = (bf16[1,64,640]{2,1,0:T(8,128)(2,1)S(1)}, bf16[1,64,640]{2,1,0:T(8,128)(2,1)S(1)}, u32[]{:S(2)}, u32[]{:S(2)}) collective-permute-start(bf16[1,64,640]{2,1,0:T(8,128)(2,1)S(1)} %get-tuple-element.61), channel_id=1, source_target_pairs={{0,7},{1,0},{2,1},{3,2},{4,3},{5,4},{6,5},{7,6},{8,15},{9,8},{10,9... | collective-permute-start | bytes 245768 | tf_op jit(solution)/shard_map/ppermute | solution.py:146
  47.2 5.7 %collective-permute-start.6 = (bf16[1,64,640]{2,1,0:T(8,128)(2,1)S(1)}, bf16[1,64,640]{2,1,0:T(8,128)(2,1)S(1)}, u32[]{:S(2)}, u32[]{:S(2)}) collective-permute-start(bf16[1,64,640]{2,1,0:T(8,128)(2,1)S(1)} %get-tuple-element.60), channel_id=1, source_target_pairs={{0,1},{1,2},{2,3},{3,4},{4,5},{5,6},{6,7},{7,0},{8,9},{9,10},{10,1... | collective-permute-start | bytes 245768 | tf_op jit(solution)/shard_map/ppermute | solution.py:146
  47.8 5.0 %copy-start.11 = (bf16[1,64,640]{2,1,0:T(8,128)(2,1)}, bf16[1,64,640]{2,1,0:T(8,128)(2,1)S(1)}, u32[]{:S(2)}) copy-start(bf16[1,64,640]{2,1,0:T(8,128)(2,1)S(1)} %collective-permute-done.2) | copy-start | bytes 245764
  52.9 0.6 copy-start.12
  80.1 16.5 %collective-permute-start.14 = (bf16[64,3584]{1,0:T(8,128)(2,1)}, bf16[64,3584]{1,0:T(8,128)(2,1)}, u32[]{:S(2)}, u32[]{:S(2)}) collective-permute-start(bf16[64,3584]{1,0:T(8,128)(2,1)} %get-tuple-element.42), channel_id=1, source_target_pairs={{0,1},{1,2},{2,3},{3,4},{4,5},{5,6},{6,7},{7,0},{8,9},{9,10},{10,1... | collective-permute-start | bytes 1376264 | tf_op jit(solution)/shard_map/ppermute | solution.py:146
  83.5 18.3 %copy-start.10 = (bf16[64,3584]{1,0:T(8,128)(2,1)S(1)}, bf16[64,3584]{1,0:T(8,128)(2,1)}, u32[]{:S(2)}) copy-start(bf16[64,3584]{1,0:T(8,128)(2,1)} %get-tuple-element.47) | copy-start | bytes 1376260
  83.5 31.1 %all-to-all-start.1 = ((bf16[32,48,640]{2,1,0:T(8,128)(2,1)}), bf16[32,48,640]{2,1,0:T(8,128)(2,1)S(1)}, u32[]{:S(2)}, u32[]{:S(2)}) async-start(bf16[32,48,640]{2,1,0:T(8,128)(2,1)} %get-tuple-element.31), calls=%async_computation.1 | async-start | bytes 3932160 | tf_op jit(solution)/shard_map/all_to_all | solution.py:212
  87.5 23.2 %copy-start.9 = (bf16[64,3584]{1,0:T(8,128)(2,1)S(1)}, bf16[64,3584]{1,0:T(8,128)(2,1)}, u32[]{:S(2)}) copy-start(bf16[64,3584]{1,0:T(8,128)(2,1)} %get-tuple-element.44) | copy-start | bytes 1376260
  87.5 27.0 %copy-start.8 = (bf16[64,3584]{1,0:T(8,128)(2,1)S(1)}, bf16[64,3584]{1,0:T(8,128)(2,1)}, u32[]{:S(2)}) copy-start(bf16[64,3584]{1,0:T(8,128)(2,1)} %get-tuple-element.48) | copy-start | bytes 1376260
  87.5 14.3 %collective-permute-start.18 = (bf16[64,3584]{1,0:T(8,128)(2,1)}, bf16[64,3584]{1,0:T(8,128)(2,1)S(1)}, u32[]{:S(2)}, u32[]{:S(2)}) collective-permute-start(bf16[64,3584]{1,0:T(8,128)(2,1)} %get-tuple-element.46), channel_id=1, source_target_pairs={{0,7},{1,0},{2,1},{3,2},{4,3},{5,4},{6,5},{7,6},{8,15},{9,8},{10,9... | collective-permute-start | bytes 1376264 | tf_op jit(solution)/shard_map/ppermute | solution.py:146
  97.9 12.8 %collective-permute-start.15 = (bf16[64,3584]{1,0:T(8,128)(2,1)S(1)}, bf16[64,3584]{1,0:T(8,128)(2,1)S(1)}, u32[]{:S(2)}, u32[]{:S(2)}) collective-permute-start(bf16[64,3584]{1,0:T(8,128)(2,1)S(1)} %add_convert_fusion.4), channel_id=1, source_target_pairs={{0,1},{1,2},{2,3},{3,4},{4,5},{5,6},{6,7},{7,0},{8,9},{9,10},{10,1... | collective-permute-start | bytes 1376264 | tf_op jit(solution)/shard_map/ppermute | solution.py:146
  101.9 12.6 %collective-permute-start.19 = (bf16[64,3584]{1,0:T(8,128)(2,1)S(1)}, bf16[64,3584]{1,0:T(8,128)(2,1)S(1)}, u32[]{:S(2)}, u32[]{:S(2)}) collective-permute-start(bf16[64,3584]{1,0:T(8,128)(2,1)S(1)} %add_convert_fusion.1), channel_id=1, source_target_pairs={{0,7},{1,0},{2,1},{3,2},{4,3},{5,4},{6,5},{7,6},{8,15},{9,8},{10,9... | collective-permute-start | bytes 1376264 | tf_op jit(solution)/shard_map/ppermute | solution.py:146
  111.5 12.1 %collective-permute-start.16 = (bf16[64,3584]{1,0:T(8,128)(2,1)}, bf16[64,3584]{1,0:T(8,128)(2,1)}, u32[]{:S(2)}, u32[]{:S(2)}) collective-permute-start(bf16[64,3584]{1,0:T(8,128)(2,1)} %add_convert_fusion.3), channel_id=1, source_target_pairs={{0,1},{1,2},{2,3},{3,4},{4,5},{5,6},{6,7},{7,0},{8,9},{9,10},{10,1... | collective-permute-start | bytes 1376264 | tf_op jit(solution)/shard_map/ppermute | solution.py:146
  114.6 9.0 %copy-start.7 = (bf16[64,3584]{1,0:T(8,128)(2,1)S(1)}, bf16[64,3584]{1,0:T(8,128)(2,1)}, u32[]{:S(2)}) copy-start(bf16[64,3584]{1,0:T(8,128)(2,1)} %get-tuple-element.45) | copy-start | bytes 1376260
  116.7 35.0 %copy-start.1 = (bf16[896,1280]{1,0:T(8,128)(2,1)S(1)}, bf16[896,1280]{1,0:T(8,128)(2,1)}, u32[]{:S(2)}) copy-start(bf16[896,1280]{1,0:T(8,128)(2,1)} %get-tuple-element.50.place) | copy-start | bytes 6881284
  116.7 35.0 %copy-start.3 = (bf16[64,5120]{1,0:T(8,128)(2,1)S(1)}, bf16[64,5120]{1,0:T(8,128)(2,1)}, u32[]{:S(2)}) copy-start(bf16[64,5120]{1,0:T(8,128)(2,1)} %other_ref.1) | copy-start | bytes 1966084
  116.7 35.0 %copy-start.4 = (bf16[64,3584]{1,0:T(8,128)(2,1)S(1)}, bf16[64,3584]{1,0:T(8,128)(2,1)}, u32[]{:S(2)}) copy-start(bf16[64,3584]{1,0:T(8,128)(2,1)} %get-tuple-element.41.own) | copy-start | bytes 1376260
  116.7 11.5 %collective-permute-start.7 = (bf16[64,1536]{1,0:T(8,128)(2,1)S(1)}, bf16[64,1536]{1,0:T(8,128)(2,1)S(1)}, u32[]{:S(2)}, u32[]{:S(2)}) collective-permute-start(bf16[64,1536]{1,0:T(8,128)(2,1)S(1)} %get-tuple-element.33), channel_id=1, source_target_pairs={{0,7},{1,0},{2,1},{3,2},{4,3},{5,4},{6,5},{7,6},{8,15},{9,8},{10,9... | collective-permute-start | bytes 589832 | tf_op jit(solution)/shard_map/ppermute | solution.py:146
  124.8 26.9 %collective-permute-start.17 = (bf16[64,3584]{1,0:T(8,128)(2,1)S(1)}, bf16[64,3584]{1,0:T(8,128)(2,1)S(1)}, u32[]{:S(2)}, u32[]{:S(2)}) collective-permute-start(bf16[64,3584]{1,0:T(8,128)(2,1)S(1)} %add_convert_fusion.2), channel_id=1, source_target_pairs={{0,1},{1,2},{2,3},{3,4},{4,5},{5,6},{6,7},{7,0},{8,9},{9,10},{10,1... | collective-permute-start | bytes 1376264 | tf_op jit(solution)/shard_map/ppermute | solution.py:146
  124.9 15.0 %collective-permute-start.11 = (bf16[64,1536]{1,0:T(8,128)(2,1)S(1)}, bf16[64,1536]{1,0:T(8,128)(2,1)S(1)}, u32[]{:S(2)}, u32[]{:S(2)}) collective-permute-start(bf16[64,1536]{1,0:T(8,128)(2,1)S(1)} %get-tuple-element.37), channel_id=1, source_target_pairs={{0,1},{1,2},{2,3},{3,4},{4,5},{5,6},{6,7},{7,0},{8,9},{9,10},{10,1... | collective-permute-start | bytes 589832 | tf_op jit(solution)/shard_map/ppermute | solution.py:146
  125.0 26.8 %collective-permute-start.20 = (bf16[64,3584]{1,0:T(8,128)(2,1)S(1)}, bf16[64,3584]{1,0:T(8,128)(2,1)S(1)}, u32[]{:S(2)}, u32[]{:S(2)}) collective-permute-start(bf16[64,3584]{1,0:T(8,128)(2,1)S(1)} %add_convert_fusion), channel_id=1, source_target_pairs={{0,7},{1,0},{2,1},{3,2},{4,3},{5,4},{6,5},{7,6},{8,15},{9,8},{10,9... | collective-permute-start | bytes 1376264 | tf_op jit(solution)/shard_map/ppermute | solution.py:146
  128.2 11.8 %collective-permute-start.8 = (bf16[64,1536]{1,0:T(8,128)(2,1)S(1)}, bf16[64,1536]{1,0:T(8,128)(2,1)S(1)}, u32[]{:S(2)}, u32[]{:S(2)}) collective-permute-start(bf16[64,1536]{1,0:T(8,128)(2,1)S(1)} %add_convert_fusion.9), channel_id=1, source_target_pairs={{0,7},{1,0},{2,1},{3,2},{4,3},{5,4},{6,5},{7,6},{8,15},{9,8},{10,9... | collective-permute-start | bytes 589832 | tf_op jit(solution)/shard_map/ppermute | solution.py:146
  140.0 7.9 %collective-permute-start.12 = (bf16[64,1536]{1,0:T(8,128)(2,1)S(1)}, bf16[64,1536]{1,0:T(8,128)(2,1)S(1)}, u32[]{:S(2)}, u32[]{:S(2)}) collective-permute-start(bf16[64,1536]{1,0:T(8,128)(2,1)S(1)} %add_convert_fusion.6), channel_id=1, source_target_pairs={{0,1},{1,2},{2,3},{3,4},{4,5},{5,6},{6,7},{7,0},{8,9},{9,10},{10,1... | collective-permute-start | bytes 589832 | tf_op jit(solution)/shard_map/ppermute | solution.py:146
  140.1 8.4 %collective-permute-start.9 = (bf16[64,1536]{1,0:T(8,128)(2,1)S(1)}, bf16[64,1536]{1,0:T(8,128)(2,1)S(1)}, u32[]{:S(2)}, u32[]{:S(2)}) collective-permute-start(bf16[64,1536]{1,0:T(8,128)(2,1)S(1)} %add_convert_fusion.8), channel_id=1, source_target_pairs={{0,7},{1,0},{2,1},{3,2},{4,3},{5,4},{6,5},{7,6},{8,15},{9,8},{10,9... | collective-permute-start | bytes 589832 | tf_op jit(solution)/shard_map/ppermute | solution.py:146
  147.9 7.0 %collective-permute-start.13 = (bf16[64,1536]{1,0:T(8,128)(2,1)S(1)}, bf16[64,1536]{1,0:T(8,128)(2,1)S(1)}, u32[]{:S(2)}, u32[]{:S(2)}) collective-permute-start(bf16[64,1536]{1,0:T(8,128)(2,1)S(1)} %add_convert_fusion.5), channel_id=1, source_target_pairs={{0,1},{1,2},{2,3},{3,4},{4,5},{5,6},{6,7},{7,0},{8,9},{9,10},{10,1... | collective-permute-start | bytes 589832 | tf_op jit(solution)/shard_map/ppermute | solution.py:146
  148.6 6.2 %collective-permute-start.10 = (bf16[64,1536]{1,0:T(8,128)(2,1)S(1)}, bf16[64,1536]{1,0:T(8,128)(2,1)S(1)}, u32[]{:S(2)}, u32[]{:S(2)}) collective-permute-start(bf16[64,1536]{1,0:T(8,128)(2,1)S(1)} %add_convert_fusion.7), channel_id=1, source_target_pairs={{0,7},{1,0},{2,1},{3,2},{4,3},{5,4},{6,5},{7,6},{8,15},{9,8},{10,9... | collective-permute-start | bytes 589832 | tf_op jit(solution)/shard_map/ppermute | solution.py:146
  151.8 3.1 %copy-start.2 = (bf16[384,1280]{1,0:T(8,128)(2,1)S(1)}, bf16[384,1280]{1,0:T(8,128)(2,1)}, u32[]{:S(2)}) copy-start(bf16[384,1280]{1,0:T(8,128)(2,1)} %get-tuple-element.40.place) | copy-start | bytes 2949124
  151.8 3.1 %copy-start.5 = (f32[5120]{0:T(1024)S(1)}, f32[5120]{0:T(1024)}, u32[]{:S(2)}) copy-start(f32[5120]{0:T(1024)} %param.13) | copy-start | bytes 61444

commit v5 on v4

--- a/solution.py
+++ b/solution.py
@@ -11,7 +11,7 @@
 UNIT = 16
 COST = pl.CostEstimate(flops=1000, bytes_accessed=1000, transcendentals=0)
 CHUNKS = (112, 48)
-STEPS = (1792, 768)
+STEPS = (1792, 1536)
 SPAN = 1280
 
 

time: 159 us -> 159 us (level)
  transfers between devices with their start and end apart: 23 -> 23, of which waited for: 13 -> 13; matrix products, arithmetic and copies ran while one was open for 11% -> 11% of each run, Pallas kernels for 4% -> 3%
where the time goes in v5:
time: 159 us; the launch traced here: 158 us
  waiting for transfers between devices  69.2 us (44%)
  starting transfers between devices  49.9 us (31%)
  Pallas kernels  14.8 us (9%)
  local copies, waits for them, and re-layouts  13.1 us (8%)
  other arithmetic  7.31 us (5%)
  matrix products  3.09 us (2%)
    ppermute x21, waiting for transfers between devices, shift(): lax.ppermute(values, 'ka', [(i, (i + step) % count) for i in range(count)])  50.6 us
    ppermute x21, starting transfers between devices, shift(): lax.ppermute(values, 'ka', [(i, (i + step) % count) for i in range(count)])  38.2 us
    all_to_all x2, waiting for transfers between devices, exchange(): lax.all_to_all(sent, 'ta', split_axis=0, concat_axis=0, tiled=True)  18.7 us
    all_to_all x2, starting transfers between devices, exchange(): lax.all_to_all(sent, 'ta', split_axis=0, concat_axis=0, tiled=True)  11.6 us
    pallas_call x2, Pallas kernels, product(): pl.pallas_call(functools.partial(product_kernel, rings), grid=(count // s...  8.23 us
    slice x2, local copies, waits for them, and re-layouts, shards(): dealt[:, first:first + size]  7.95 us
    convert_element_type x6, other arithmetic, reduced(): (long.astype(jnp.float32) + mine.astype(jnp.float32)).astype(jnp.bfloat16)  3.44 us
  transfers between devices with their start and end apart: 23, of which 13 were waited for; matrix products, arithmetic and copies ran while one was open for 11% of the time, Pallas kernels for 3%

profile of v5, /device:TPU:8, one launch (start us, length us, event | category | flops | bytes accessed | tf_op | source)
XLA Modules:
  0.0 157.9 jit_solution(4037775744780668995)
XLA Ops:
  0.0 4.9 %slice.67 = bf16[32,112,640]{2,1,0:T(8,128)(2,1)} slice(bf16[32,160,640]{2,1,0:T(8,128)(2,1)} %bitcast.47), slice={[0:32], [0:112], [0:640]} | slice | bytes 9175040 | tf_op jit(solution)/shard_map/slice | solution.py:196
  4.9 7.7 %all-to-all-start = ((bf16[32,112,640]{2,1,0:T(8,128)(2,1)}), bf16[32,112,640]{2,1,0:T(8,128)(2,1)}, u32[]{:S(2)}, u32[]{:S(2)}) async-start(bf16[32,112,640]{2,1,0:T(8,128)(2,1)} %slice.67), calls=%async_computation | async-start | bytes 9175040 | tf_op jit(solution)/shard_map/all_to_all | solution.py:212
  12.7 0.7 dynamic-slice_bitcast_fusion.3
  13.4 5.9 %collective-permute-start = (bf16[3,64,640]{2,1,0:T(8,128)(2,1)S(1)}, bf16[3,64,640]{2,1,0:T(8,128)(2,1)S(1)}, u32[]{:S(2)}, u32[]{:S(2)}) collective-permute-start(bf16[3,64,640]{2,1,0:T(8,128)(2,1)S(1)} %pad_maximum_fusion.1), channel_id=1, source_target_pairs={{0,7},{1,0},{2,1},{3,2},{4,3},{5,4},{6,5},{7,6},{8,15},{9,8},{10,9... | collective-permute-start | bytes 737288 | tf_op jit(solution)/shard_map/ppermute | solution.py:146
  19.6 0.9 fusion.3
  20.5 1.3 fusion.1.refs_10_
  21.8 1.8 %fusion.refs_9_ = bf16[896,1280]{1,0:T(8,128)(2,1)} fusion(s32[896]{0:T(1024)S(1)} %fusion.14), kind=kLoop, calls=%fused_computation.1 | loop fusion | flops 2293760 | bytes 2297344 | tf_op jit(solution)/shard_map/convert_element_type | solution.py:204
  23.6 1.1 convolution_reduce_fusion
  24.7 3.1 %slice.66.refs_8_ = bf16[32,48,640]{2,1,0:T(8,128)(2,1)} slice(bf16[32,160,640]{2,1,0:T(8,128)(2,1)} %bitcast.48), slice={[0:32], [112:160], [0:640]} | slice | bytes 3932160 | tf_op jit(solution)/shard_map/slice | solution.py:196
  28.2 3.3 %collective-permute-start.1 = (bf16[2,64,640]{2,1,0:T(8,128)(2,1)S(1)}, bf16[2,64,640]{2,1,0:T(8,128)(2,1)S(1)}, u32[]{:S(2)}, u32[]{:S(2)}) collective-permute-start(bf16[2,64,640]{2,1,0:T(8,128)(2,1)S(1)} %slice.57), channel_id=1, source_target_pairs={{0,7},{1,0},{2,1},{3,2},{4,3},{5,4},{6,5},{7,6},{8,15},{9,8},{10,9... | collective-permute-start | bytes 491528 | tf_op jit(solution)/shard_map/ppermute | solution.py:146
  31.6 0.6 slice_bitcast_fusion.4.refs_1_
  32.2 0.6 slice_bitcast_fusion.refs_7_
  32.9 7.1 %collective-permute-done.4 = bf16[3,64,640]{2,1,0:T(8,128)(2,1)S(1)} collective-permute-done((bf16[3,64,640]{2,1,0:T(8,128)(2,1)S(1)}, bf16[3,64,640]{2,1,0:T(8,128)(2,1)S(1)}, u32[]{:S(2)}, u32[]{:S(2)}) %collective-permute-start.4) | collective-permute-done | bytes 245792 | tf_op jit(solution)/shard_map/ppermute | solution.py:146
  40.1 0.6 fusion.38
  40.7 3.2 %collective-permute-start.2 = (bf16[1,64,640]{2,1,0:T(8,128)(2,1)S(1)}, bf16[1,64,640]{2,1,0:T(8,128)(2,1)S(1)}, u32[]{:S(2)}, u32[]{:S(2)}) collective-permute-start(bf16[1,64,640]{2,1,0:T(8,128)(2,1)S(1)} %get-tuple-element.61), channel_id=1, source_target_pairs={{0,7},{1,0},{2,1},{3,2},{4,3},{5,4},{6,5},{7,6},{8,15},{9,8},{10,9... | collective-permute-start | bytes 245768 | tf_op jit(solution)/shard_map/ppermute | solution.py:146
  43.9 2.6 %collective-permute-done.5 = bf16[2,64,640]{2,1,0:T(8,128)(2,1)S(1)} collective-permute-done((bf16[2,64,640]{2,1,0:T(8,128)(2,1)S(1)}, bf16[2,64,640]{2,1,0:T(8,128)(2,1)S(1)}, u32[]{:S(2)}, u32[]{:S(2)}) %collective-permute-start.5) | collective-permute-done | bytes 163872 | tf_op jit(solution)/shard_map/ppermute | solution.py:146
  46.6 0.6 slice_bitcast_fusion.2
  47.2 0.6 slice_bitcast_fusion.1.refs_6_
  47.8 5.0 %collective-permute-done.6 = bf16[1,64,640]{2,1,0:T(8,128)(2,1)S(1)} collective-permute-done((bf16[1,64,640]{2,1,0:T(8,128)(2,1)S(1)}, bf16[1,64,640]{2,1,0:T(8,128)(2,1)S(1)}, u32[]{:S(2)}, u32[]{:S(2)}) %collective-permute-start.6) | collective-permute-done | bytes 81952 | tf_op jit(solution)/shard_map/ppermute | solution.py:146
  52.9 0.6 copy-done.12
  53.5 1.2 gather_window.1
  54.7 18.7 %all-to-all-done = bf16[32,112,640]{2,1,0:T(8,128)(2,1)} async-done(((bf16[32,112,640]{2,1,0:T(8,128)(2,1)}), bf16[32,112,640]{2,1,0:T(8,128)(2,1)}, u32[]{:S(2)}, u32[]{:S(2)}) %all-to-all-start) | async-done | bytes 4587552 | tf_op jit(solution)/shard_map/all_to_all | solution.py:212
  73.4 6.7 %product.3 = (bf16[64,3584]{1,0:T(8,128)(2,1)}, bf16[64,3584]{1,0:T(8,128)(2,1)}, bf16[64,3584]{1,0:T(8,128)(2,1)}, bf16[64,3584]{1,0:T(8,128)(2,1)}, bf16[64,35...) custom-call(f32[224,640]{1,0:T(8,128)S(1)} %compare_convert_fusion.keep_ref, ...), custom_call_target="tpu_custom_call" | custom-call | flops 1000 | bytes 1000 | tf_op jit(solution)/shard_map/product/pallas_call | solution.py:71
  80.1 1.9 %collective-permute-start.14 = (bf16[64,3584]{1,0:T(8,128)(2,1)}, bf16[64,3584]{1,0:T(8,128)(2,1)}, u32[]{:S(2)}, u32[]{:S(2)}) collective-permute-start(bf16[64,3584]{1,0:T(8,128)(2,1)} %get-tuple-element.42), channel_id=1, source_target_pairs={{0,1},{1,2},{2,3},{3,4},{4,5},{5,6},{6,7},{7,0},{8,9},{9,10},{10,1... | collective-permute-start | bytes 1376264 | tf_op jit(solution)/shard_map/ppermute | solution.py:146
  82.5 0.9 convolution_bitcast_fusion.1
  83.5 3.9 %all-to-all-start.1 = ((bf16[32,48,640]{2,1,0:T(8,128)(2,1)}), bf16[32,48,640]{2,1,0:T(8,128)(2,1)S(1)}, u32[]{:S(2)}, u32[]{:S(2)}) async-start(bf16[32,48,640]{2,1,0:T(8,128)(2,1)} %get-tuple-element.31), calls=%async_computation.1 | async-start | bytes 3932160 | tf_op jit(solution)/shard_map/all_to_all | solution.py:212
  87.5 4.2 %collective-permute-start.18 = (bf16[64,3584]{1,0:T(8,128)(2,1)}, bf16[64,3584]{1,0:T(8,128)(2,1)S(1)}, u32[]{:S(2)}, u32[]{:S(2)}) collective-permute-start(bf16[64,3584]{1,0:T(8,128)(2,1)} %get-tuple-element.46), channel_id=1, source_target_pairs={{0,7},{1,0},{2,1},{3,2},{4,3},{5,4},{6,5},{7,6},{8,15},{9,8},{10,9... | collective-permute-start | bytes 1376264 | tf_op jit(solution)/shard_map/ppermute | solution.py:146
  91.7 4.9 %collective-permute-done.14 = bf16[64,3584]{1,0:T(8,128)(2,1)} collective-permute-done((bf16[64,3584]{1,0:T(8,128)(2,1)}, bf16[64,3584]{1,0:T(8,128)(2,1)}, u32[]{:S(2)}, u32[]{:S(2)}) %collective-permute-start.14) | collective-permute-done | bytes 458784 | tf_op jit(solution)/shard_map/ppermute | solution.py:146
  96.6 1.3 add_convert_fusion.4
  98.0 3.8 %collective-permute-done.18 = bf16[64,3584]{1,0:T(8,128)(2,1)S(1)} collective-permute-done((bf16[64,3584]{1,0:T(8,128)(2,1)}, bf16[64,3584]{1,0:T(8,128)(2,1)S(1)}, u32[]{:S(2)}, u32[]{:S(2)}) %collective-permute-start.18) | collective-permute-done | bytes 458784 | tf_op jit(solution)/shard_map/ppermute | solution.py:146
  101.9 3.7 %collective-permute-start.19 = (bf16[64,3584]{1,0:T(8,128)(2,1)S(1)}, bf16[64,3584]{1,0:T(8,128)(2,1)S(1)}, u32[]{:S(2)}, u32[]{:S(2)}) collective-permute-start(bf16[64,3584]{1,0:T(8,128)(2,1)S(1)} %add_convert_fusion.1), channel_id=1, source_target_pairs={{0,7},{1,0},{2,1},{3,2},{4,3},{5,4},{6,5},{7,6},{8,15},{9,8},{10,9... | collective-permute-start | bytes 1376264 | tf_op jit(solution)/shard_map/ppermute | solution.py:146
  105.6 5.1 %collective-permute-done.15 = bf16[64,3584]{1,0:T(8,128)(2,1)S(1)} collective-permute-done((bf16[64,3584]{1,0:T(8,128)(2,1)S(1)}, bf16[64,3584]{1,0:T(8,128)(2,1)S(1)}, u32[]{:S(2)}, u32[]{:S(2)}) %collective-permute-start.15) | collective-permute-done | bytes 458784 | tf_op jit(solution)/shard_map/ppermute | solution.py:146
  110.7 0.9 add_convert_fusion.3
  111.5 2.9 %collective-permute-done.19 = bf16[64,3584]{1,0:T(8,128)(2,1)S(1)} collective-permute-done((bf16[64,3584]{1,0:T(8,128)(2,1)S(1)}, bf16[64,3584]{1,0:T(8,128)(2,1)S(1)}, u32[]{:S(2)}, u32[]{:S(2)}) %collective-permute-start.19) | collective-permute-done | bytes 458784 | tf_op jit(solution)/shard_map/ppermute | solution.py:146
  114.6 1.5 product.2
  116.1 3.8 %collective-permute-start.7 = (bf16[64,1536]{1,0:T(8,128)(2,1)S(1)}, bf16[64,1536]{1,0:T(8,128)(2,1)S(1)}, u32[]{:S(2)}, u32[]{:S(2)}) collective-permute-start(bf16[64,1536]{1,0:T(8,128)(2,1)S(1)} %get-tuple-element.33), channel_id=1, source_target_pairs={{0,7},{1,0},{2,1},{3,2},{4,3},{5,4},{6,5},{7,6},{8,15},{9,8},{10,9... | collective-permute-start | bytes 589832 | tf_op jit(solution)/shard_map/ppermute | solution.py:146
  119.9 3.7 %collective-permute-done.16 = bf16[64,3584]{1,0:T(8,128)(2,1)} collective-permute-done((bf16[64,3584]{1,0:T(8,128)(2,1)}, bf16[64,3584]{1,0:T(8,128)(2,1)}, u32[]{:S(2)}, u32[]{:S(2)}) %collective-permute-start.16) | collective-permute-done | bytes 458784 | tf_op jit(solution)/shard_map/ppermute | solution.py:146
  123.6 1.1 add_convert_fusion.2
  125.0 3.2 %collective-permute-start.20 = (bf16[64,3584]{1,0:T(8,128)(2,1)S(1)}, bf16[64,3584]{1,0:T(8,128)(2,1)S(1)}, u32[]{:S(2)}, u32[]{:S(2)}) collective-permute-start(bf16[64,3584]{1,0:T(8,128)(2,1)S(1)} %add_convert_fusion), channel_id=1, source_target_pairs={{0,7},{1,0},{2,1},{3,2},{4,3},{5,4},{6,5},{7,6},{8,15},{9,8},{10,9... | collective-permute-start | bytes 1376264 | tf_op jit(solution)/shard_map/ppermute | solution.py:146
  128.2 2.0 %collective-permute-start.8 = (bf16[64,1536]{1,0:T(8,128)(2,1)S(1)}, bf16[64,1536]{1,0:T(8,128)(2,1)S(1)}, u32[]{:S(2)}, u32[]{:S(2)}) collective-permute-start(bf16[64,1536]{1,0:T(8,128)(2,1)S(1)} %add_convert_fusion.9), channel_id=1, source_target_pairs={{0,7},{1,0},{2,1},{3,2},{4,3},{5,4},{6,5},{7,6},{8,15},{9,8},{10,9... | collective-permute-start | bytes 589832 | tf_op jit(solution)/shard_map/ppermute | solution.py:146
  130.3 9.7 %collective-permute-done.11 = bf16[64,1536]{1,0:T(8,128)(2,1)S(1)} collective-permute-done((bf16[64,1536]{1,0:T(8,128)(2,1)S(1)}, bf16[64,1536]{1,0:T(8,128)(2,1)S(1)}, u32[]{:S(2)}, u32[]{:S(2)}) %collective-permute-start.11) | collective-permute-done | bytes 196640 | tf_op jit(solution)/shard_map/ppermute | solution.py:146
  140.1 3.3 %collective-permute-start.9 = (bf16[64,1536]{1,0:T(8,128)(2,1)S(1)}, bf16[64,1536]{1,0:T(8,128)(2,1)S(1)}, u32[]{:S(2)}, u32[]{:S(2)}) collective-permute-start(bf16[64,1536]{1,0:T(8,128)(2,1)S(1)} %add_convert_fusion.8), channel_id=1, source_target_pairs={{0,7},{1,0},{2,1},{3,2},{4,3},{5,4},{6,5},{7,6},{8,15},{9,8},{10,9... | collective-permute-start | bytes 589832 | tf_op jit(solution)/shard_map/ppermute | solution.py:146
  143.4 4.4 %collective-permute-done.12 = bf16[64,1536]{1,0:T(8,128)(2,1)S(1)} collective-permute-done((bf16[64,1536]{1,0:T(8,128)(2,1)S(1)}, bf16[64,1536]{1,0:T(8,128)(2,1)S(1)}, u32[]{:S(2)}, u32[]{:S(2)}) %collective-permute-start.12) | collective-permute-done | bytes 196640 | tf_op jit(solution)/shard_map/ppermute | solution.py:146
  148.0 0.6 collective-permute-done.9
  148.6 3.0 %collective-permute-start.10 = (bf16[64,1536]{1,0:T(8,128)(2,1)S(1)}, bf16[64,1536]{1,0:T(8,128)(2,1)S(1)}, u32[]{:S(2)}, u32[]{:S(2)}) collective-permute-start(bf16[64,1536]{1,0:T(8,128)(2,1)S(1)} %add_convert_fusion.7), channel_id=1, source_target_pairs={{0,7},{1,0},{2,1},{3,2},{4,3},{5,4},{6,5},{7,6},{8,15},{9,8},{10,9... | collective-permute-start | bytes 589832 | tf_op jit(solution)/shard_map/ppermute | solution.py:146
  151.8 2.4 %begin.1.refs_0_ = f32[64,5120]{1,0:T(8,128)S(1)} custom-call(bf16[64,3584]{1,0:T(8,128)(2,1)S(1)} %copy-done.4, bf16[64,3584]{1,0:T(8,128)(2,1)S(1)} %collective-permute-done.17.up, bf16[64,3584]{1,0:T(8,128)(2,1)S(1)} %collective-permute-done.20.down, bf16[896,1280]{1,0:T(8,128)(2,1)S(1)} %copy-done.1, bf16[64,5120]{1,0:T(8,128)(2,1)S(1)} %copy-done.3), custom_call_target="tpu_custom_call" | custom-call | flops 1000 | bytes 1000 | tf_op jit(solution)/shard_map/begin/pallas_call | solution.py:104
  154.2 0.7 collective-permute-done.13.down
  154.9 3.0 %finish.1 = f32[64,5120]{1,0:T(8,128)} custom-call(bf16[64,1536]{1,0:T(8,128)(2,1)S(1)} %get-tuple-element.32.own, bf16[64,1536]{1,0:T(8,128)(2,1)S(1)} %collective-permute-done.10.up, bf16[64,1536]{1,0:T(8,128)(2,1)S(1)} %collective-permute-done.13.down, bf16[384,1280]{1,0:T(8,128)(2,1)S(1)} %copy-done.2, f32[64,5120]{1,0:T(8,128)S(1)} %begin.1.refs_0_, ...), custom_call_target="tpu_custom_call" | custom-call | flops 1000 | bytes 1000 | tf_op jit(solution)/shard_map/finish/pallas_call | solution.py:130
  (71 shorter events, 2.4 us)
Async XLA Ops:
  0.0 82.0 %copy-start = (f32[150]{0:T(256)S(1)}, f32[150]{0:T(256)}, u32[]{:S(2)}) copy-start(f32[150]{0:T(256)} %param.12) | copy-start | bytes 1804
  4.9 7.8 %copy-start.6 = (bf16[64,5120]{1,0:T(8,128)(2,1)S(1)}, bf16[64,5120]{1,0:T(8,128)(2,1)}, u32[]{:S(2)}) copy-start(bf16[64,5120]{1,0:T(8,128)(2,1)} %param.7) | copy-start | bytes 1966084
  4.9 68.5 %all-to-all-start = ((bf16[32,112,640]{2,1,0:T(8,128)(2,1)}), bf16[32,112,640]{2,1,0:T(8,128)(2,1)}, u32[]{:S(2)}, u32[]{:S(2)}) async-start(bf16[32,112,640]{2,1,0:T(8,128)(2,1)} %slice.67), calls=%async_computation | async-start | bytes 9175040 | tf_op jit(solution)/shard_map/all_to_all | solution.py:212
  13.4 14.7 %collective-permute-start = (bf16[3,64,640]{2,1,0:T(8,128)(2,1)S(1)}, bf16[3,64,640]{2,1,0:T(8,128)(2,1)S(1)}, u32[]{:S(2)}, u32[]{:S(2)}) collective-permute-start(bf16[3,64,640]{2,1,0:T(8,128)(2,1)S(1)} %pad_maximum_fusion.1), channel_id=1, source_target_pairs={{0,7},{1,0},{2,1},{3,2},{4,3},{5,4},{6,5},{7,6},{8,15},{9,8},{10,9... | collective-permute-start | bytes 737288 | tf_op jit(solution)/shard_map/ppermute | solution.py:146
  19.4 12.0 %collective-permute-start.3 = (bf16[4,64,640]{2,1,0:T(8,128)(2,1)S(1)}, bf16[4,64,640]{2,1,0:T(8,128)(2,1)S(1)}, u32[]{:S(2)}, u32[]{:S(2)}) collective-permute-start(bf16[4,64,640]{2,1,0:T(8,128)(2,1)S(1)} %pad_maximum_fusion), channel_id=1, source_target_pairs={{0,1},{1,2},{2,3},{3,4},{4,5},{5,6},{6,7},{7,0},{8,9},{9,10},{10,1... | collective-permute-start | bytes 983048 | tf_op jit(solution)/shard_map/ppermute | solution.py:146
  23.6 4.2 %copy-start.13 = (s32[64,2]{0,1:T(2,128)S(1)}, s32[64,2]{0,1:T(2,128)}, u32[]{:S(2)}) copy-start(s32[64,2]{0,1:T(2,128)} %param.11) | copy-start | bytes 1540
  28.2 11.9 %collective-permute-start.1 = (bf16[2,64,640]{2,1,0:T(8,128)(2,1)S(1)}, bf16[2,64,640]{2,1,0:T(8,128)(2,1)S(1)}, u32[]{:S(2)}, u32[]{:S(2)}) collective-permute-start(bf16[2,64,640]{2,1,0:T(8,128)(2,1)S(1)} %slice.57), channel_id=1, source_target_pairs={{0,7},{1,0},{2,1},{3,2},{4,3},{5,4},{6,5},{7,6},{8,15},{9,8},{10,9... | collective-permute-start | bytes 491528 | tf_op jit(solution)/shard_map/ppermute | solution.py:146
  31.5 8.5 %collective-permute-start.4 = (bf16[3,64,640]{2,1,0:T(8,128)(2,1)S(1)}, bf16[3,64,640]{2,1,0:T(8,128)(2,1)S(1)}, u32[]{:S(2)}, u32[]{:S(2)}) collective-permute-start(bf16[3,64,640]{2,1,0:T(8,128)(2,1)S(1)} %slice.60), channel_id=1, source_target_pairs={{0,1},{1,2},{2,3},{3,4},{4,5},{5,6},{6,7},{7,0},{8,9},{9,10},{10,1... | collective-permute-start | bytes 737288 | tf_op jit(solution)/shard_map/ppermute | solution.py:146
  40.0 6.6 %collective-permute-start.5 = (bf16[2,64,640]{2,1,0:T(8,128)(2,1)S(1)}, bf16[2,64,640]{2,1,0:T(8,128)(2,1)S(1)}, u32[]{:S(2)}, u32[]{:S(2)}) collective-permute-start(bf16[2,64,640]{2,1,0:T(8,128)(2,1)S(1)} %slice.61), channel_id=1, source_target_pairs={{0,1},{1,2},{2,3},{3,4},{4,5},{5,6},{6,7},{7,0},{8,9},{9,10},{10,1... | collective-permute-start | bytes 491528 | tf_op jit(solution)/shard_map/ppermute | solution.py:146
  40.7 7.1 %collective-permute-start.2 = (bf16[1,64,640]{2,1,0:T(8,128)(2,1)S(1)}, bf16[1,64,640]{2,1,0:T(8,128)(2,1)S(1)}, u32[]{:S(2)}, u32[]{:S(2)}) collective-permute-start(bf16[1,64,640]{2,1,0:T(8,128)(2,1)S(1)} %get-tuple-element.61), channel_id=1, source_target_pairs={{0,7},{1,0},{2,1},{3,2},{4,3},{5,4},{6,5},{7,6},{8,15},{9,8},{10,9... | collective-permute-start | bytes 245768 | tf_op jit(solution)/shard_map/ppermute | solution.py:146
  47.2 5.7 %collective-permute-start.6 = (bf16[1,64,640]{2,1,0:T(8,128)(2,1)S(1)}, bf16[1,64,640]{2,1,0:T(8,128)(2,1)S(1)}, u32[]{:S(2)}, u32[]{:S(2)}) collective-permute-start(bf16[1,64,640]{2,1,0:T(8,128)(2,1)S(1)} %get-tuple-element.60), channel_id=1, source_target_pairs={{0,1},{1,2},{2,3},{3,4},{4,5},{5,6},{6,7},{7,0},{8,9},{9,10},{10,1... | collective-permute-start | bytes 245768 | tf_op jit(solution)/shard_map/ppermute | solution.py:146
  47.8 5.0 %copy-start.11 = (bf16[1,64,640]{2,1,0:T(8,128)(2,1)}, bf16[1,64,640]{2,1,0:T(8,128)(2,1)S(1)}, u32[]{:S(2)}) copy-start(bf16[1,64,640]{2,1,0:T(8,128)(2,1)S(1)} %collective-permute-done.2) | copy-start | bytes 245764
  52.9 0.6 copy-start.12
  80.1 16.5 %collective-permute-start.14 = (bf16[64,3584]{1,0:T(8,128)(2,1)}, bf16[64,3584]{1,0:T(8,128)(2,1)}, u32[]{:S(2)}, u32[]{:S(2)}) collective-permute-start(bf16[64,3584]{1,0:T(8,128)(2,1)} %get-tuple-element.42), channel_id=1, source_target_pairs={{0,1},{1,2},{2,3},{3,4},{4,5},{5,6},{6,7},{7,0},{8,9},{9,10},{10,1... | collective-permute-start | bytes 1376264 | tf_op jit(solution)/shard_map/ppermute | solution.py:146
  83.5 18.3 %copy-start.10 = (bf16[64,3584]{1,0:T(8,128)(2,1)S(1)}, bf16[64,3584]{1,0:T(8,128)(2,1)}, u32[]{:S(2)}) copy-start(bf16[64,3584]{1,0:T(8,128)(2,1)} %get-tuple-element.47) | copy-start | bytes 1376260
  83.5 31.1 %all-to-all-start.1 = ((bf16[32,48,640]{2,1,0:T(8,128)(2,1)}), bf16[32,48,640]{2,1,0:T(8,128)(2,1)S(1)}, u32[]{:S(2)}, u32[]{:S(2)}) async-start(bf16[32,48,640]{2,1,0:T(8,128)(2,1)} %get-tuple-element.31), calls=%async_computation.1 | async-start | bytes 3932160 | tf_op jit(solution)/shard_map/all_to_all | solution.py:212
  87.5 23.2 %copy-start.9 = (bf16[64,3584]{1,0:T(8,128)(2,1)S(1)}, bf16[64,3584]{1,0:T(8,128)(2,1)}, u32[]{:S(2)}) copy-start(bf16[64,3584]{1,0:T(8,128)(2,1)} %get-tuple-element.44) | copy-start | bytes 1376260
  87.5 27.0 %copy-start.8 = (bf16[64,3584]{1,0:T(8,128)(2,1)S(1)}, bf16[64,3584]{1,0:T(8,128)(2,1)}, u32[]{:S(2)}) copy-start(bf16[64,3584]{1,0:T(8,128)(2,1)} %get-tuple-element.48) | copy-start | bytes 1376260
  87.5 14.3 %collective-permute-start.18 = (bf16[64,3584]{1,0:T(8,128)(2,1)}, bf16[64,3584]{1,0:T(8,128)(2,1)S(1)}, u32[]{:S(2)}, u32[]{:S(2)}) collective-permute-start(bf16[64,3584]{1,0:T(8,128)(2,1)} %get-tuple-element.46), channel_id=1, source_target_pairs={{0,7},{1,0},{2,1},{3,2},{4,3},{5,4},{6,5},{7,6},{8,15},{9,8},{10,9... | collective-permute-start | bytes 1376264 | tf_op jit(solution)/shard_map/ppermute | solution.py:146
  97.9 12.8 %collective-permute-start.15 = (bf16[64,3584]{1,0:T(8,128)(2,1)S(1)}, bf16[64,3584]{1,0:T(8,128)(2,1)S(1)}, u32[]{:S(2)}, u32[]{:S(2)}) collective-permute-start(bf16[64,3584]{1,0:T(8,128)(2,1)S(1)} %add_convert_fusion.4), channel_id=1, source_target_pairs={{0,1},{1,2},{2,3},{3,4},{4,5},{5,6},{6,7},{7,0},{8,9},{9,10},{10,1... | collective-permute-start | bytes 1376264 | tf_op jit(solution)/shard_map/ppermute | solution.py:146
  101.9 12.6 %collective-permute-start.19 = (bf16[64,3584]{1,0:T(8,128)(2,1)S(1)}, bf16[64,3584]{1,0:T(8,128)(2,1)S(1)}, u32[]{:S(2)}, u32[]{:S(2)}) collective-permute-start(bf16[64,3584]{1,0:T(8,128)(2,1)S(1)} %add_convert_fusion.1), channel_id=1, source_target_pairs={{0,7},{1,0},{2,1},{3,2},{4,3},{5,4},{6,5},{7,6},{8,15},{9,8},{10,9... | collective-permute-start | bytes 1376264 | tf_op jit(solution)/shard_map/ppermute | solution.py:146
  111.5 12.1 %collective-permute-start.16 = (bf16[64,3584]{1,0:T(8,128)(2,1)}, bf16[64,3584]{1,0:T(8,128)(2,1)}, u32[]{:S(2)}, u32[]{:S(2)}) collective-permute-start(bf16[64,3584]{1,0:T(8,128)(2,1)} %add_convert_fusion.3), channel_id=1, source_target_pairs={{0,1},{1,2},{2,3},{3,4},{4,5},{5,6},{6,7},{7,0},{8,9},{9,10},{10,1... | collective-permute-start | bytes 1376264 | tf_op jit(solution)/shard_map/ppermute | solution.py:146
  114.6 9.0 %copy-start.7 = (bf16[64,3584]{1,0:T(8,128)(2,1)S(1)}, bf16[64,3584]{1,0:T(8,128)(2,1)}, u32[]{:S(2)}) copy-start(bf16[64,3584]{1,0:T(8,128)(2,1)} %get-tuple-element.45) | copy-start | bytes 1376260
  116.1 35.7 %copy-start.1 = (bf16[896,1280]{1,0:T(8,128)(2,1)S(1)}, bf16[896,1280]{1,0:T(8,128)(2,1)}, u32[]{:S(2)}) copy-start(bf16[896,1280]{1,0:T(8,128)(2,1)} %get-tuple-element.50.place) | copy-start | bytes 6881284
  116.1 35.7 %copy-start.3 = (bf16[64,5120]{1,0:T(8,128)(2,1)S(1)}, bf16[64,5120]{1,0:T(8,128)(2,1)}, u32[]{:S(2)}) copy-start(bf16[64,5120]{1,0:T(8,128)(2,1)} %other_ref.1) | copy-start | bytes 1966084
  116.1 35.6 %copy-start.4 = (bf16[64,3584]{1,0:T(8,128)(2,1)S(1)}, bf16[64,3584]{1,0:T(8,128)(2,1)}, u32[]{:S(2)}) copy-start(bf16[64,3584]{1,0:T(8,128)(2,1)} %get-tuple-element.41.own) | copy-start | bytes 1376260
  116.1 12.1 %collective-permute-start.7 = (bf16[64,1536]{1,0:T(8,128)(2,1)S(1)}, bf16[64,1536]{1,0:T(8,128)(2,1)S(1)}, u32[]{:S(2)}, u32[]{:S(2)}) collective-permute-start(bf16[64,1536]{1,0:T(8,128)(2,1)S(1)} %get-tuple-element.33), channel_id=1, source_target_pairs={{0,7},{1,0},{2,1},{3,2},{4,3},{5,4},{6,5},{7,6},{8,15},{9,8},{10,9... | collective-permute-start | bytes 589832 | tf_op jit(solution)/shard_map/ppermute | solution.py:146
  124.8 26.9 %collective-permute-start.17 = (bf16[64,3584]{1,0:T(8,128)(2,1)S(1)}, bf16[64,3584]{1,0:T(8,128)(2,1)S(1)}, u32[]{:S(2)}, u32[]{:S(2)}) collective-permute-start(bf16[64,3584]{1,0:T(8,128)(2,1)S(1)} %add_convert_fusion.2), channel_id=1, source_target_pairs={{0,1},{1,2},{2,3},{3,4},{4,5},{5,6},{6,7},{7,0},{8,9},{9,10},{10,1... | collective-permute-start | bytes 1376264 | tf_op jit(solution)/shard_map/ppermute | solution.py:146
  124.9 15.0 %collective-permute-start.11 = (bf16[64,1536]{1,0:T(8,128)(2,1)S(1)}, bf16[64,1536]{1,0:T(8,128)(2,1)S(1)}, u32[]{:S(2)}, u32[]{:S(2)}) collective-permute-start(bf16[64,1536]{1,0:T(8,128)(2,1)S(1)} %get-tuple-element.37), channel_id=1, source_target_pairs={{0,1},{1,2},{2,3},{3,4},{4,5},{5,6},{6,7},{7,0},{8,9},{9,10},{10,1... | collective-permute-start | bytes 589832 | tf_op jit(solution)/shard_map/ppermute | solution.py:146
  125.0 26.8 %collective-permute-start.20 = (bf16[64,3584]{1,0:T(8,128)(2,1)S(1)}, bf16[64,3584]{1,0:T(8,128)(2,1)S(1)}, u32[]{:S(2)}, u32[]{:S(2)}) collective-permute-start(bf16[64,3584]{1,0:T(8,128)(2,1)S(1)} %add_convert_fusion), channel_id=1, source_target_pairs={{0,7},{1,0},{2,1},{3,2},{4,3},{5,4},{6,5},{7,6},{8,15},{9,8},{10,9... | collective-permute-start | bytes 1376264 | tf_op jit(solution)/shard_map/ppermute | solution.py:146
  128.2 11.8 %collective-permute-start.8 = (bf16[64,1536]{1,0:T(8,128)(2,1)S(1)}, bf16[64,1536]{1,0:T(8,128)(2,1)S(1)}, u32[]{:S(2)}, u32[]{:S(2)}) collective-permute-start(bf16[64,1536]{1,0:T(8,128)(2,1)S(1)} %add_convert_fusion.9), channel_id=1, source_target_pairs={{0,7},{1,0},{2,1},{3,2},{4,3},{5,4},{6,5},{7,6},{8,15},{9,8},{10,9... | collective-permute-start | bytes 589832 | tf_op jit(solution)/shard_map/ppermute | solution.py:146
  140.0 7.9 %collective-permute-start.12 = (bf16[64,1536]{1,0:T(8,128)(2,1)S(1)}, bf16[64,1536]{1,0:T(8,128)(2,1)S(1)}, u32[]{:S(2)}, u32[]{:S(2)}) collective-permute-start(bf16[64,1536]{1,0:T(8,128)(2,1)S(1)} %add_convert_fusion.6), channel_id=1, source_target_pairs={{0,1},{1,2},{2,3},{3,4},{4,5},{5,6},{6,7},{7,0},{8,9},{9,10},{10,1... | collective-permute-start | bytes 589832 | tf_op jit(solution)/shard_map/ppermute | solution.py:146
  140.1 8.4 %collective-permute-start.9 = (bf16[64,1536]{1,0:T(8,128)(2,1)S(1)}, bf16[64,1536]{1,0:T(8,128)(2,1)S(1)}, u32[]{:S(2)}, u32[]{:S(2)}) collective-permute-start(bf16[64,1536]{1,0:T(8,128)(2,1)S(1)} %add_convert_fusion.8), channel_id=1, source_target_pairs={{0,7},{1,0},{2,1},{3,2},{4,3},{5,4},{6,5},{7,6},{8,15},{9,8},{10,9... | collective-permute-start | bytes 589832 | tf_op jit(solution)/shard_map/ppermute | solution.py:146
  147.9 7.0 %collective-permute-start.13 = (bf16[64,1536]{1,0:T(8,128)(2,1)S(1)}, bf16[64,1536]{1,0:T(8,128)(2,1)S(1)}, u32[]{:S(2)}, u32[]{:S(2)}) collective-permute-start(bf16[64,1536]{1,0:T(8,128)(2,1)S(1)} %add_convert_fusion.5), channel_id=1, source_target_pairs={{0,1},{1,2},{2,3},{3,4},{4,5},{5,6},{6,7},{7,0},{8,9},{9,10},{10,1... | collective-permute-start | bytes 589832 | tf_op jit(solution)/shard_map/ppermute | solution.py:146
  148.6 6.2 %collective-permute-start.10 = (bf16[64,1536]{1,0:T(8,128)(2,1)S(1)}, bf16[64,1536]{1,0:T(8,128)(2,1)S(1)}, u32[]{:S(2)}, u32[]{:S(2)}) collective-permute-start(bf16[64,1536]{1,0:T(8,128)(2,1)S(1)} %add_convert_fusion.7), channel_id=1, source_target_pairs={{0,7},{1,0},{2,1},{3,2},{4,3},{5,4},{6,5},{7,6},{8,15},{9,8},{10,9... | collective-permute-start | bytes 589832 | tf_op jit(solution)/shard_map/ppermute | solution.py:146
  151.8 3.1 %copy-start.2 = (bf16[384,1280]{1,0:T(8,128)(2,1)S(1)}, bf16[384,1280]{1,0:T(8,128)(2,1)}, u32[]{:S(2)}) copy-start(bf16[384,1280]{1,0:T(8,128)(2,1)} %get-tuple-element.40.place) | copy-start | bytes 2949124
  151.8 3.1 %copy-start.5 = (f32[5120]{0:T(1024)S(1)}, f32[5120]{0:T(1024)}, u32[]{:S(2)}) copy-start(f32[5120]{0:T(1024)} %param.13) | copy-start | bytes 61444
